TPU v7x, 32 devices: a whole 2x2x4 slice. The times are simulated.
32 devices in a mesh: ctx: 8 (over y, x, core), head: 4 (over z).
Axes of the slice: x: 2, y: 2, z: 4, core: 2. Of those that a mesh axis runs over, the one named last changes fastest.
Arguments:
- query_input: bfloat16 [1024, 2048], P(('ctx', 'head')), may hold values from -9 to 9
- key_input: bfloat16 [1024, 512], P(('ctx', 'head')), may hold values from -6 to 6
- value_input: bfloat16 [1024, 512], P(('ctx', 'head')), may hold values from -0.625 to 0.625
- output_gradient: bfloat16 [1024, 2048], P(('ctx', 'head')), may hold values from -6 to 6
- log_softmax_norm: float32 [1024, 32], P('ctx', 'head'), as said below
- output_delta_rows: float32 [1024, 32], P('ctx', 'head'), may hold values from -6 to 6
- positions: int32 [1024], P('ctx'), may hold values from 0 to 1023, as said below
Outputs:
- grad_query: bfloat16 [1024, 2048], P(('ctx', 'head'))
- key_gradient: bfloat16 [1024, 512], P(('ctx', 'head'))
- value_gradient: bfloat16 [1024, 512], P(('ctx', 'head'))
Inputs may be any that keep to these rules, and one draw needn't show every extreme that they name: positions is a permutation of 0 to 1023; each aligned block of 128 rows holds 64 ascending consecutive positions starting at a 64, then 64 ascending consecutive positions starting at (15 - a) * 64, with a different number a in each block. log_softmax_norm of a row lies between log(p + 1) + 0.7 and log(p + 1) + 1.6, where p is the row's position.
All inputs are finite; a program needn't handle non-finite values.
Results may differ from a plain program's by a relative error of at most 0.0055.
Values may be sent and summed in bfloat16 or wider, within the bound.
No kernel may reach another device: no remote copies, remote signals or barrier semaphores. Data moves between devices by JAX's collectives and lax.ppermute only.
A program may use at most 64 MiB of HBM per device.

v0:
```python
import jax
import jax.numpy as jnp
from jax import lax
from jax.sharding import PartitionSpec as P

HEAD_WIDTH = 64


def for_sending(array):
    return jax.tree.map(lambda a: a.astype(jnp.bfloat16) if a.dtype == jnp.float32 else a, array)


def from_behind(array, axis, by):
    count = lax.axis_size(axis)
    return lax.ppermute(array, axis, [(i, (i + by) % count) for i in range(count)])


def block_terms(
    query, grad_rows, norm_rows, delta_part, query_pos, key_block, value_block, key_pos
):
    row_count = query.shape[0]
    col_count = key_block.shape[0]
    kv_heads = key_block.shape[1] // HEAD_WIDTH
    query_group_width = query.shape[1] // (kv_heads * HEAD_WIDTH)
    score_scale = HEAD_WIDTH ** (-0.5)
    query_per_head = query.reshape(row_count, kv_heads, query_group_width, HEAD_WIDTH)
    gradient_per_head = grad_rows.reshape(row_count, kv_heads, query_group_width, HEAD_WIDTH)
    key_per_head = key_block.reshape(col_count, kv_heads, HEAD_WIDTH)
    value_per_head = value_block.reshape(col_count, kv_heads, HEAD_WIDTH)
    scores = (
        jnp.einsum(
            "qhgd,khd->qhgk", query_per_head, key_per_head, preferred_element_type=jnp.float32
        )
        * score_scale
    )
    visible = (query_pos[:, None] >= key_pos[None, :])[:, None, None, :]
    norm_cols = norm_rows.reshape(row_count, kv_heads, query_group_width, 1)
    probabilities = jnp.where(visible, jnp.exp(scores - norm_cols), 0.0)
    grad_prob = jnp.einsum(
        "qhgd,khd->qhgk", gradient_per_head, value_per_head, preferred_element_type=jnp.float32
    )
    grad_score = probabilities * (
        grad_prob - delta_part.reshape(row_count, kv_heads, query_group_width, 1)
    )
    prob_rounded = probabilities.astype(jnp.bfloat16)
    score_rounded = grad_score.astype(jnp.bfloat16)
    value_term = jnp.einsum(
        "qhgk,qhgd->khd", prob_rounded, gradient_per_head, preferred_element_type=jnp.float32
    )
    key_term = score_scale * jnp.einsum(
        "qhgk,qhgd->khd", score_rounded, query_per_head, preferred_element_type=jnp.float32
    )
    query_term = score_scale * jnp.einsum(
        "qhgk,khd->qhgd", score_rounded, key_per_head, preferred_element_type=jnp.float32
    )
    return (
        query_term.reshape(row_count, -1),
        key_term.reshape(col_count, -1),
        value_term.reshape(col_count, -1),
    )


def no_terms(operands):
    query = operands[0]
    key_block = operands[5]
    return (
        jnp.zeros(query.shape, jnp.float32),
        jnp.zeros(key_block.shape, jnp.float32),
        jnp.zeros(key_block.shape, jnp.float32),
    )


def all_terms(operands):
    return block_terms(*operands)


def pair_terms(query, grad_rows, norm_rows, delta_part, query_pos, key_block, value_block, key_pos):
    row_half = query.shape[0] // 2
    col_half = key_block.shape[0] // 2
    zero_cols = jnp.zeros((col_half, key_block.shape[1]), jnp.float32)
    key_sums = [zero_cols, zero_cols]
    value_sums = [zero_cols, zero_cols]
    query_parts = []
    for row_side in range(2):
        rows_here = slice(row_side * row_half, (row_side + 1) * row_half)
        query_sum = jnp.zeros((row_half, query.shape[1]), jnp.float32)
        for col_side in range(2):
            cols_here = slice(col_side * col_half, (col_side + 1) * col_half)
            operands = (
                query[rows_here],
                grad_rows[rows_here],
                norm_rows[rows_here],
                delta_part[rows_here],
                query_pos[rows_here],
                key_block[cols_here],
                value_block[cols_here],
                key_pos[cols_here],
            )
            reached = jnp.any(query_pos[rows_here][:, None] >= key_pos[cols_here][None, :])
            query_term, key_term, value_term = lax.cond(reached, all_terms, no_terms, operands)
            query_sum = query_sum + query_term
            key_sums[col_side] = key_sums[col_side] + key_term
            value_sums[col_side] = value_sums[col_side] + value_term
        query_parts.append(query_sum)
    return (
        jnp.concatenate(query_parts, 0),
        jnp.concatenate(key_sums, 0),
        jnp.concatenate(value_sums, 0),
    )


def pass_keys(traveler, offset):
    return from_behind((for_sending(traveler[0]), for_sending(traveler[1])), "ctx", offset)


def pass_sums(traveler, offset):
    return from_behind((traveler[2], traveler[3], traveler[4]), "ctx", offset)


def on_device(
    query_input,
    key_input,
    value_input,
    output_gradient,
    log_softmax_norm,
    output_delta_rows,
    positions,
):
    query, key_local, value_local, grad_rows = (
        lax.all_to_all(query_input, "head", split_axis=1, concat_axis=0, tiled=True),
        lax.all_to_all(key_input, "head", split_axis=1, concat_axis=0, tiled=True),
        lax.all_to_all(value_input, "head", split_axis=1, concat_axis=0, tiled=True),
        lax.all_to_all(output_gradient, "head", split_axis=1, concat_axis=0, tiled=True),
    )
    query_pos = positions.astype(jnp.float32)
    row_count = query.shape[0]
    feature_width = key_local.shape[1]
    grad_query = jnp.zeros(query.shape, jnp.float32)

    def visit(key_block, value_block, key_pos):
        return pair_terms(
            query,
            grad_rows,
            log_softmax_norm,
            output_delta_rows,
            query_pos,
            key_block,
            value_block,
            key_pos,
        )

    offsets = (1,)
    bounds = ((0, row_count),)
    travelers = tuple(
        (
            (
                key_local,
                value_local,
                jnp.zeros((upper_row - lower_row, feature_width), jnp.float32),
                jnp.zeros((upper_row - lower_row, feature_width), jnp.float32),
                query_pos,
            )
            for lower_row, upper_row in bounds
        )
    )

    def absorb_all(query_sum, travelers):
        updated = []
        for traveler in travelers:
            key_block, value_block, key_acc, value_acc, key_pos = traveler
            query_term, key_term, value_term = visit(key_block, value_block, key_pos)
            query_sum = query_sum + query_term
            updated.append(
                (key_block, value_block, key_acc + key_term, value_acc + value_term, key_pos)
            )
        return (query_sum, tuple(updated))

    def cycle_turn(turn_index, running):
        query_sum, travelers = absorb_all(running[0], running[1])
        moved = []
        for traveler, offset in zip(travelers, offsets):
            key_block, value_block = pass_keys(traveler, offset)
            key_acc, value_acc, key_pos = pass_sums(traveler, offset)
            moved.append((key_block, value_block, key_acc, value_acc, key_pos))
        return (query_sum, tuple(moved))

    grad_query, travelers = lax.fori_loop(
        0, lax.axis_size("ctx") - 1, cycle_turn, (grad_query, travelers)
    )
    grad_query, travelers = absorb_all(grad_query, travelers)
    returned = [pass_sums(traveler, offset) for traveler, offset in zip(travelers, offsets)]
    key_gradient = jnp.concatenate([arrived[0] for arrived in returned], 0)
    value_gradient = jnp.concatenate([arrived[1] for arrived in returned], 0)
    query_out, key_out, value_out = (
        lax.all_to_all(
            grad_query.astype(jnp.bfloat16), "head", split_axis=0, concat_axis=1, tiled=True
        ),
        lax.all_to_all(
            key_gradient.astype(jnp.bfloat16), "head", split_axis=0, concat_axis=1, tiled=True
        ),
        lax.all_to_all(
            value_gradient.astype(jnp.bfloat16), "head", split_axis=0, concat_axis=1, tiled=True
        ),
    )
    return (query_out, key_out, value_out)


def solution(mesh):
    return jax.shard_map(
        on_device,
        mesh=mesh,
        in_specs=(
            P(("ctx", "head"), None),
            P(("ctx", "head"), None),
            P(("ctx", "head"), None),
            P(("ctx", "head"), None),
            P("ctx", "head"),
            P("ctx", "head"),
            P("ctx"),
        ),
        out_specs=(P(("ctx", "head"), None), P(("ctx", "head"), None), P(("ctx", "head"), None)),
        check_vma=False,
    )
```

profile of v0, /device:TPU:0, one launch (start us, length us, event | category | flops | bytes accessed | tf_op | source)
XLA Modules:
  0.0 196.0 jit_solution(9265536280605234849)
XLA Ops:
  2.0 6.3 %all-to-all-start = ((bf16[32,4,128]{2,0,1:T(8,128)(2,1)}), bf16[32,4,128]{2,0,1:T(8,128)(2,1)S(1)}, u32[]{:S(2)}, u32[]{:S(2)}) async-start(bf16[32,4,128]{2,0,1:T(8,128)(2,1)} %copy_bitcast_fusion.5), calls=%async_computation | async-start | bytes 65536 | tf_op jit(solution)/shard_map/all_to_all | solution.py:131
  14.0 3.5 %all-to-all-start.3 = ((bf16[32,4,512]{2,0,1:T(8,128)(2,1)}), bf16[32,4,512]{2,0,1:T(8,128)(2,1)S(1)}, u32[]{:S(2)}, u32[]{:S(2)}) async-start(bf16[32,4,512]{2,0,1:T(8,128)(2,1)} %bitcast.362), calls=%async_computation.3 | async-start | bytes 262144 | tf_op jit(solution)/shard_map/all_to_all | solution.py:133
  17.6 5.8 %all-to-all-done.3 = bf16[32,4,512]{2,0,1:T(8,128)(2,1)S(1)} async-done(((bf16[32,4,512]{2,0,1:T(8,128)(2,1)}), bf16[32,4,512]{2,0,1:T(8,128)(2,1)S(1)}, u32[]{:S(2)}, u32[]{:S(2)}) %all-to-all-start.3) | async-done | bytes 131104 | tf_op jit(solution)/shard_map/all_to_all | solution.py:133
  23.4 3.3 %all-to-all-start.2 = ((bf16[32,4,512]{2,0,1:T(8,128)(2,1)}), bf16[32,4,512]{2,0,1:T(8,128)(2,1)S(1)}, u32[]{:S(2)}, u32[]{:S(2)}) async-start(bf16[32,4,512]{2,0,1:T(8,128)(2,1)} %bitcast.363), calls=%async_computation.2 | async-start | bytes 262144 | tf_op jit(solution)/shard_map/all_to_all | solution.py:130
  26.7 5.9 %all-to-all-done.2 = bf16[32,4,512]{2,0,1:T(8,128)(2,1)S(1)} async-done(((bf16[32,4,512]{2,0,1:T(8,128)(2,1)}), bf16[32,4,512]{2,0,1:T(8,128)(2,1)S(1)}, u32[]{:S(2)}, u32[]{:S(2)}) %all-to-all-start.2) | async-done | bytes 131104 | tf_op jit(solution)/shard_map/all_to_all | solution.py:130
  32.6 3.3 %all-to-all-start.1 = ((bf16[32,4,128]{2,0,1:T(8,128)(2,1)}), bf16[32,4,128]{2,0,1:T(8,128)(2,1)S(1)}, u32[]{:S(2)}, u32[]{:S(2)}) async-start(bf16[32,4,128]{2,0,1:T(8,128)(2,1)} %copy_bitcast_fusion.4), calls=%async_computation.1 | async-start | bytes 65536 | tf_op jit(solution)/shard_map/all_to_all | solution.py:132
  35.9 5.6 %all-to-all-done.1 = bf16[32,4,128]{2,0,1:T(8,128)(2,1)S(1)} async-done(((bf16[32,4,128]{2,0,1:T(8,128)(2,1)}), bf16[32,4,128]{2,0,1:T(8,128)(2,1)S(1)}, u32[]{:S(2)}, u32[]{:S(2)}) %all-to-all-start.1) | async-done | bytes 32800 | tf_op jit(solution)/shard_map/all_to_all | solution.py:132
  41.5 114.1 %while.21 = (s32[]{:T(128)}, f32[128,512]{1,0:T(8,128)S(1)}, bf16[128,128]{1,0:T(8,128)(2,1)S(1)}, bf16[128,128]{1,0:T(8,128)(2,1)S(1)}, f32[128,128]{1,0:T(8,12...) while((s32[]{:T(128)}, f32[128,512]{1,0:T(8,128)S(1)}, ...), condition=%wide.region_13.14_spmd.clone, body=%wide.region_0.13_spmd.clone.sunk | while | flops 85377024 | bytes 12853967 | solution.py:187
  56.0 2.7 %collective-permute-done.2 = f32[128,128]{1,0:T(8,128)S(1)} collective-permute-done((f32[128,128]{1,0:T(8,128)S(1)}, f32[128,128]{1,0:T(8,128)S(1)}, u32[]{:S(2)}, u32[]{:S(2)}) %collective-permute-start.2) | collective-permute-done | bytes 65568 | tf_op jit(solution)/shard_map/while/body/eval_jaxpr/ppermute | solution.py:15
  71.4 2.7 %collective-permute-done.2 = f32[128,128]{1,0:T(8,128)S(1)} collective-permute-done((f32[128,128]{1,0:T(8,128)S(1)}, f32[128,128]{1,0:T(8,128)S(1)}, u32[]{:S(2)}, u32[]{:S(2)}) %collective-permute-start.2) | collective-permute-done | bytes 65568 | tf_op jit(solution)/shard_map/while/body/eval_jaxpr/ppermute | solution.py:15
  84.4 3.0 %collective-permute-start.2 = (f32[128,128]{1,0:T(8,128)S(1)}, f32[128,128]{1,0:T(8,128)S(1)}, u32[]{:S(2)}, u32[]{:S(2)}) collective-permute-start(f32[128,128]{1,0:T(8,128)S(1)} %maximum_add_fusion.10), channel_id=1, source_target_pairs={{0,4},{4,8},{8,12},{12,16},{16,20},{20,24},{24,28},{28,0},{1,5},{5... | collective-permute-start | bytes 196616 | tf_op jit(solution)/shard_map/while/body/eval_jaxpr/ppermute | solution.py:15
  89.0 3.0 %collective-permute-done.3 = f32[128,128]{1,0:T(8,128)S(1)} collective-permute-done((f32[128,128]{1,0:T(8,128)S(1)}, f32[128,128]{1,0:T(8,128)S(1)}, u32[]{:S(2)}, u32[]{:S(2)}) %collective-permute-start.3) | collective-permute-done | bytes 65568 | tf_op jit(solution)/shard_map/while/body/eval_jaxpr/ppermute | solution.py:15
  113.5 2.4 %conditional.20 = (f32[64,512]{1,0:T(8,128)S(1)}, f32[64,128]{1,0:T(8,128)S(1)}, f32[64,128]{1,0:T(8,128)S(1)}) conditional(s32[]{:T(128)} %convert_element_type.125, () %tuple.160, (f32[64]{0:T(128)S(1)}, f32[64]{0:T(128)S(1)}, bf16[64,128]{1,0:T(8,128)(2,1)S(1)}, bf16[64,512]{1,0:T(8,128)(2,1)S(1)}, f32[64,8]{0,1:T(8,128)S(1)}, ...), branch_computations={%region_8.8_spmd, %region_9.9_spmd} | conditional | flops 21245952 | bytes 2224664 | solution.py:100
  116.1 3.0 %collective-permute-start.2 = (f32[128,128]{1,0:T(8,128)S(1)}, f32[128,128]{1,0:T(8,128)S(1)}, u32[]{:S(2)}, u32[]{:S(2)}) collective-permute-start(f32[128,128]{1,0:T(8,128)S(1)} %maximum_add_fusion.10), channel_id=1, source_target_pairs={{0,4},{4,8},{8,12},{12,16},{16,20},{20,24},{24,28},{28,0},{1,5},{5... | collective-permute-start | bytes 196616 | tf_op jit(solution)/shard_map/while/body/eval_jaxpr/ppermute | solution.py:15
  120.8 3.0 %collective-permute-done.3 = f32[128,128]{1,0:T(8,128)S(1)} collective-permute-done((f32[128,128]{1,0:T(8,128)S(1)}, f32[128,128]{1,0:T(8,128)S(1)}, u32[]{:S(2)}, u32[]{:S(2)}) %collective-permute-start.3) | collective-permute-done | bytes 65568 | tf_op jit(solution)/shard_map/while/body/eval_jaxpr/ppermute | solution.py:15
  147.9 3.0 %collective-permute-start.2 = (f32[128,128]{1,0:T(8,128)S(1)}, f32[128,128]{1,0:T(8,128)S(1)}, u32[]{:S(2)}, u32[]{:S(2)}) collective-permute-start(f32[128,128]{1,0:T(8,128)S(1)} %maximum_add_fusion.10), channel_id=1, source_target_pairs={{0,4},{4,8},{8,12},{12,16},{16,20},{20,24},{24,28},{28,0},{1,5},{5... | collective-permute-start | bytes 196616 | tf_op jit(solution)/shard_map/while/body/eval_jaxpr/ppermute | solution.py:15
  152.5 3.0 %collective-permute-done.3 = f32[128,128]{1,0:T(8,128)S(1)} collective-permute-done((f32[128,128]{1,0:T(8,128)S(1)}, f32[128,128]{1,0:T(8,128)S(1)}, u32[]{:S(2)}, u32[]{:S(2)}) %collective-permute-start.3) | collective-permute-done | bytes 65568 | tf_op jit(solution)/shard_map/while/body/eval_jaxpr/ppermute | solution.py:15
  164.2 4.2 %collective-permute-done.5 = bf16[128,128]{1,0:T(8,128)(2,1)} collective-permute-done((bf16[128,128]{1,0:T(8,128)(2,1)S(1)}, bf16[128,128]{1,0:T(8,128)(2,1)}, u32[]{:S(2)}, u32[]{:S(2)}) %collective-permute-start.5) | collective-permute-done | bytes 32800 | tf_op jit(solution)/shard_map/ppermute | solution.py:15
  168.3 3.3 %all-to-all-start.5 = ((bf16[4,32,128]{2,1,0:T(8,128)(2,1)}), bf16[4,32,128]{2,1,0:T(8,128)(2,1)S(1)}, u32[]{:S(2)}, u32[]{:S(2)}) async-start(bf16[4,32,128]{2,1,0:T(8,128)(2,1)} %bitcast.126), calls=%async_computation.5 | async-start | bytes 65536 | tf_op jit(solution)/shard_map/all_to_all | solution.py:198
  172.3 4.9 %all-to-all-done.5 = bf16[4,32,128]{2,1,0:T(8,128)(2,1)S(1)} async-done(((bf16[4,32,128]{2,1,0:T(8,128)(2,1)}), bf16[4,32,128]{2,1,0:T(8,128)(2,1)S(1)}, u32[]{:S(2)}, u32[]{:S(2)}) %all-to-all-start.5) | async-done | bytes 32800 | tf_op jit(solution)/shard_map/all_to_all | solution.py:198
  177.2 3.3 %all-to-all-start.6 = ((bf16[4,32,128]{2,1,0:T(8,128)(2,1)}), bf16[4,32,128]{2,1,0:T(8,128)(2,1)S(1)}, u32[]{:S(2)}, u32[]{:S(2)}) async-start(bf16[4,32,128]{2,1,0:T(8,128)(2,1)} %bitcast.128), calls=%async_computation.6 | async-start | bytes 65536 | tf_op jit(solution)/shard_map/all_to_all | solution.py:201
  181.1 5.0 %all-to-all-done.6 = bf16[4,32,128]{2,1,0:T(8,128)(2,1)S(1)} async-done(((bf16[4,32,128]{2,1,0:T(8,128)(2,1)}), bf16[4,32,128]{2,1,0:T(8,128)(2,1)S(1)}, u32[]{:S(2)}, u32[]{:S(2)}) %all-to-all-start.6) | async-done | bytes 32800 | tf_op jit(solution)/shard_map/all_to_all | solution.py:201
  186.1 3.3 %all-to-all-start.4 = ((bf16[4,32,512]{2,1,0:T(8,128)(2,1)}), bf16[4,32,512]{2,1,0:T(8,128)(2,1)S(1)}, u32[]{:S(2)}, u32[]{:S(2)}) async-start(bf16[4,32,512]{2,1,0:T(8,128)(2,1)} %bitcast.124), calls=%async_computation.4 | async-start | bytes 262144 | tf_op jit(solution)/shard_map/all_to_all | solution.py:195
  190.1 5.3 %all-to-all-done.4 = bf16[4,32,512]{2,1,0:T(8,128)(2,1)S(1)} async-done(((bf16[4,32,512]{2,1,0:T(8,128)(2,1)}), bf16[4,32,512]{2,1,0:T(8,128)(2,1)S(1)}, u32[]{:S(2)}, u32[]{:S(2)}) %all-to-all-start.4) | async-done | bytes 131104 | tf_op jit(solution)/shard_map/all_to_all | solution.py:195
  (572 shorter events, 125.0 us)
Async XLA Ops:
  2.0 12.0 %all-to-all-start = ((bf16[32,4,128]{2,0,1:T(8,128)(2,1)}), bf16[32,4,128]{2,0,1:T(8,128)(2,1)S(1)}, u32[]{:S(2)}, u32[]{:S(2)}) async-start(bf16[32,4,128]{2,0,1:T(8,128)(2,1)} %copy_bitcast_fusion.5), calls=%async_computation | async-start | bytes 65536 | tf_op jit(solution)/shard_map/all_to_all | solution.py:131
  14.0 9.3 %all-to-all-start.3 = ((bf16[32,4,512]{2,0,1:T(8,128)(2,1)}), bf16[32,4,512]{2,0,1:T(8,128)(2,1)S(1)}, u32[]{:S(2)}, u32[]{:S(2)}) async-start(bf16[32,4,512]{2,0,1:T(8,128)(2,1)} %bitcast.362), calls=%async_computation.3 | async-start | bytes 262144 | tf_op jit(solution)/shard_map/all_to_all | solution.py:133
  23.4 9.2 %all-to-all-start.2 = ((bf16[32,4,512]{2,0,1:T(8,128)(2,1)}), bf16[32,4,512]{2,0,1:T(8,128)(2,1)S(1)}, u32[]{:S(2)}, u32[]{:S(2)}) async-start(bf16[32,4,512]{2,0,1:T(8,128)(2,1)} %bitcast.363), calls=%async_computation.2 | async-start | bytes 262144 | tf_op jit(solution)/shard_map/all_to_all | solution.py:130
  41.5 14.4 %collective-permute-start.4 = (f32[128]{0:T(128)S(1)}, f32[128]{0:T(128)S(1)}, u32[]{:S(2)}, u32[]{:S(2)}) collective-permute-start(f32[128]{0:T(128)S(1)} %copy.718), channel_id=1, source_target_pairs={{0,4},{4,8},{8,12},{12,16},{16,20},{20,24},{24,28},{28,0},{1,5},{5... | collective-permute-start | bytes 1544 | tf_op jit(solution)/shard_map/while/body/eval_jaxpr/ppermute | solution.py:15
  41.6 14.3 %collective-permute-start = (bf16[128,128]{1,0:T(8,128)(2,1)S(1)}, bf16[128,128]{1,0:T(8,128)(2,1)S(1)}, u32[]{:S(2)}, u32[]{:S(2)}) collective-permute-start(bf16[128,128]{1,0:T(8,128)(2,1)S(1)} %copy.714), channel_id=1, source_target_pairs={{0,4},{4,8},{8,12},{12,16},{16,20},{20,24},{24,28},{28,0},{1,5},{5... | collective-permute-start | bytes 98312 | tf_op jit(solution)/shard_map/while/body/eval_jaxpr/ppermute | solution.py:15
  43.2 12.8 %collective-permute-start.1 = (bf16[128,128]{1,0:T(8,128)(2,1)S(1)}, bf16[128,128]{1,0:T(8,128)(2,1)S(1)}, u32[]{:S(2)}, u32[]{:S(2)}) collective-permute-start(bf16[128,128]{1,0:T(8,128)(2,1)S(1)} %copy.715), channel_id=1, source_target_pairs={{0,4},{4,8},{8,12},{12,16},{16,20},{20,24},{24,28},{28,0},{1,5},{5... | collective-permute-start | bytes 98312 | tf_op jit(solution)/shard_map/while/body/eval_jaxpr/ppermute | solution.py:15
  60.3 11.1 %collective-permute-start.4 = (f32[128]{0:T(128)S(1)}, f32[128]{0:T(128)S(1)}, u32[]{:S(2)}, u32[]{:S(2)}) collective-permute-start(f32[128]{0:T(128)S(1)} %copy.718), channel_id=1, source_target_pairs={{0,4},{4,8},{8,12},{12,16},{16,20},{20,24},{24,28},{28,0},{1,5},{5... | collective-permute-start | bytes 1544 | tf_op jit(solution)/shard_map/while/body/eval_jaxpr/ppermute | solution.py:15
  60.3 11.1 %collective-permute-start = (bf16[128,128]{1,0:T(8,128)(2,1)S(1)}, bf16[128,128]{1,0:T(8,128)(2,1)S(1)}, u32[]{:S(2)}, u32[]{:S(2)}) collective-permute-start(bf16[128,128]{1,0:T(8,128)(2,1)S(1)} %copy.714), channel_id=1, source_target_pairs={{0,4},{4,8},{8,12},{12,16},{16,20},{20,24},{24,28},{28,0},{1,5},{5... | collective-permute-start | bytes 98312 | tf_op jit(solution)/shard_map/while/body/eval_jaxpr/ppermute | solution.py:15
  61.0 10.4 %collective-permute-start.1 = (bf16[128,128]{1,0:T(8,128)(2,1)S(1)}, bf16[128,128]{1,0:T(8,128)(2,1)S(1)}, u32[]{:S(2)}, u32[]{:S(2)}) collective-permute-start(bf16[128,128]{1,0:T(8,128)(2,1)S(1)} %copy.715), channel_id=1, source_target_pairs={{0,4},{4,8},{8,12},{12,16},{16,20},{20,24},{24,28},{28,0},{1,5},{5... | collective-permute-start | bytes 98312 | tf_op jit(solution)/shard_map/while/body/eval_jaxpr/ppermute | solution.py:15
  75.8 11.9 %collective-permute-start.4 = (f32[128]{0:T(128)S(1)}, f32[128]{0:T(128)S(1)}, u32[]{:S(2)}, u32[]{:S(2)}) collective-permute-start(f32[128]{0:T(128)S(1)} %copy.718), channel_id=1, source_target_pairs={{0,4},{4,8},{8,12},{12,16},{16,20},{20,24},{24,28},{28,0},{1,5},{5... | collective-permute-start | bytes 1544 | tf_op jit(solution)/shard_map/while/body/eval_jaxpr/ppermute | solution.py:15
  75.8 11.9 %collective-permute-start = (bf16[128,128]{1,0:T(8,128)(2,1)S(1)}, bf16[128,128]{1,0:T(8,128)(2,1)S(1)}, u32[]{:S(2)}, u32[]{:S(2)}) collective-permute-start(bf16[128,128]{1,0:T(8,128)(2,1)S(1)} %copy.714), channel_id=1, source_target_pairs={{0,4},{4,8},{8,12},{12,16},{16,20},{20,24},{24,28},{28,0},{1,5},{5... | collective-permute-start | bytes 98312 | tf_op jit(solution)/shard_map/while/body/eval_jaxpr/ppermute | solution.py:15
  75.9 11.8 %collective-permute-start.1 = (bf16[128,128]{1,0:T(8,128)(2,1)S(1)}, bf16[128,128]{1,0:T(8,128)(2,1)S(1)}, u32[]{:S(2)}, u32[]{:S(2)}) collective-permute-start(bf16[128,128]{1,0:T(8,128)(2,1)S(1)} %copy.715), channel_id=1, source_target_pairs={{0,4},{4,8},{8,12},{12,16},{16,20},{20,24},{24,28},{28,0},{1,5},{5... | collective-permute-start | bytes 98312 | tf_op jit(solution)/shard_map/while/body/eval_jaxpr/ppermute | solution.py:15
  92.1 11.1 %collective-permute-start.4 = (f32[128]{0:T(128)S(1)}, f32[128]{0:T(128)S(1)}, u32[]{:S(2)}, u32[]{:S(2)}) collective-permute-start(f32[128]{0:T(128)S(1)} %copy.718), channel_id=1, source_target_pairs={{0,4},{4,8},{8,12},{12,16},{16,20},{20,24},{24,28},{28,0},{1,5},{5... | collective-permute-start | bytes 1544 | tf_op jit(solution)/shard_map/while/body/eval_jaxpr/ppermute | solution.py:15
  92.1 11.1 %collective-permute-start = (bf16[128,128]{1,0:T(8,128)(2,1)S(1)}, bf16[128,128]{1,0:T(8,128)(2,1)S(1)}, u32[]{:S(2)}, u32[]{:S(2)}) collective-permute-start(bf16[128,128]{1,0:T(8,128)(2,1)S(1)} %copy.714), channel_id=1, source_target_pairs={{0,4},{4,8},{8,12},{12,16},{16,20},{20,24},{24,28},{28,0},{1,5},{5... | collective-permute-start | bytes 98312 | tf_op jit(solution)/shard_map/while/body/eval_jaxpr/ppermute | solution.py:15
  92.2 11.0 %collective-permute-start.1 = (bf16[128,128]{1,0:T(8,128)(2,1)S(1)}, bf16[128,128]{1,0:T(8,128)(2,1)S(1)}, u32[]{:S(2)}, u32[]{:S(2)}) collective-permute-start(bf16[128,128]{1,0:T(8,128)(2,1)S(1)} %copy.715), channel_id=1, source_target_pairs={{0,4},{4,8},{8,12},{12,16},{16,20},{20,24},{24,28},{28,0},{1,5},{5... | collective-permute-start | bytes 98312 | tf_op jit(solution)/shard_map/while/body/eval_jaxpr/ppermute | solution.py:15
  107.5 11.9 %collective-permute-start.4 = (f32[128]{0:T(128)S(1)}, f32[128]{0:T(128)S(1)}, u32[]{:S(2)}, u32[]{:S(2)}) collective-permute-start(f32[128]{0:T(128)S(1)} %copy.718), channel_id=1, source_target_pairs={{0,4},{4,8},{8,12},{12,16},{16,20},{20,24},{24,28},{28,0},{1,5},{5... | collective-permute-start | bytes 1544 | tf_op jit(solution)/shard_map/while/body/eval_jaxpr/ppermute | solution.py:15
  107.5 11.9 %collective-permute-start = (bf16[128,128]{1,0:T(8,128)(2,1)S(1)}, bf16[128,128]{1,0:T(8,128)(2,1)S(1)}, u32[]{:S(2)}, u32[]{:S(2)}) collective-permute-start(bf16[128,128]{1,0:T(8,128)(2,1)S(1)} %copy.714), channel_id=1, source_target_pairs={{0,4},{4,8},{8,12},{12,16},{16,20},{20,24},{24,28},{28,0},{1,5},{5... | collective-permute-start | bytes 98312 | tf_op jit(solution)/shard_map/while/body/eval_jaxpr/ppermute | solution.py:15
  107.6 11.8 %collective-permute-start.1 = (bf16[128,128]{1,0:T(8,128)(2,1)S(1)}, bf16[128,128]{1,0:T(8,128)(2,1)S(1)}, u32[]{:S(2)}, u32[]{:S(2)}) collective-permute-start(bf16[128,128]{1,0:T(8,128)(2,1)S(1)} %copy.715), channel_id=1, source_target_pairs={{0,4},{4,8},{8,12},{12,16},{16,20},{20,24},{24,28},{28,0},{1,5},{5... | collective-permute-start | bytes 98312 | tf_op jit(solution)/shard_map/while/body/eval_jaxpr/ppermute | solution.py:15
  123.8 11.1 %collective-permute-start.4 = (f32[128]{0:T(128)S(1)}, f32[128]{0:T(128)S(1)}, u32[]{:S(2)}, u32[]{:S(2)}) collective-permute-start(f32[128]{0:T(128)S(1)} %copy.718), channel_id=1, source_target_pairs={{0,4},{4,8},{8,12},{12,16},{16,20},{20,24},{24,28},{28,0},{1,5},{5... | collective-permute-start | bytes 1544 | tf_op jit(solution)/shard_map/while/body/eval_jaxpr/ppermute | solution.py:15
  123.8 11.1 %collective-permute-start = (bf16[128,128]{1,0:T(8,128)(2,1)S(1)}, bf16[128,128]{1,0:T(8,128)(2,1)S(1)}, u32[]{:S(2)}, u32[]{:S(2)}) collective-permute-start(bf16[128,128]{1,0:T(8,128)(2,1)S(1)} %copy.714), channel_id=1, source_target_pairs={{0,4},{4,8},{8,12},{12,16},{16,20},{20,24},{24,28},{28,0},{1,5},{5... | collective-permute-start | bytes 98312 | tf_op jit(solution)/shard_map/while/body/eval_jaxpr/ppermute | solution.py:15
  123.9 11.0 %collective-permute-start.1 = (bf16[128,128]{1,0:T(8,128)(2,1)S(1)}, bf16[128,128]{1,0:T(8,128)(2,1)S(1)}, u32[]{:S(2)}, u32[]{:S(2)}) collective-permute-start(bf16[128,128]{1,0:T(8,128)(2,1)S(1)} %copy.715), channel_id=1, source_target_pairs={{0,4},{4,8},{8,12},{12,16},{16,20},{20,24},{24,28},{28,0},{1,5},{5... | collective-permute-start | bytes 98312 | tf_op jit(solution)/shard_map/while/body/eval_jaxpr/ppermute | solution.py:15
  139.3 11.9 %collective-permute-start.4 = (f32[128]{0:T(128)S(1)}, f32[128]{0:T(128)S(1)}, u32[]{:S(2)}, u32[]{:S(2)}) collective-permute-start(f32[128]{0:T(128)S(1)} %copy.718), channel_id=1, source_target_pairs={{0,4},{4,8},{8,12},{12,16},{16,20},{20,24},{24,28},{28,0},{1,5},{5... | collective-permute-start | bytes 1544 | tf_op jit(solution)/shard_map/while/body/eval_jaxpr/ppermute | solution.py:15
  139.3 11.9 %collective-permute-start = (bf16[128,128]{1,0:T(8,128)(2,1)S(1)}, bf16[128,128]{1,0:T(8,128)(2,1)S(1)}, u32[]{:S(2)}, u32[]{:S(2)}) collective-permute-start(bf16[128,128]{1,0:T(8,128)(2,1)S(1)} %copy.714), channel_id=1, source_target_pairs={{0,4},{4,8},{8,12},{12,16},{16,20},{20,24},{24,28},{28,0},{1,5},{5... | collective-permute-start | bytes 98312 | tf_op jit(solution)/shard_map/while/body/eval_jaxpr/ppermute | solution.py:15
  139.4 11.8 %collective-permute-start.1 = (bf16[128,128]{1,0:T(8,128)(2,1)S(1)}, bf16[128,128]{1,0:T(8,128)(2,1)S(1)}, u32[]{:S(2)}, u32[]{:S(2)}) collective-permute-start(bf16[128,128]{1,0:T(8,128)(2,1)S(1)} %copy.715), channel_id=1, source_target_pairs={{0,4},{4,8},{8,12},{12,16},{16,20},{20,24},{24,28},{28,0},{1,5},{5... | collective-permute-start | bytes 98312 | tf_op jit(solution)/shard_map/while/body/eval_jaxpr/ppermute | solution.py:15
  (26 other events, 132.6 us)
where the time goes:
time: 197 us; the launch traced here: 196 us
  waiting for transfers between devices  69.1 us (35%)
  starting transfers between devices  46.8 us (24%)
  local copies, waits for them, and re-layouts  26.8 us (14%)
  loops' own time  20.5 us (10%)
  matrix products  20.1 us (10%)
  other arithmetic  9.31 us (5%)
  between operations  3.36 us (2%)
    ppermute x37, waiting for transfers between devices, from_behind(): lax.ppermute(array, axis, [(i, (i + by) % count) for i in range(count)])  34.6 us
    ppermute x37, starting transfers between devices, from_behind(): lax.ppermute(array, axis, [(i, (i + by) % count) for i in range(count)])  20.6 us
    another operation x1, loops' own time, on_device(): lax.fori_loop(0, lax.axis_size('ctx') - 1, cycle_turn, (grad_query, trave...  18.6 us
    all_to_all x1, starting transfers between devices, on_device(): lax.all_to_all(key_input, 'head', split_axis=1, concat_axis=0, tiled=True)  6.35 us
    reduce_or x8, other arithmetic, pair_terms(): jnp.any(query_pos[rows_here][:, None] >= key_pos[cols_here][None, :])  6.03 us
    all_to_all x1, waiting for transfers between devices, on_device(): lax.all_to_all(query_input, 'head', split_axis=1, concat_axis=0, tiled=True)  5.87 us
    all_to_all x1, waiting for transfers between devices, on_device(): lax.all_to_all(output_gradient, 'head', split_axis=1, concat_axis=0, tile...  5.79 us
    all_to_all x1, waiting for transfers between devices, on_device(): lax.all_to_all(value_input, 'head', split_axis=1, concat_axis=0, tiled=True)  5.6 us
  transfers between devices with their start and end apart: 44, of which 22 were waited for; matrix products, arithmetic and copies ran while one was open for 24% of the time, Pallas kernels for 0%

commit v1 on v0

--- a/solution.py
+++ b/solution.py
@@ -1,9 +1,16 @@
 import jax
 import jax.numpy as jnp
 from jax import lax
+from jax.experimental import pallas as pl
+from jax.experimental.pallas import tpu as pltpu
 from jax.sharding import PartitionSpec as P
 
 HEAD_WIDTH = 64
+LANES = 128
+PIECES = 2
+MASKED = 16384.0
+F32 = jnp.float32
+BF16 = jnp.bfloat16
 
 
 def for_sending(array):
@@ -205,9 +212,359 @@
     return (query_out, key_out, value_out)
 
 
+def lane_of(shape):
+    return lax.broadcasted_iota(jnp.int32, shape, len(shape) - 1)
+
+
+def pack_kernel(pos_ref, q_ref, g_ref, k_ref, v_ref, n_ref, d_ref, out_ref, wide_ref):
+    rows = q_ref.shape[0]
+    planes = n_ref.shape[0] // rows
+    block = lax.axis_index("ctx")
+    kv_heads = out_ref.shape[0]
+    group = q_ref.shape[1] // k_ref.shape[1]
+    lane = lane_of((rows, LANES))
+    low = lane < HEAD_WIDTH
+    scale = HEAD_WIDTH ** (-0.5)
+    for m in range(q_ref.shape[1] // LANES):
+        cols = slice(m * LANES, (m + 1) * LANES)
+        q = q_ref[:, cols].astype(F32) * scale
+        g = g_ref[:, cols].astype(F32)
+        c, e = (2 * m) // group, (2 * m) % group
+        even = jnp.where(low, q, pltpu.roll(g, HEAD_WIDTH, 1))
+        odd = jnp.where(low, pltpu.roll(q, HEAD_WIDTH, 1), g)
+        out_ref[c, e * rows : (e + 1) * rows, :] = even.astype(BF16)
+        out_ref[c, (e + 1) * rows : (e + 2) * rows, :] = odd.astype(BF16)
+    at = group * rows
+    for m in range(k_ref.shape[1] // LANES):
+        cols = slice(m * LANES, (m + 1) * LANES)
+        k = k_ref[:, cols].astype(F32)
+        v = v_ref[:, cols].astype(F32)
+        even = jnp.where(low, k, pltpu.roll(v, HEAD_WIDTH, 1))
+        odd = jnp.where(low, pltpu.roll(k, HEAD_WIDTH, 1), v)
+        out_ref[2 * m, at : at + rows, :] = even.astype(BF16)
+        out_ref[2 * m + 1, at : at + rows, :] = odd.astype(BF16)
+    at = at + rows
+    tall = n_ref.shape[0]
+    wide_ref[...] = jnp.zeros(wide_ref.shape, F32)
+    wide_ref[0, :, 0 : n_ref.shape[1]] = n_ref[...]
+    wide_ref[1, :, 0 : d_ref.shape[1]] = d_ref[...]
+    tall_lane = lane_of((tall, LANES))
+    row_half = tall // 2
+    lead = (pos_ref[0] // row_half).astype(F32)
+    for parity in range(2):
+        spread = jnp.zeros((tall, LANES), F32)
+        for t in range(2):
+            rest = wide_ref[t]
+            for s in range(PIECES):
+                piece = rest.astype(BF16).astype(F32)
+                rest = rest - piece
+                to = s * 2 * group + t * group
+                here = (tall_lane >= to) & (tall_lane < to + group)
+                moved = pltpu.roll(piece, (to - group * parity) % LANES, 1)
+                spread = jnp.where(here, moved, spread)
+        width = PIECES * 2 * group
+        tile = jnp.zeros((rows, LANES), F32)
+        for h in range(planes):
+            part = spread[h * rows : (h + 1) * rows]
+            moved = pltpu.roll(part, h * width, 1) if h else part
+            tile = jnp.where((lane >= h * width) & (lane < (h + 1) * width), moved, tile)
+        first = planes * width
+        mine = (lane >= first) & (lane < first + planes * kv_heads) & (lane % kv_heads == block)
+        tile = jnp.where(mine, lead, tile).astype(BF16)
+        for c in range(parity, kv_heads, 2):
+            out_ref[c, at : at + rows, :] = tile
+
+
+def spread_kernel(in_ref, own_ref, *send_refs):
+    blocks, double, _ = in_ref.shape
+    rows = double // 2
+    plane = lax.axis_index("head")
+    width = LANES // blocks
+    lane = lane_of((rows, LANES))
+    kv = in_ref[:, 0:rows, :].reshape(blocks * rows, LANES)
+    tiles = [in_ref[b, rows:double, :].astype(F32) for b in range(blocks)]
+    for j in range(len(send_refs) + 1):
+        wanted = plane ^ j
+        tile = jnp.zeros((rows, LANES), F32)
+        for b in range(blocks):
+            shift = lax.rem(b * width - wanted * width + LANES, LANES)
+            here = (lane >= b * width) & (lane < (b + 1) * width)
+            tile = jnp.where(here, pltpu.roll(tiles[b], shift, 1), tile)
+        if j == 0:
+            own_ref[...] = tile.astype(BF16)
+        else:
+            send_refs[j - 1][0 : blocks * rows, :] = kv
+            send_refs[j - 1][blocks * rows : (blocks + 1) * rows, :] = tile.astype(BF16)
+
+
+def make_attend(planes):
+    def attend_kernel(in_ref, own_ref, *refs):
+        got = refs[: planes - 1]
+        out_ref, sum_ref = refs[planes - 1 : planes + 1]
+        send_refs = refs[planes + 1 : 2 * planes]
+        left_ref, right_ref, both_ref, prob_ref, score_ref = refs[2 * planes :]
+        blocks = in_ref.shape[0]
+        rows = own_ref.shape[0]
+        group = in_ref.shape[1] // rows - 2
+        tokens = blocks * rows
+        width = LANES // blocks
+        plane = lax.axis_index("head")
+        holder = plane ^ (lax.axis_index("ctx") // (blocks // planes))
+        lane = lane_of((rows, LANES))
+        lane_row = lane_of((1, LANES))
+        first = planes * width
+
+        tile = own_ref[...].astype(F32)
+        for j in range(1, planes):
+            other = got[j - 1][tokens : tokens + rows, :].astype(F32)
+            tile = jnp.where(holder == j, other, tile)
+        folds = (tile, pltpu.roll(tile, LANES // 2, 1))
+
+        lead = jnp.zeros((1, LANES), F32)
+        for b in range(blocks):
+            at = (group + 1) * rows
+            lead = lead + in_ref[b, at : at + rows, :].astype(F32)[0:1]
+        key_plane = (lane_row - first) // blocks
+        per_half = planes // 2
+        count = 2 * blocks
+
+        def place(lead_of, which):
+            front = per_half * lead_of + which
+            back = per_half * (count - 1 - lead_of) + (which - per_half)
+            return jnp.where(which < per_half, front, back)
+
+        key_place = place(lead, key_plane.astype(F32))
+        in_mask = (lane_row >= first) & (lane_row < first + planes * blocks)
+
+        low = lane_of((tokens, LANES)) < HEAD_WIDTH
+        nothing = jnp.zeros((tokens, LANES), BF16)
+        for e in range(group):
+            pair = in_ref[:, e * rows : (e + 1) * rows, :].reshape(tokens, LANES)
+            both_ref[e * tokens : (e + 1) * tokens, :] = pair
+            right_ref[e, 0:tokens, 0:LANES] = jnp.where(low, pair, nothing)
+            right_ref[e, tokens : 2 * tokens, 0:LANES] = jnp.where(low, nothing, pair)
+        for b in range(blocks):
+            lead_b = jnp.sum(
+                jnp.where(lane_row == first + b, lead, 0.0), axis=1, keepdims=True
+            )
+            query_place = place(lead_b, plane.astype(F32))
+            hidden = jnp.where(in_mask & (key_place > query_place), MASKED, 0.0)
+            fold = folds[(b * width) // (LANES // 2)]
+            at = (b * width) % (LANES // 2)
+            near = (lane >= at) & (lane < at + width)
+            for e in range(group):
+                norm = jnp.where(near & (lane % (2 * group) == e), fold, hidden)
+                delta = jnp.where(near & (lane % (2 * group) == group + e), fold, 0.0)
+                down = slice(b * rows, (b + 1) * rows)
+                right_ref[e, down, LANES:] = norm.astype(BF16)
+                down = slice(tokens + b * rows, tokens + (b + 1) * rows)
+                right_ref[e, down, LANES:] = delta.astype(BF16)
+
+        key_row = lax.broadcasted_iota(jnp.int32, (tokens, LANES), 0)
+        wide_lane = lane_of((tokens, LANES))
+        square_key = lax.broadcasted_iota(jnp.int32, (tokens, tokens), 0)
+        square_query = lane_of((tokens, tokens))
+        allowed = (square_key <= square_query) | (square_key // rows != square_query // rows)
+        query_sum = None
+        for j in range(planes):
+            if j == 0:
+                kv = in_ref[:, group * rows : (group + 1) * rows, :].reshape(tokens, LANES)
+            else:
+                kv = got[j - 1][0:tokens, :]
+            mark = first + (plane ^ j) * blocks + key_row // rows
+            ones = jnp.where((wide_lane < first) | (wide_lane == mark), -1.0, 0.0)
+            left_ref[:, 0:LANES] = kv
+            left_ref[:, LANES:] = ones.astype(BF16)
+            for e in range(group):
+                both = lax.dot_general(
+                    left_ref[...],
+                    right_ref[e],
+                    (((1,), (1,)), ((), ())),
+                    preferred_element_type=F32,
+                )
+                prob = jnp.exp(both[:, 0:tokens])
+                if j == 0:
+                    prob = jnp.where(allowed, prob, 0.0)
+                score = prob * both[:, tokens:]
+                across = slice(e * tokens, (e + 1) * tokens)
+                prob_ref[:, across] = prob.astype(BF16)
+                score_ref[:, across] = score.astype(BF16)
+            value_side = jnp.dot(prob_ref[...], both_ref[...], preferred_element_type=F32)
+            key_side = jnp.dot(score_ref[...], both_ref[...], preferred_element_type=F32)
+            kv_sum = jnp.where(low, key_side, value_side)
+            if j == 0:
+                sum_ref[...] = kv_sum
+            else:
+                send_refs[j - 1][...] = kv_sum.astype(BF16)
+            turned = kv.astype(F32).T[0:HEAD_WIDTH].astype(BF16)
+            part = jnp.dot(turned, score_ref[...], preferred_element_type=F32)
+            query_sum = part if query_sum is None else query_sum + part
+        scale = HEAD_WIDTH ** (-0.5)
+        for m in range(group // 2):
+            pair = jnp.concatenate(
+                [
+                    query_sum[:, 2 * m * tokens : (2 * m + 1) * tokens],
+                    query_sum[:, (2 * m + 1) * tokens : (2 * m + 2) * tokens],
+                ],
+                0,
+            )
+            done = (pair.T * scale).astype(BF16)
+            out_ref[:, m * rows : (m + 1) * rows, :] = done.reshape(blocks, rows, LANES)
+
+    return attend_kernel
+
+
+def total_kernel(sum_ref, *refs):
+    got, out_ref = refs[:-2], refs[-1]
+    total = sum_ref[...]
+    for ref in got:
+        total = total + ref[...].astype(F32)
+    out_ref[...] = total.astype(BF16).reshape(out_ref.shape)
+
+
+def unpack_kernel(in_ref, q_ref, k_ref, v_ref):
+    rows = q_ref.shape[0]
+    heads = in_ref.shape[0]
+    tiles = in_ref.shape[1] // rows - 1
+    low = lane_of((rows, LANES)) < HEAD_WIDTH
+    for c in range(heads):
+        for m in range(tiles):
+            at = (c * tiles + m) * LANES
+            q_ref[:, at : at + LANES] = in_ref[c, m * rows : (m + 1) * rows, :]
+    for m in range(heads // 2):
+        even = in_ref[2 * m, tiles * rows : (tiles + 1) * rows, :].astype(F32)
+        odd = in_ref[2 * m + 1, tiles * rows : (tiles + 1) * rows, :].astype(F32)
+        cols = slice(m * LANES, (m + 1) * LANES)
+        k_ref[:, cols] = jnp.where(low, even, pltpu.roll(odd, HEAD_WIDTH, 1)).astype(BF16)
+        v_ref[:, cols] = jnp.where(low, pltpu.roll(even, HEAD_WIDTH, 1), odd).astype(BF16)
+
+
+def whole(shape):
+    return pl.BlockSpec(shape, lambda: (0,) * len(shape))
+
+
+def by_heads(
+    query_input,
+    key_input,
+    value_input,
+    output_gradient,
+    log_softmax_norm,
+    output_delta_rows,
+    positions,
+):
+    blocks = lax.axis_size("ctx")
+    planes = lax.axis_size("head")
+    rows = query_input.shape[0]
+    tokens = blocks * rows
+    group = query_input.shape[1] // key_input.shape[1]
+    packet = (group + 2) * rows
+    tall = positions.shape[0]
+    packed = pl.pallas_call(
+        pack_kernel,
+        name="pack",
+        out_shape=jax.ShapeDtypeStruct((blocks, packet, LANES), BF16),
+        in_specs=[pl.BlockSpec(memory_space=pltpu.SMEM)]
+        + [
+            whole(a.shape)
+            for a in (
+                query_input,
+                output_gradient,
+                key_input,
+                value_input,
+                log_softmax_norm,
+                output_delta_rows,
+            )
+        ],
+        out_specs=whole((blocks, packet, LANES)),
+        scratch_shapes=[pltpu.VMEM((2, tall, LANES), F32)],
+    )(
+        positions,
+        query_input,
+        output_gradient,
+        key_input,
+        value_input,
+        log_softmax_norm,
+        output_delta_rows,
+    )
+    packed = lax.all_to_all(packed, "ctx", split_axis=0, concat_axis=0, tiled=True)
+    sent = jax.ShapeDtypeStruct((tokens + rows, LANES), BF16)
+    own, *sends = pl.pallas_call(
+        spread_kernel,
+        name="spread",
+        grid=(1,),
+        out_shape=[jax.ShapeDtypeStruct((rows, LANES), BF16)] + [sent] * (planes - 1),
+        in_specs=[pl.BlockSpec((blocks, 2 * rows, LANES), lambda i: (0, group // 2, 0))],
+        out_specs=[pl.BlockSpec((rows, LANES), lambda i: (0, 0))]
+        + [pl.BlockSpec((tokens + rows, LANES), lambda i: (0, 0))] * (planes - 1),
+    )(packed)
+
+    def swap(array, by):
+        return lax.ppermute(array, "head", [(i, i ^ by) for i in range(planes)])
+
+    got = [swap(sends[j - 1], j) for j in range(1, planes)]
+    part = jax.ShapeDtypeStruct((tokens, LANES), BF16)
+    packet = (group // 2 + 1) * rows
+    back, total, *parts = pl.pallas_call(
+        make_attend(planes),
+        name="attend",
+        out_shape=[
+            jax.ShapeDtypeStruct((blocks, packet, LANES), BF16),
+            jax.ShapeDtypeStruct((tokens, LANES), F32),
+        ]
+        + [part] * (planes - 1),
+        in_specs=[whole(packed.shape), whole(own.shape)] + [whole(g.shape) for g in got],
+        out_specs=[whole((blocks, packet, LANES)), whole((tokens, LANES))]
+        + [whole((tokens, LANES))] * (planes - 1),
+        scratch_shapes=[
+            pltpu.VMEM((tokens, 2 * LANES), BF16),
+            pltpu.VMEM((group, 2 * tokens, 2 * LANES), BF16),
+            pltpu.VMEM((group * tokens, LANES), BF16),
+            pltpu.VMEM((tokens, group * tokens), BF16),
+            pltpu.VMEM((tokens, group * tokens), BF16),
+        ],
+    )(packed, own, *got)
+    parts = [swap(parts[j - 1], j) for j in range(1, planes)]
+    last = pl.BlockSpec((blocks, rows, LANES), lambda i: (0, group // 2, 0))
+    flat = pl.BlockSpec((tokens, LANES), lambda i: (0, 0))
+    back = pl.pallas_call(
+        total_kernel,
+        name="total",
+        grid=(1,),
+        out_shape=jax.ShapeDtypeStruct(back.shape, BF16),
+        in_specs=[flat] * planes + [pl.BlockSpec(memory_space=pl.ANY)],
+        out_specs=last,
+        input_output_aliases={planes: 0},
+    )(total, *parts, back)
+    back = lax.all_to_all(back, "ctx", split_axis=0, concat_axis=0, tiled=True)
+    shapes = [query_input.shape, key_input.shape, value_input.shape]
+    return tuple(
+        pl.pallas_call(
+            unpack_kernel,
+            name="unpack",
+            out_shape=[jax.ShapeDtypeStruct(s, BF16) for s in shapes],
+            in_specs=[whole(back.shape)],
+            out_specs=[whole(s) for s in shapes],
+        )(back)
+    )
+
+
 def solution(mesh):
+    def on_each(*args):
+        query_input, key_input = args[0], args[1]
+        kv_heads = key_input.shape[1] // HEAD_WIDTH
+        group = query_input.shape[1] // key_input.shape[1]
+        blocks, planes = mesh.shape["ctx"], mesh.shape["head"]
+        by_head = (
+            blocks == kv_heads
+            and group == 4
+            and planes == 4
+            and kv_heads == 8
+            and query_input.shape[0] % 16 == 0
+        )
+        return (by_heads if by_head else on_device)(*args)
+
     return jax.shard_map(
-        on_device,
+        on_each,
         mesh=mesh,
         in_specs=(
             P(("ctx", "head"), None),

time: 197 us -> 59.9 us (0.30)
  waiting for transfers between devices: 69.1 us -> 10.9 us
  starting transfers between devices: 46.8 us -> 8.81 us
  blocking collectives: 0 us -> 23.8 us
  local copies, waits for them, and re-layouts: 26.8 us -> 3.4 us
  loops' own time: 20.5 us -> 0 us
  matrix products: 20.1 us -> 0 us
  Pallas kernels: 0 us -> 11.9 us
  other arithmetic: 9.31 us -> 0 us
  between operations: 3.36 us -> 0.66 us
    all_to_all x7 -> x0, waiting for transfers between devices: 34.5 us -> none  [the longest x1 5.87 us: on_device(): lax.all_to_all(query_input, 'head', split_axis=1, concat_axis=0, tiled=True)]
    all_to_all x7 -> x0, starting transfers between devices: 26.2 us -> none  [the longest x1 6.35 us: on_device(): lax.all_to_all(key_input, 'head', split_axis=1, concat_axis=0, tiled=True)]
    all_to_all x0 -> x2, blocking collectives: none -> 23.8 us  [the longest x1 13.6 us: by_heads(): lax.all_to_all(packed, 'ctx', split_axis=0, concat_axis=0, tiled=True)]
    ppermute x37 -> x6, waiting for transfers between devices: 34.6 us -> 10.9 us  [swap(): return lax.ppermute(array, 'head', [(i, i ^ by) for i in range(planes)])]
    another operation x33 -> x0, loops' own time: 20.5 us -> none  [the longest x1 18.6 us: on_device(): lax.fori_loop(0, lax.axis_size('ctx') - 1, cycle_turn, (grad_query, trave...]
    dot_general x85 -> x0, matrix products: 20.1 us -> none  [the longest x17 4.51 us: block_terms(): jnp.einsum('qhgd,khd->qhgk', query_per_head, key_per_head, preferred_elem...]
    reshape x119 -> x0, local copies, waits for them, and re-layouts: 13.5 us -> none  [the longest x17 2.74 us: block_terms(): query_term.reshape(row_count, -1)]
    pallas_call x0 -> x5, Pallas kernels: none -> 11.9 us  [the longest x1 4.77 us: by_heads(): pl.pallas_call(make_attend(planes), name='attend', out_shape=[jax.ShapeDt...]
  transfers between devices with their start and end apart: 44 -> 6, of which waited for: 22 -> 6; matrix products, arithmetic and copies ran while one was open for 24% -> 0% of each run, Pallas kernels for 0% -> 0%
where the time goes in v1:
time: 59.9 us; the launch traced here: 59.4 us
  blocking collectives  23.8 us (40%)
  Pallas kernels  11.9 us (20%)
  waiting for transfers between devices  10.9 us (18%)
  starting transfers between devices  8.81 us (15%)
  local copies, waits for them, and re-layouts  3.4 us (6%)
  between operations  0.66 us (1%)
    all_to_all x1, blocking collectives, by_heads(): lax.all_to_all(packed, 'ctx', split_axis=0, concat_axis=0, tiled=True)  13.6 us
    ppermute x6, waiting for transfers between devices, swap(): return lax.ppermute(array, 'head', [(i, i ^ by) for i in range(planes)])  10.9 us
    all_to_all x1, blocking collectives, by_heads(): back = lax.all_to_all(back, 'ctx', split_axis=0, concat_axis=0, tiled=True)  10.2 us
    ppermute x6, starting transfers between devices, swap(): return lax.ppermute(array, 'head', [(i, i ^ by) for i in range(planes)])  8.81 us
    pallas_call x1, Pallas kernels, by_heads(): pl.pallas_call(make_attend(planes), name='attend', out_shape=[jax.ShapeDt...  4.77 us
    unnamed x16, local copies, waits for them, and re-layouts  3.4 us
    pallas_call x1, Pallas kernels, by_heads(): pl.pallas_call(pack_kernel, name='pack', out_shape=jax.ShapeDtypeStruct((...  2.15 us
    pallas_call x1, Pallas kernels, by_heads(): pl.pallas_call(spread_kernel, name='spread', grid=(1,), out_shape=[jax.Sh...  1.7 us
  transfers between devices with their start and end apart: 6, of which 6 were waited for; matrix products, arithmetic and copies ran while one was open for 0% of the time, Pallas kernels for 0%

profile of v1, /device:TPU:0, one launch (start us, length us, event | category | flops | bytes accessed | tf_op | source)
XLA Modules:
  0.0 59.4 jit_solution(902551802812425141)
XLA Ops:
  0.6 1.4 %copy.11.n_ref = f32[128,8]{1,0:T(8,128)} copy(f32[128,8]{0,1:T(8,128)} %param.11) | data formatting | bytes 8192 | tf_op args[4]
  2.1 0.7 %copy.12.d_ref = f32[128,8]{1,0:T(8,128)} copy(f32[128,8]{0,1:T(8,128)S(1)} %copy-done.6) | data formatting | bytes 8192 | tf_op args[5]
  2.8 2.2 %pack.1 = bf16[8,192,128]{2,1,0:T(8,128)(2,1)} custom-call(s32[128]{0:T(128)} %pos_ref.1, bf16[32,2048]{1,0:T(8,128)(2,1)} %q_ref.1, bf16[32,2048]{1,0:T(8,128)(2,1)} %g_ref.1, bf16[32,512]{1,0:T(8,128)(2,1)} %k_ref.1, bf16[32,512]{1,0:T(8,128)(2,1)} %v_ref.1, f32[128,8]{1,0:T(8,128)} %copy.11.n_ref, f32[128,8]{1,0:T(8,128)} %copy.12.d_ref), custom_call_target="tpu_custom_call" | custom-call | tf_op jit(solution)/shard_map/pack/pallas_call | solution.py:462
  4.9 13.6 %all_to_all.10.in_ref = bf16[8,192,128]{2,1,0:T(8,128)(2,1)} all-to-all(bf16[8,192,128]{2,1,0:T(8,128)(2,1)} %pack.1), channel_id=1, replica_groups=mesh['ctx'=8,'head'=4] {'ctx'}, dimensions={0} | all-to-all | bytes 786432 | tf_op jit(solution)/shard_map/all_to_all | solution.py:489
  18.5 1.7 %spread.1 = (bf16[32,128]{1,0:T(8,128)(2,1)}, bf16[288,128]{1,0:T(8,128)(2,1)}, bf16[288,128]{1,0:T(8,128)(2,1)}, bf16[288,128]{1,0:T(8,128)(2,1)}) custom-call(bf16[8,192,128]{2,1,0:T(8,128)(2,1)} %all_to_all.10.in_ref), custom_call_target="tpu_custom_call" | custom-call | tf_op jit(solution)/shard_map/spread/pallas_call | solution.py:491
  20.2 1.8 %collective-permute-start = (bf16[288,128]{1,0:T(8,128)(2,1)}, bf16[288,128]{1,0:T(8,128)(2,1)S(1)}, u32[]{:S(2)}, u32[]{:S(2)}) collective-permute-start(bf16[288,128]{1,0:T(8,128)(2,1)} %get-tuple-element.13), channel_id=1, source_target_pairs={{0,1},{1,0},{2,3},{3,2},{4,5},{5,4},{6,7},{7,6},{8,9},{9,8},{10,11... | collective-permute-start | bytes 221192 | tf_op jit(solution)/shard_map/ppermute | solution.py:502
  22.1 2.6 %collective-permute-start.1 = (bf16[288,128]{1,0:T(8,128)(2,1)}, bf16[288,128]{1,0:T(8,128)(2,1)S(1)}, u32[]{:S(2)}, u32[]{:S(2)}) collective-permute-start(bf16[288,128]{1,0:T(8,128)(2,1)} %get-tuple-element.14), channel_id=1, source_target_pairs={{0,2},{1,3},{2,0},{3,1},{4,6},{5,7},{6,4},{7,5},{8,10},{9,11},{10,... | collective-permute-start | bytes 221192 | tf_op jit(solution)/shard_map/ppermute | solution.py:502
  24.7 0.0 collective-permute-start.2
  24.7 0.1 collective-permute-done.refs_0_
  24.8 5.0 %collective-permute-done.1.refs_1_ = bf16[288,128]{1,0:T(8,128)(2,1)S(1)} collective-permute-done((bf16[288,128]{1,0:T(8,128)(2,1)}, bf16[288,128]{1,0:T(8,128)(2,1)S(1)}, u32[]{:S(2)}, u32[]{:S(2)}) %collective-permute-start.1) | collective-permute-done | bytes 73760 | tf_op jit(solution)/shard_map/ppermute | solution.py:502
  29.8 1.3 %collective-permute-done.2.refs_2_ = bf16[288,128]{1,0:T(8,128)(2,1)S(1)} collective-permute-done((bf16[288,128]{1,0:T(8,128)(2,1)}, bf16[288,128]{1,0:T(8,128)(2,1)S(1)}, u32[]{:S(2)}, u32[]{:S(2)}) %collective-permute-start.2) | collective-permute-done | bytes 73760 | tf_op jit(solution)/shard_map/ppermute | solution.py:502
  31.1 0.0 copy-done
  31.1 0.6 %copy-done.2 = bf16[288,128]{1,0:T(8,128)(2,1)} copy-done((bf16[288,128]{1,0:T(8,128)(2,1)}, bf16[288,128]{1,0:T(8,128)(2,1)S(1)}, u32[]{:S(2)}) %copy-start.2) | copy-done | bytes 73752
  31.8 4.8 %attend.1 = (bf16[8,96,128]{2,1,0:T(8,128)(2,1)}, f32[256,128]{1,0:T(8,128)}, bf16[256,128]{1,0:T(8,128)(2,1)}, bf16[256,128]{1,0:T(8,128)(2,1)}, bf16[256,128]{1,0:T(8,128)(2,1)}) custom-call(bf16[8,192,128]{2,1,0:T(8,128)(2,1)} %all_to_all.10.in_ref, bf16[32,128]{1,0:T(8,128)(2,1)} %get-tuple-element.12.own_ref, bf16[288,128]{1,0:T(8,128)(2,1)} %copy-done, ...), custom_call_target="tpu_custom_call" | custom-call | tf_op jit(solution)/shard_map/attend/pallas_call | solution.py:507
  36.5 0.8 %collective-permute-start.3 = (bf16[256,128]{1,0:T(8,128)(2,1)}, bf16[256,128]{1,0:T(8,128)(2,1)S(1)}, u32[]{:S(2)}, u32[]{:S(2)}) collective-permute-start(bf16[256,128]{1,0:T(8,128)(2,1)} %get-tuple-element.17), channel_id=1, source_target_pairs={{0,1},{1,0},{2,3},{3,2},{4,5},{5,4},{6,7},{7,6},{8,9},{9,8},{10,11... | collective-permute-start | bytes 196616 | tf_op jit(solution)/shard_map/ppermute | solution.py:502
  37.3 1.7 %collective-permute-start.4 = (bf16[256,128]{1,0:T(8,128)(2,1)}, bf16[256,128]{1,0:T(8,128)(2,1)S(1)}, u32[]{:S(2)}, u32[]{:S(2)}) collective-permute-start(bf16[256,128]{1,0:T(8,128)(2,1)} %get-tuple-element.18), channel_id=1, source_target_pairs={{0,2},{1,3},{2,0},{3,1},{4,6},{5,7},{6,4},{7,5},{8,10},{9,11},{10,... | collective-permute-start | bytes 196616 | tf_op jit(solution)/shard_map/ppermute | solution.py:502
  39.1 1.9 %collective-permute-start.5 = (bf16[256,128]{1,0:T(8,128)(2,1)}, bf16[256,128]{1,0:T(8,128)(2,1)S(1)}, u32[]{:S(2)}, u32[]{:S(2)}) collective-permute-start(bf16[256,128]{1,0:T(8,128)(2,1)} %get-tuple-element.19), channel_id=1, source_target_pairs={{0,3},{1,2},{2,1},{3,0},{4,7},{5,6},{6,5},{7,4},{8,11},{9,10},{10,... | collective-permute-start | bytes 196616 | tf_op jit(solution)/shard_map/ppermute | solution.py:502
  40.9 0.1 collective-permute-done.3.refs_0_
  41.0 2.8 %collective-permute-done.4.refs_1_ = bf16[256,128]{1,0:T(8,128)(2,1)S(1)} collective-permute-done((bf16[256,128]{1,0:T(8,128)(2,1)}, bf16[256,128]{1,0:T(8,128)(2,1)S(1)}, u32[]{:S(2)}, u32[]{:S(2)}) %collective-permute-start.4) | collective-permute-done | bytes 65568 | tf_op jit(solution)/shard_map/ppermute | solution.py:502
  43.8 1.6 %collective-permute-done.5.refs_2_ = bf16[256,128]{1,0:T(8,128)(2,1)S(1)} collective-permute-done((bf16[256,128]{1,0:T(8,128)(2,1)}, bf16[256,128]{1,0:T(8,128)(2,1)S(1)}, u32[]{:S(2)}, u32[]{:S(2)}) %collective-permute-start.5) | collective-permute-done | bytes 65568 | tf_op jit(solution)/shard_map/ppermute | solution.py:502
  45.3 0.6 %copy-done.5 = bf16[256,128]{1,0:T(8,128)(2,1)} copy-done((bf16[256,128]{1,0:T(8,128)(2,1)}, bf16[256,128]{1,0:T(8,128)(2,1)S(1)}, u32[]{:S(2)}) %copy-start.5) | copy-done | bytes 65560
  45.9 1.6 %total.1 = bf16[8,96,128]{2,1,0:T(8,128)(2,1)} custom-call(f32[256,128]{1,0:T(8,128)} %get-tuple-element.16.sum_ref, bf16[256,128]{1,0:T(8,128)(2,1)} %copy-done.3, bf16[256,128]{1,0:T(8,128)(2,1)} %copy-done.4, bf16[256,128]{1,0:T(8,128)(2,1)} %copy-done.5, bf16[8,96,128]{2,1,0:T(8,128)(2,1)} %get-tuple-element.20.refs_3_), custom_call_target="tpu_custom_call", output_to_operand_aliasing={{}: (4, {})} | custom-call | tf_op jit(solution)/shard_map/total/pallas_call | solution.py:529
  47.6 10.2 %all_to_all.11.in_ref = bf16[8,96,128]{2,1,0:T(8,128)(2,1)} all-to-all(bf16[8,96,128]{2,1,0:T(8,128)(2,1)} %total.1), channel_id=1, replica_groups=mesh['ctx'=8,'head'=4] {'ctx'}, dimensions={0} | all-to-all | bytes 393216 | tf_op jit(solution)/shard_map/all_to_all | solution.py:538
  57.8 1.6 %unpack.1 = (bf16[32,2048]{1,0:T(8,128)(2,1)}, bf16[32,512]{1,0:T(8,128)(2,1)}, bf16[32,512]{1,0:T(8,128)(2,1)}) custom-call(bf16[8,96,128]{2,1,0:T(8,128)(2,1)} %all_to_all.11.in_ref), custom_call_target="tpu_custom_call" | custom-call | tf_op jit(solution)/shard_map/unpack/pallas_call | solution.py:541
  (11 shorter events, 0.0 us)
Async XLA Ops:
  0.6 1.4 %copy-start.6 = (f32[128,8]{0,1:T(8,128)S(1)}, f32[128,8]{0,1:T(8,128)}, u32[]{:S(2)}) copy-start(f32[128,8]{0,1:T(8,128)} %param.12) | copy-start | bytes 12292
  20.2 4.6 %collective-permute-start = (bf16[288,128]{1,0:T(8,128)(2,1)}, bf16[288,128]{1,0:T(8,128)(2,1)S(1)}, u32[]{:S(2)}, u32[]{:S(2)}) collective-permute-start(bf16[288,128]{1,0:T(8,128)(2,1)} %get-tuple-element.13), channel_id=1, source_target_pairs={{0,1},{1,0},{2,3},{3,2},{4,5},{5,4},{6,7},{7,6},{8,9},{9,8},{10,11... | collective-permute-start | bytes 221192 | tf_op jit(solution)/shard_map/ppermute | solution.py:502
  22.1 7.7 %collective-permute-start.1 = (bf16[288,128]{1,0:T(8,128)(2,1)}, bf16[288,128]{1,0:T(8,128)(2,1)S(1)}, u32[]{:S(2)}, u32[]{:S(2)}) collective-permute-start(bf16[288,128]{1,0:T(8,128)(2,1)} %get-tuple-element.14), channel_id=1, source_target_pairs={{0,2},{1,3},{2,0},{3,1},{4,6},{5,7},{6,4},{7,5},{8,10},{9,11},{10,... | collective-permute-start | bytes 221192 | tf_op jit(solution)/shard_map/ppermute | solution.py:502
  24.7 6.5 %collective-permute-start.2 = (bf16[288,128]{1,0:T(8,128)(2,1)}, bf16[288,128]{1,0:T(8,128)(2,1)S(1)}, u32[]{:S(2)}, u32[]{:S(2)}) collective-permute-start(bf16[288,128]{1,0:T(8,128)(2,1)} %get-tuple-element.15), channel_id=1, source_target_pairs={{0,3},{1,2},{2,1},{3,0},{4,7},{5,6},{6,5},{7,4},{8,11},{9,10},{10,... | collective-permute-start | bytes 221192 | tf_op jit(solution)/shard_map/ppermute | solution.py:502
  24.8 6.3 %copy-start = (bf16[288,128]{1,0:T(8,128)(2,1)}, bf16[288,128]{1,0:T(8,128)(2,1)S(1)}, u32[]{:S(2)}) copy-start(bf16[288,128]{1,0:T(8,128)(2,1)S(1)} %collective-permute-done.refs_0_) | copy-start | bytes 221188
  29.8 1.4 %copy-start.1 = (bf16[288,128]{1,0:T(8,128)(2,1)}, bf16[288,128]{1,0:T(8,128)(2,1)S(1)}, u32[]{:S(2)}) copy-start(bf16[288,128]{1,0:T(8,128)(2,1)S(1)} %collective-permute-done.1.refs_1_) | copy-start | bytes 221188
  31.1 0.6 %copy-start.2 = (bf16[288,128]{1,0:T(8,128)(2,1)}, bf16[288,128]{1,0:T(8,128)(2,1)S(1)}, u32[]{:S(2)}) copy-start(bf16[288,128]{1,0:T(8,128)(2,1)S(1)} %collective-permute-done.2.refs_2_) | copy-start | bytes 221188
  36.5 4.5 %collective-permute-start.3 = (bf16[256,128]{1,0:T(8,128)(2,1)}, bf16[256,128]{1,0:T(8,128)(2,1)S(1)}, u32[]{:S(2)}, u32[]{:S(2)}) collective-permute-start(bf16[256,128]{1,0:T(8,128)(2,1)} %get-tuple-element.17), channel_id=1, source_target_pairs={{0,1},{1,0},{2,3},{3,2},{4,5},{5,4},{6,7},{7,6},{8,9},{9,8},{10,11... | collective-permute-start | bytes 196616 | tf_op jit(solution)/shard_map/ppermute | solution.py:502
  37.3 6.4 %collective-permute-start.4 = (bf16[256,128]{1,0:T(8,128)(2,1)}, bf16[256,128]{1,0:T(8,128)(2,1)S(1)}, u32[]{:S(2)}, u32[]{:S(2)}) collective-permute-start(bf16[256,128]{1,0:T(8,128)(2,1)} %get-tuple-element.18), channel_id=1, source_target_pairs={{0,2},{1,3},{2,0},{3,1},{4,6},{5,7},{6,4},{7,5},{8,10},{9,11},{10,... | collective-permute-start | bytes 196616 | tf_op jit(solution)/shard_map/ppermute | solution.py:502
  39.1 6.3 %collective-permute-start.5 = (bf16[256,128]{1,0:T(8,128)(2,1)}, bf16[256,128]{1,0:T(8,128)(2,1)S(1)}, u32[]{:S(2)}, u32[]{:S(2)}) collective-permute-start(bf16[256,128]{1,0:T(8,128)(2,1)} %get-tuple-element.19), channel_id=1, source_target_pairs={{0,3},{1,2},{2,1},{3,0},{4,7},{5,6},{6,5},{7,4},{8,11},{9,10},{10,... | collective-permute-start | bytes 196616 | tf_op jit(solution)/shard_map/ppermute | solution.py:502
  41.0 4.3 %copy-start.3 = (bf16[256,128]{1,0:T(8,128)(2,1)}, bf16[256,128]{1,0:T(8,128)(2,1)S(1)}, u32[]{:S(2)}) copy-start(bf16[256,128]{1,0:T(8,128)(2,1)S(1)} %collective-permute-done.3.refs_0_) | copy-start | bytes 196612
  43.8 1.6 %copy-start.4 = (bf16[256,128]{1,0:T(8,128)(2,1)}, bf16[256,128]{1,0:T(8,128)(2,1)S(1)}, u32[]{:S(2)}) copy-start(bf16[256,128]{1,0:T(8,128)(2,1)S(1)} %collective-permute-done.4.refs_1_) | copy-start | bytes 196612
  45.3 0.6 %copy-start.5 = (bf16[256,128]{1,0:T(8,128)(2,1)}, bf16[256,128]{1,0:T(8,128)(2,1)S(1)}, u32[]{:S(2)}) copy-start(bf16[256,128]{1,0:T(8,128)(2,1)S(1)} %collective-permute-done.5.refs_2_) | copy-start | bytes 196612

commit v2 on v1

--- a/solution.py
+++ b/solution.py
@@ -216,9 +216,20 @@
     return lax.broadcasted_iota(jnp.int32, shape, len(shape) - 1)
 
 
-def pack_kernel(pos_ref, q_ref, g_ref, k_ref, v_ref, n_ref, d_ref, out_ref, wide_ref):
+def pack_kernel(*refs):
+    sources, out_ref, near, wide_ref, sems = refs[:7], refs[7], refs[8:15], refs[15], refs[16]
+    pos_ref, q_ref, g_ref, k_ref, v_ref, n_ref, d_ref = near
+    copies = [
+        pltpu.make_async_copy(source, target, sems.at[i])
+        for i, (source, target) in enumerate(zip(sources, near))
+    ]
+    for i in (1, 2, 3, 4, 5, 6, 0):
+        copies[i].start()
+    copies[1].wait()
+    copies[2].wait()
     rows = q_ref.shape[0]
-    planes = n_ref.shape[0] // rows
+    tall = pos_ref.shape[0]
+    planes = tall // rows
     block = lax.axis_index("ctx")
     kv_heads = out_ref.shape[0]
     group = q_ref.shape[1] // k_ref.shape[1]
@@ -235,6 +246,8 @@
         out_ref[c, e * rows : (e + 1) * rows, :] = even.astype(BF16)
         out_ref[c, (e + 1) * rows : (e + 2) * rows, :] = odd.astype(BF16)
     at = group * rows
+    copies[3].wait()
+    copies[4].wait()
     for m in range(k_ref.shape[1] // LANES):
         cols = slice(m * LANES, (m + 1) * LANES)
         k = k_ref[:, cols].astype(F32)
@@ -244,17 +257,19 @@
         out_ref[2 * m, at : at + rows, :] = even.astype(BF16)
         out_ref[2 * m + 1, at : at + rows, :] = odd.astype(BF16)
     at = at + rows
-    tall = n_ref.shape[0]
+    copies[5].wait()
+    copies[6].wait()
+    copies[0].wait()
     wide_ref[...] = jnp.zeros(wide_ref.shape, F32)
-    wide_ref[0, :, 0 : n_ref.shape[1]] = n_ref[...]
-    wide_ref[1, :, 0 : d_ref.shape[1]] = d_ref[...]
+    wide_ref[0, 0 : n_ref.shape[0], :] = n_ref[...]
+    wide_ref[1, 0 : d_ref.shape[0], :] = d_ref[...]
     tall_lane = lane_of((tall, LANES))
     row_half = tall // 2
     lead = (pos_ref[0] // row_half).astype(F32)
     for parity in range(2):
         spread = jnp.zeros((tall, LANES), F32)
         for t in range(2):
-            rest = wide_ref[t]
+            rest = wide_ref[t].T
             for s in range(PIECES):
                 piece = rest.astype(BF16).astype(F32)
                 rest = rest - piece
@@ -276,13 +291,13 @@
 
 
 def spread_kernel(in_ref, own_ref, *send_refs):
-    blocks, double, _ = in_ref.shape
-    rows = double // 2
+    blocks, packet, _ = in_ref.shape
+    rows = own_ref.shape[0]
     plane = lax.axis_index("head")
     width = LANES // blocks
     lane = lane_of((rows, LANES))
-    kv = in_ref[:, 0:rows, :].reshape(blocks * rows, LANES)
-    tiles = [in_ref[b, rows:double, :].astype(F32) for b in range(blocks)]
+    kv = in_ref[:, packet - 2 * rows : packet - rows, :].reshape(blocks * rows, LANES)
+    tiles = [in_ref[b, packet - rows : packet, :].astype(F32) for b in range(blocks)]
     for j in range(len(send_refs) + 1):
         wanted = plane ^ j
         tile = jnp.zeros((rows, LANES), F32)
@@ -297,12 +312,11 @@
             send_refs[j - 1][blocks * rows : (blocks + 1) * rows, :] = tile.astype(BF16)
 
 
-def make_attend(planes):
-    def attend_kernel(in_ref, own_ref, *refs):
+def make_attend_others(planes):
+    def attend_others_kernel(in_ref, own_ref, *refs):
         got = refs[: planes - 1]
-        out_ref, sum_ref = refs[planes - 1 : planes + 1]
-        send_refs = refs[planes + 1 : 2 * planes]
-        left_ref, right_ref, both_ref, prob_ref, score_ref = refs[2 * planes :]
+        send_refs = refs[planes - 1 : 2 * planes - 2]
+        right_ref, both_ref, scores_ref, query_ref, left_ref, prob_ref = refs[2 * planes - 2 :]
         blocks = in_ref.shape[0]
         rows = own_ref.shape[0]
         group = in_ref.shape[1] // rows - 2
@@ -360,58 +374,86 @@
                 down = slice(tokens + b * rows, tokens + (b + 1) * rows)
                 right_ref[e, down, LANES:] = delta.astype(BF16)
 
-        key_row = lax.broadcasted_iota(jnp.int32, (tokens, LANES), 0)
-        wide_lane = lane_of((tokens, LANES))
-        square_key = lax.broadcasted_iota(jnp.int32, (tokens, tokens), 0)
-        square_query = lane_of((tokens, tokens))
-        allowed = (square_key <= square_query) | (square_key // rows != square_query // rows)
-        query_sum = None
-        for j in range(planes):
-            if j == 0:
-                kv = in_ref[:, group * rows : (group + 1) * rows, :].reshape(tokens, LANES)
-            else:
-                kv = got[j - 1][0:tokens, :]
-            mark = first + (plane ^ j) * blocks + key_row // rows
-            ones = jnp.where((wide_lane < first) | (wide_lane == mark), -1.0, 0.0)
-            left_ref[:, 0:LANES] = kv
-            left_ref[:, LANES:] = ones.astype(BF16)
-            for e in range(group):
-                both = lax.dot_general(
-                    left_ref[...],
-                    right_ref[e],
-                    (((1,), (1,)), ((), ())),
-                    preferred_element_type=F32,
-                )
-                prob = jnp.exp(both[:, 0:tokens])
-                if j == 0:
-                    prob = jnp.where(allowed, prob, 0.0)
-                score = prob * both[:, tokens:]
-                across = slice(e * tokens, (e + 1) * tokens)
-                prob_ref[:, across] = prob.astype(BF16)
-                score_ref[:, across] = score.astype(BF16)
-            value_side = jnp.dot(prob_ref[...], both_ref[...], preferred_element_type=F32)
-            key_side = jnp.dot(score_ref[...], both_ref[...], preferred_element_type=F32)
-            kv_sum = jnp.where(low, key_side, value_side)
-            if j == 0:
-                sum_ref[...] = kv_sum
-            else:
-                send_refs[j - 1][...] = kv_sum.astype(BF16)
-            turned = kv.astype(F32).T[0:HEAD_WIDTH].astype(BF16)
-            part = jnp.dot(turned, score_ref[...], preferred_element_type=F32)
-            query_sum = part if query_sum is None else query_sum + part
-        scale = HEAD_WIDTH ** (-0.5)
-        for m in range(group // 2):
-            pair = jnp.concatenate(
-                [
-                    query_sum[:, 2 * m * tokens : (2 * m + 1) * tokens],
-                    query_sum[:, (2 * m + 1) * tokens : (2 * m + 2) * tokens],
-                ],
-                0,
+        for j in range(1, planes):
+            kv = got[j - 1][0:tokens, :]
+            scores_here = scores_ref.at[(j - 1) * tokens : j * tokens]
+            kv_sum = pair_sums(
+                kv, first + (plane ^ j) * blocks, first, rows, None,
+                left_ref, right_ref, both_ref, prob_ref, scores_here,
             )
-            done = (pair.T * scale).astype(BF16)
-            out_ref[:, m * rows : (m + 1) * rows, :] = done.reshape(blocks, rows, LANES)
-
-    return attend_kernel
+            send_refs[j - 1][...] = kv_sum.astype(BF16)
+            query_ref[j - 1] = kv
+
+    return attend_others_kernel
+
+
+def pair_sums(
+    kv, mark_from, first, rows, allowed, left_ref, right_ref, both_ref, prob_ref, score_ref
+):
+    tokens = kv.shape[0]
+    group = right_ref.shape[0]
+    key_row = lax.broadcasted_iota(jnp.int32, (tokens, LANES), 0)
+    wide_lane = lane_of((tokens, LANES))
+    low = wide_lane < HEAD_WIDTH
+    mark = mark_from + key_row // rows
+    ones = jnp.where((wide_lane < first) | (wide_lane == mark), -1.0, 0.0)
+    left_ref[:, 0:LANES] = kv
+    left_ref[:, LANES:] = ones.astype(BF16)
+    for e in range(group):
+        both = lax.dot_general(
+            left_ref[...],
+            right_ref[e],
+            (((1,), (1,)), ((), ())),
+            preferred_element_type=F32,
+        )
+        prob = jnp.exp(both[:, 0:tokens])
+        if allowed is not None:
+            prob = jnp.where(allowed, prob, 0.0)
+        score = prob * both[:, tokens:]
+        across = slice(e * tokens, (e + 1) * tokens)
+        prob_ref[:, across] = prob.astype(BF16)
+        score_ref[:, across] = score.astype(BF16)
+    value_side = jnp.dot(prob_ref[...], both_ref[...], preferred_element_type=F32)
+    key_side = jnp.dot(score_ref[...], both_ref[...], preferred_element_type=F32)
+    return jnp.where(low, key_side, value_side)
+
+
+def attend_own_kernel(
+    in_ref, right_ref, both_ref, scores_ref, keys_ref, out_ref, sum_ref, left_ref, prob_ref, score_ref
+):
+    others, tokens, _ = keys_ref.shape
+    blocks = in_ref.shape[0]
+    rows = tokens // blocks
+    group = right_ref.shape[0]
+    plane = lax.axis_index("head")
+    planes = others + 1
+    first = planes * (LANES // blocks)
+    square_key = lax.broadcasted_iota(jnp.int32, (tokens, tokens), 0)
+    square_query = lane_of((tokens, tokens))
+    allowed = (square_key <= square_query) | (square_key // rows != square_query // rows)
+    kv = in_ref[:, group * rows : (group + 1) * rows, :].reshape(tokens, LANES)
+    sum_ref[...] = pair_sums(
+        kv, first + plane * blocks, first, rows, allowed,
+        left_ref, right_ref, both_ref, prob_ref, score_ref,
+    )
+    turned = kv.astype(F32).T[0:HEAD_WIDTH].astype(BF16)
+    query_sum = jnp.dot(turned, score_ref[...], preferred_element_type=F32)
+    for j in range(others):
+        turned = keys_ref[j].astype(F32).T[0:HEAD_WIDTH].astype(BF16)
+        query_sum = query_sum + jnp.dot(
+            turned, scores_ref[j * tokens : (j + 1) * tokens, :], preferred_element_type=F32
+        )
+    scale = HEAD_WIDTH ** (-0.5)
+    for m in range(group // 2):
+        pair = jnp.concatenate(
+            [
+                query_sum[:, 2 * m * tokens : (2 * m + 1) * tokens],
+                query_sum[:, (2 * m + 1) * tokens : (2 * m + 2) * tokens],
+            ],
+            0,
+        )
+        done = (pair.T * scale).astype(BF16)
+        out_ref[:, m * rows : (m + 1) * rows, :] = done.reshape(blocks, rows, LANES)
 
 
 def total_kernel(sum_ref, *refs):
@@ -441,6 +483,14 @@
 
 def whole(shape):
     return pl.BlockSpec(shape, lambda: (0,) * len(shape))
+
+
+ROOMY = pltpu.CompilerParams(vmem_limit_bytes=24 << 20)
+KEPT = pl.BlockSpec(memory_space=pltpu.VMEM)
+
+
+def kept(*arrays):
+    return [pltpu.with_memory_space_constraint(a, pltpu.VMEM) for a in arrays]
 
 
 def by_heads(
@@ -459,90 +509,106 @@
     group = query_input.shape[1] // key_input.shape[1]
     packet = (group + 2) * rows
     tall = positions.shape[0]
-    packed = pl.pallas_call(
-        pack_kernel,
-        name="pack",
-        out_shape=jax.ShapeDtypeStruct((blocks, packet, LANES), BF16),
-        in_specs=[pl.BlockSpec(memory_space=pltpu.SMEM)]
-        + [
-            whole(a.shape)
-            for a in (
-                query_input,
-                output_gradient,
-                key_input,
-                value_input,
-                log_softmax_norm,
-                output_delta_rows,
-            )
-        ],
-        out_specs=whole((blocks, packet, LANES)),
-        scratch_shapes=[pltpu.VMEM((2, tall, LANES), F32)],
-    )(
+    norm_cols, delta_cols = log_softmax_norm.T, output_delta_rows.T
+    arguments = (
         positions,
         query_input,
         output_gradient,
         key_input,
         value_input,
-        log_softmax_norm,
-        output_delta_rows,
-    )
+        norm_cols,
+        delta_cols,
+    )
+    packed = pl.pallas_call(
+        pack_kernel,
+        name="pack",
+        compiler_params=ROOMY,
+        out_shape=pltpu.VMEM((blocks, packet, LANES), BF16),
+        in_specs=[pl.BlockSpec(memory_space=pl.ANY)] * len(arguments),
+        out_specs=KEPT,
+        scratch_shapes=[
+            pltpu.SMEM(a.shape, a.dtype) if a.ndim == 1 else pltpu.VMEM(a.shape, a.dtype)
+            for a in arguments
+        ]
+        + [pltpu.VMEM((2, LANES, tall), F32), pltpu.SemaphoreType.DMA((len(arguments),))],
+    )(*[pltpu.with_memory_space_constraint(a, pltpu.HBM) for a in arguments])
     packed = lax.all_to_all(packed, "ctx", split_axis=0, concat_axis=0, tiled=True)
-    sent = jax.ShapeDtypeStruct((tokens + rows, LANES), BF16)
+    (packed,) = kept(packed)
     own, *sends = pl.pallas_call(
         spread_kernel,
         name="spread",
-        grid=(1,),
-        out_shape=[jax.ShapeDtypeStruct((rows, LANES), BF16)] + [sent] * (planes - 1),
-        in_specs=[pl.BlockSpec((blocks, 2 * rows, LANES), lambda i: (0, group // 2, 0))],
-        out_specs=[pl.BlockSpec((rows, LANES), lambda i: (0, 0))]
-        + [pl.BlockSpec((tokens + rows, LANES), lambda i: (0, 0))] * (planes - 1),
+        compiler_params=ROOMY,
+        out_shape=[pltpu.VMEM((rows, LANES), BF16)]
+        + [pltpu.VMEM((tokens + rows, LANES), BF16)] * (planes - 1),
+        in_specs=[KEPT],
+        out_specs=[KEPT] * planes,
     )(packed)
 
     def swap(array, by):
         return lax.ppermute(array, "head", [(i, i ^ by) for i in range(planes)])
 
     got = [swap(sends[j - 1], j) for j in range(1, planes)]
-    part = jax.ShapeDtypeStruct((tokens, LANES), BF16)
+    wide = group * tokens
+    *parts, right, both, scores, keys = pl.pallas_call(
+        make_attend_others(planes),
+        name="attend_others",
+        compiler_params=ROOMY,
+        out_shape=[pltpu.VMEM((tokens, LANES), BF16)] * (planes - 1)
+        + [
+            pltpu.VMEM((group, 2 * tokens, 2 * LANES), BF16),
+            pltpu.VMEM((wide, LANES), BF16),
+            pltpu.VMEM(((planes - 1) * tokens, wide), BF16),
+            pltpu.VMEM((planes - 1, tokens, LANES), BF16),
+        ],
+        in_specs=[KEPT] * (planes + 1),
+        out_specs=[KEPT] * (planes + 3),
+        scratch_shapes=[
+            pltpu.VMEM((tokens, 2 * LANES), BF16),
+            pltpu.VMEM((tokens, wide), BF16),
+        ],
+    )(*kept(packed, own, *got))
+    parts = [swap(parts[j - 1], j) for j in range(1, planes)]
     packet = (group // 2 + 1) * rows
-    back, total, *parts = pl.pallas_call(
-        make_attend(planes),
-        name="attend",
+    back, total = pl.pallas_call(
+        attend_own_kernel,
+        name="attend_own",
+        compiler_params=ROOMY,
         out_shape=[
             jax.ShapeDtypeStruct((blocks, packet, LANES), BF16),
-            jax.ShapeDtypeStruct((tokens, LANES), F32),
-        ]
-        + [part] * (planes - 1),
-        in_specs=[whole(packed.shape), whole(own.shape)] + [whole(g.shape) for g in got],
-        out_specs=[whole((blocks, packet, LANES)), whole((tokens, LANES))]
-        + [whole((tokens, LANES))] * (planes - 1),
+            pltpu.VMEM((tokens, LANES), F32),
+        ],
+        in_specs=[KEPT] * 5,
+        out_specs=[whole((blocks, packet, LANES)), KEPT],
         scratch_shapes=[
             pltpu.VMEM((tokens, 2 * LANES), BF16),
-            pltpu.VMEM((group, 2 * tokens, 2 * LANES), BF16),
-            pltpu.VMEM((group * tokens, LANES), BF16),
-            pltpu.VMEM((tokens, group * tokens), BF16),
-            pltpu.VMEM((tokens, group * tokens), BF16),
+            pltpu.VMEM((tokens, wide), BF16),
+            pltpu.VMEM((tokens, wide), BF16),
         ],
-    )(packed, own, *got)
-    parts = [swap(parts[j - 1], j) for j in range(1, planes)]
+        cost_estimate=pl.CostEstimate(
+            flops=4 * wide * tokens * LANES * 4, transcendentals=wide * tokens, bytes_accessed=1 << 22
+        ),
+    )(*kept(packed, right, both, scores, keys))
     last = pl.BlockSpec((blocks, rows, LANES), lambda i: (0, group // 2, 0))
-    flat = pl.BlockSpec((tokens, LANES), lambda i: (0, 0))
     back = pl.pallas_call(
         total_kernel,
         name="total",
+        compiler_params=ROOMY,
         grid=(1,),
         out_shape=jax.ShapeDtypeStruct(back.shape, BF16),
-        in_specs=[flat] * planes + [pl.BlockSpec(memory_space=pl.ANY)],
+        in_specs=[KEPT] * planes + [pl.BlockSpec(memory_space=pl.ANY)],
         out_specs=last,
         input_output_aliases={planes: 0},
-    )(total, *parts, back)
+    )(*kept(total, *parts), back)
     back = lax.all_to_all(back, "ctx", split_axis=0, concat_axis=0, tiled=True)
+    (back,) = kept(back)
     shapes = [query_input.shape, key_input.shape, value_input.shape]
     return tuple(
         pl.pallas_call(
             unpack_kernel,
             name="unpack",
+        compiler_params=ROOMY,
             out_shape=[jax.ShapeDtypeStruct(s, BF16) for s in shapes],
-            in_specs=[whole(back.shape)],
+            in_specs=[KEPT],
             out_specs=[whole(s) for s in shapes],
         )(back)
     )

time: 59.9 us -> 46.4 us (0.77)
  Pallas kernels: 11.9 us -> 5.73 us
  local copies, waits for them, and re-layouts: 3.4 us -> 0 us
  blocking collectives: 23.8 us -> 21.9 us
  waiting for transfers between devices: 10.9 us -> 9.01 us
    pallas_call x5 -> x6, Pallas kernels: 11.9 us -> 5.73 us  [the longest x1 2.05 us: by_heads(): pl.pallas_call(make_attend_others(planes), name='attend_others', compiler...]
    unnamed x16 -> x0, local copies, waits for them, and re-layouts: 3.4 us -> none
    ppermute x6, waiting for transfers between devices: 10.9 us -> 9.01 us  [swap(): return lax.ppermute(array, 'head', [(i, i ^ by) for i in range(planes)])]
    all_to_all x1, blocking collectives: 10.2 us -> 8.6 us  [by_heads(): back = lax.all_to_all(back, 'ctx', split_axis=0, concat_axis=0, tiled=True)]
  transfers between devices with their start and end apart: 6 -> 6, of which waited for: 6 -> 4; matrix products, arithmetic and copies ran while one was open for 0% -> 0% of each run, Pallas kernels for 0% -> 3%
where the time goes in v2:
time: 46.4 us; the launch traced here: 46.2 us
  blocking collectives  21.9 us (47%)
  waiting for transfers between devices  9.01 us (19%)
  starting transfers between devices  8.9 us (19%)
  Pallas kernels  5.73 us (12%)
  between operations  0.67 us (1%)
    all_to_all x1, blocking collectives, by_heads(): lax.all_to_all(packed, 'ctx', split_axis=0, concat_axis=0, tiled=True)  13.3 us
    ppermute x6, waiting for transfers between devices, swap(): return lax.ppermute(array, 'head', [(i, i ^ by) for i in range(planes)])  9.01 us
    ppermute x6, starting transfers between devices, swap(): return lax.ppermute(array, 'head', [(i, i ^ by) for i in range(planes)])  8.9 us
    all_to_all x1, blocking collectives, by_heads(): back = lax.all_to_all(back, 'ctx', split_axis=0, concat_axis=0, tiled=True)  8.6 us
    pallas_call x1, Pallas kernels, by_heads(): pl.pallas_call(make_attend_others(planes), name='attend_others', compiler...  2.05 us
    pallas_call x1, Pallas kernels, by_heads(): pl.pallas_call(pack_kernel, name='pack', compiler_params=ROOMY, out_shape...  1.63 us
    pallas_call x1, Pallas kernels, by_heads(): pl.pallas_call(attend_own_kernel, name='attend_own', compiler_params=ROOM...  1.16 us
  transfers between devices with their start and end apart: 6, of which 4 were waited for; matrix products, arithmetic and copies ran while one was open for 0% of the time, Pallas kernels for 3%

profile of v2, /device:TPU:0, one launch (start us, length us, event | category | flops | bytes accessed | tf_op | source)
XLA Modules:
  0.0 46.2 jit_solution(1902894642394731934)
XLA Ops:
  0.6 1.6 %pack.1 = bf16[8,192,128]{2,1,0:T(8,128)(2,1)S(1)} custom-call(s32[128]{0:T(128)} %refs_0_.1, bf16[32,2048]{1,0:T(8,128)(2,1)} %refs_1_.1, bf16[32,2048]{1,0:T(8,128)(2,1)} %refs_2_.1, bf16[32,512]{1,0:T(8,128)(2,1)} %refs_3_.1, bf16[32,512]{1,0:T(8,128)(2,1)} %refs_4_.1, f32[8,128]{1,0:T(8,128)} %bitcast.2, f32[8,128]{1,0:T(8,128)} %bitcast.3), custom_call_target="tpu_custom_call" | custom-call | tf_op jit(solution)/shard_map/pack/pallas_call | solution.py:522
  2.3 13.3 %all_to_all.10.in_ref = bf16[8,192,128]{2,1,0:T(8,128)(2,1)S(1)} all-to-all(bf16[8,192,128]{2,1,0:T(8,128)(2,1)S(1)} %pack.1), channel_id=1, replica_groups=mesh['ctx'=8,'head'=4] {'ctx'}, dimensions={0} | all-to-all | bytes 786432 | tf_op jit(solution)/shard_map/all_to_all | solution.py:535
  15.6 0.1 spread.1
  15.7 1.6 %collective-permute-start = (bf16[288,128]{1,0:T(8,128)(2,1)S(1)}, bf16[288,128]{1,0:T(8,128)(2,1)S(1)}, u32[]{:S(2)}, u32[]{:S(2)}) collective-permute-start(bf16[288,128]{1,0:T(8,128)(2,1)S(1)} %get-tuple-element.17), channel_id=1, source_target_pairs={{0,1},{1,0},{2,3},{3,2},{4,5},{5,4},{6,7},{7,6},{8,9},{9,8},{10,11... | collective-permute-start | bytes 221192 | tf_op jit(solution)/shard_map/ppermute | solution.py:548
  17.4 2.6 %collective-permute-start.1 = (bf16[288,128]{1,0:T(8,128)(2,1)S(1)}, bf16[288,128]{1,0:T(8,128)(2,1)S(1)}, u32[]{:S(2)}, u32[]{:S(2)}) collective-permute-start(bf16[288,128]{1,0:T(8,128)(2,1)S(1)} %get-tuple-element.18), channel_id=1, source_target_pairs={{0,2},{1,3},{2,0},{3,1},{4,6},{5,7},{6,4},{7,5},{8,10},{9,11},{10,... | collective-permute-start | bytes 221192 | tf_op jit(solution)/shard_map/ppermute | solution.py:548
  19.9 0.2 collective-permute-start.2
  20.2 0.0 collective-permute-done.refs_0_
  20.2 4.7 %collective-permute-done.1.refs_1_ = bf16[288,128]{1,0:T(8,128)(2,1)S(1)} collective-permute-done((bf16[288,128]{1,0:T(8,128)(2,1)S(1)}, bf16[288,128]{1,0:T(8,128)(2,1)S(1)}, u32[]{:S(2)}, u32[]{:S(2)}) %collective-permute-start.1) | collective-permute-done | bytes 73760 | tf_op jit(solution)/shard_map/ppermute | solution.py:548
  24.9 1.3 %collective-permute-done.2.refs_2_ = bf16[288,128]{1,0:T(8,128)(2,1)S(1)} collective-permute-done((bf16[288,128]{1,0:T(8,128)(2,1)S(1)}, bf16[288,128]{1,0:T(8,128)(2,1)S(1)}, u32[]{:S(2)}, u32[]{:S(2)}) %collective-permute-start.2) | collective-permute-done | bytes 73760 | tf_op jit(solution)/shard_map/ppermute | solution.py:548
  26.2 2.1 %attend_others.1 = (bf16[256,128]{1,0:T(8,128)(2,1)S(1)}, bf16[256,128]{1,0:T(8,128)(2,1)S(1)}, bf16[256,128]{1,0:T(8,128)(2,1)S(1)}, bf16[4,512,256]{2,1,0:T(8,...) custom-call(bf16[8,192,128]{2,1,0:T(8,128)(2,1)S(1)} %all_to_all.10.in, ...), custom_call_target="tpu_custom_call" | custom-call | tf_op jit(solution)/shard_map/attend_others/pallas_call | solution.py:552
  28.3 0.9 %collective-permute-start.3 = (bf16[256,128]{1,0:T(8,128)(2,1)S(1)}, bf16[256,128]{1,0:T(8,128)(2,1)S(1)}, u32[]{:S(2)}, u32[]{:S(2)}) collective-permute-start(bf16[256,128]{1,0:T(8,128)(2,1)S(1)} %get-tuple-element.25), channel_id=1, source_target_pairs={{0,1},{1,0},{2,3},{3,2},{4,5},{5,4},{6,7},{7,6},{8,9},{9,8},{10,11... | collective-permute-start | bytes 196616 | tf_op jit(solution)/shard_map/ppermute | solution.py:548
  29.1 1.7 %collective-permute-start.4 = (bf16[256,128]{1,0:T(8,128)(2,1)S(1)}, bf16[256,128]{1,0:T(8,128)(2,1)S(1)}, u32[]{:S(2)}, u32[]{:S(2)}) collective-permute-start(bf16[256,128]{1,0:T(8,128)(2,1)S(1)} %get-tuple-element.26), channel_id=1, source_target_pairs={{0,2},{1,3},{2,0},{3,1},{4,6},{5,7},{6,4},{7,5},{8,10},{9,11},{10,... | collective-permute-start | bytes 196616 | tf_op jit(solution)/shard_map/ppermute | solution.py:548
  30.8 1.9 %collective-permute-start.5 = (bf16[256,128]{1,0:T(8,128)(2,1)S(1)}, bf16[256,128]{1,0:T(8,128)(2,1)S(1)}, u32[]{:S(2)}, u32[]{:S(2)}) collective-permute-start(bf16[256,128]{1,0:T(8,128)(2,1)S(1)} %get-tuple-element.27), channel_id=1, source_target_pairs={{0,3},{1,2},{2,1},{3,0},{4,7},{5,6},{6,5},{7,4},{8,11},{9,10},{10,... | collective-permute-start | bytes 196616 | tf_op jit(solution)/shard_map/ppermute | solution.py:548
  32.7 1.2 %attend_own.1 = (bf16[8,96,128]{2,1,0:T(8,128)(2,1)S(1)}, f32[256,128]{1,0:T(8,128)S(1)}) custom-call(bf16[8,192,128]{2,1,0:T(8,128)(2,1)S(1)} %all_to_all.10.in_ref, bf16[4,512,256]{2,1,0:T(8,128)(2,1)S(1)} %get-tuple-element.20.right_ref, bf16[1024,128]{1,0:T(8,128)(2,1)S(1)} %get-tuple-element.21.both_ref, ...), custom_call_target="tpu_custom_call" | custom-call | flops 536870912 | bytes 4194304 | tf_op jit(solution)/shard_map/attend_own/pallas_call | solution.py:572
  33.9 0.0 collective-permute-done.3.refs_0_
  33.9 1.5 %collective-permute-done.4.refs_1_ = bf16[256,128]{1,0:T(8,128)(2,1)S(1)} collective-permute-done((bf16[256,128]{1,0:T(8,128)(2,1)S(1)}, bf16[256,128]{1,0:T(8,128)(2,1)S(1)}, u32[]{:S(2)}, u32[]{:S(2)}) %collective-permute-start.4) | collective-permute-done | bytes 65568 | tf_op jit(solution)/shard_map/ppermute | solution.py:548
  35.4 1.5 %collective-permute-done.5.refs_2_ = bf16[256,128]{1,0:T(8,128)(2,1)S(1)} collective-permute-done((bf16[256,128]{1,0:T(8,128)(2,1)S(1)}, bf16[256,128]{1,0:T(8,128)(2,1)S(1)}, u32[]{:S(2)}, u32[]{:S(2)}) %collective-permute-start.5) | collective-permute-done | bytes 65568 | tf_op jit(solution)/shard_map/ppermute | solution.py:548
  36.9 8.6 %all_to_all.11.in_ref = bf16[8,96,128]{2,1,0:T(8,128)(2,1)S(1)} all-to-all(bf16[8,96,128]{2,1,0:T(8,128)(2,1)S(1)} %total.1), channel_id=1, replica_groups=mesh['ctx'=8,'head'=4] {'ctx'}, dimensions={0} | all-to-all | bytes 393216 | tf_op jit(solution)/shard_map/all_to_all | solution.py:602
  45.5 0.7 %unpack.1 = (bf16[32,2048]{1,0:T(8,128)(2,1)}, bf16[32,512]{1,0:T(8,128)(2,1)}, bf16[32,512]{1,0:T(8,128)(2,1)}) custom-call(bf16[8,96,128]{2,1,0:T(8,128)(2,1)S(1)} %all_to_all.11.in_ref), custom_call_target="tpu_custom_call" | custom-call | tf_op jit(solution)/shard_map/unpack/pallas_call | solution.py:606
  (1 shorter events, 0.0 us)
Async XLA Ops:
  15.7 4.5 %collective-permute-start = (bf16[288,128]{1,0:T(8,128)(2,1)S(1)}, bf16[288,128]{1,0:T(8,128)(2,1)S(1)}, u32[]{:S(2)}, u32[]{:S(2)}) collective-permute-start(bf16[288,128]{1,0:T(8,128)(2,1)S(1)} %get-tuple-element.17), channel_id=1, source_target_pairs={{0,1},{1,0},{2,3},{3,2},{4,5},{5,4},{6,7},{7,6},{8,9},{9,8},{10,11... | collective-permute-start | bytes 221192 | tf_op jit(solution)/shard_map/ppermute | solution.py:548
  17.4 7.5 %collective-permute-start.1 = (bf16[288,128]{1,0:T(8,128)(2,1)S(1)}, bf16[288,128]{1,0:T(8,128)(2,1)S(1)}, u32[]{:S(2)}, u32[]{:S(2)}) collective-permute-start(bf16[288,128]{1,0:T(8,128)(2,1)S(1)} %get-tuple-element.18), channel_id=1, source_target_pairs={{0,2},{1,3},{2,0},{3,1},{4,6},{5,7},{6,4},{7,5},{8,10},{9,11},{10,... | collective-permute-start | bytes 221192 | tf_op jit(solution)/shard_map/ppermute | solution.py:548
  19.9 6.3 %collective-permute-start.2 = (bf16[288,128]{1,0:T(8,128)(2,1)S(1)}, bf16[288,128]{1,0:T(8,128)(2,1)S(1)}, u32[]{:S(2)}, u32[]{:S(2)}) collective-permute-start(bf16[288,128]{1,0:T(8,128)(2,1)S(1)} %get-tuple-element.19), channel_id=1, source_target_pairs={{0,3},{1,2},{2,1},{3,0},{4,7},{5,6},{6,5},{7,4},{8,11},{9,10},{10,... | collective-permute-start | bytes 221192 | tf_op jit(solution)/shard_map/ppermute | solution.py:548
  28.3 5.6 %collective-permute-start.3 = (bf16[256,128]{1,0:T(8,128)(2,1)S(1)}, bf16[256,128]{1,0:T(8,128)(2,1)S(1)}, u32[]{:S(2)}, u32[]{:S(2)}) collective-permute-start(bf16[256,128]{1,0:T(8,128)(2,1)S(1)} %get-tuple-element.25), channel_id=1, source_target_pairs={{0,1},{1,0},{2,3},{3,2},{4,5},{5,4},{6,7},{7,6},{8,9},{9,8},{10,11... | collective-permute-start | bytes 196616 | tf_op jit(solution)/shard_map/ppermute | solution.py:548
  29.1 6.2 %collective-permute-start.4 = (bf16[256,128]{1,0:T(8,128)(2,1)S(1)}, bf16[256,128]{1,0:T(8,128)(2,1)S(1)}, u32[]{:S(2)}, u32[]{:S(2)}) collective-permute-start(bf16[256,128]{1,0:T(8,128)(2,1)S(1)} %get-tuple-element.26), channel_id=1, source_target_pairs={{0,2},{1,3},{2,0},{3,1},{4,6},{5,7},{6,4},{7,5},{8,10},{9,11},{10,... | collective-permute-start | bytes 196616 | tf_op jit(solution)/shard_map/ppermute | solution.py:548
  30.8 6.1 %collective-permute-start.5 = (bf16[256,128]{1,0:T(8,128)(2,1)S(1)}, bf16[256,128]{1,0:T(8,128)(2,1)S(1)}, u32[]{:S(2)}, u32[]{:S(2)}) collective-permute-start(bf16[256,128]{1,0:T(8,128)(2,1)S(1)} %get-tuple-element.27), channel_id=1, source_target_pairs={{0,3},{1,2},{2,1},{3,0},{4,7},{5,6},{6,5},{7,4},{8,11},{9,10},{10,... | collective-permute-start | bytes 196616 | tf_op jit(solution)/shard_map/ppermute | solution.py:548

commit v3 on v2

--- a/solution.py
+++ b/solution.py
@@ -8,6 +8,7 @@
 HEAD_WIDTH = 64
 LANES = 128
 PIECES = 2
+ORDER = (2, 3, 1)
 MASKED = 16384.0
 F32 = jnp.float32
 BF16 = jnp.bfloat16
@@ -216,8 +217,17 @@
     return lax.broadcasted_iota(jnp.int32, shape, len(shape) - 1)
 
 
+def slots_of(near_refs, far_refs):
+    packet = near_refs[0].shape[1]
+    views = [ref.at[0] for ref in near_refs]
+    for ref in far_refs:
+        views += [ref.at[0:packet], ref.at[packet : 2 * packet]]
+    return views
+
+
 def pack_kernel(*refs):
-    sources, out_ref, near, wide_ref, sems = refs[:7], refs[7], refs[8:15], refs[15], refs[16]
+    sources, (same_ref, cross_ref) = refs[:7], refs[7:9]
+    near, wide_ref, sems = refs[9:16], refs[16], refs[17]
     pos_ref, q_ref, g_ref, k_ref, v_ref, n_ref, d_ref = near
     copies = [
         pltpu.make_async_copy(source, target, sems.at[i])
@@ -225,37 +235,50 @@
     ]
     for i in (1, 2, 3, 4, 5, 6, 0):
         copies[i].start()
-    copies[1].wait()
-    copies[2].wait()
     rows = q_ref.shape[0]
     tall = pos_ref.shape[0]
     planes = tall // rows
+    chips = same_ref.shape[0]
+    kv_heads = 2 * chips
+    group = q_ref.shape[1] // k_ref.shape[1]
     block = lax.axis_index("ctx")
-    kv_heads = out_ref.shape[0]
-    group = q_ref.shape[1] // k_ref.shape[1]
+    odd_core = (block & 1) == 1
     lane = lane_of((rows, LANES))
     low = lane < HEAD_WIDTH
     scale = HEAD_WIDTH ** (-0.5)
-    for m in range(q_ref.shape[1] // LANES):
+
+    def put(chip, at, first, second):
+        to = (block >> 1) ^ chip
+        same_ref[to, at : at + rows, :] = jnp.where(odd_core, second, first).astype(BF16)
+        cross_ref[to, at : at + rows, :] = jnp.where(odd_core, first, second).astype(BF16)
+
+    def query_tiles(m):
         cols = slice(m * LANES, (m + 1) * LANES)
         q = q_ref[:, cols].astype(F32) * scale
         g = g_ref[:, cols].astype(F32)
-        c, e = (2 * m) // group, (2 * m) % group
         even = jnp.where(low, q, pltpu.roll(g, HEAD_WIDTH, 1))
         odd = jnp.where(low, pltpu.roll(q, HEAD_WIDTH, 1), g)
-        out_ref[c, e * rows : (e + 1) * rows, :] = even.astype(BF16)
-        out_ref[c, (e + 1) * rows : (e + 2) * rows, :] = odd.astype(BF16)
+        return even, odd
+
+    copies[1].wait()
+    copies[2].wait()
+    pairs = group // 2
+    for chip in range(chips):
+        for e in range(pairs):
+            here = query_tiles(2 * chip * pairs + e)
+            there = query_tiles((2 * chip + 1) * pairs + e)
+            for side in range(2):
+                put(chip, (2 * e + side) * rows, here[side], there[side])
     at = group * rows
     copies[3].wait()
     copies[4].wait()
-    for m in range(k_ref.shape[1] // LANES):
-        cols = slice(m * LANES, (m + 1) * LANES)
+    for chip in range(chips):
+        cols = slice(chip * LANES, (chip + 1) * LANES)
         k = k_ref[:, cols].astype(F32)
         v = v_ref[:, cols].astype(F32)
         even = jnp.where(low, k, pltpu.roll(v, HEAD_WIDTH, 1))
         odd = jnp.where(low, pltpu.roll(k, HEAD_WIDTH, 1), v)
-        out_ref[2 * m, at : at + rows, :] = even.astype(BF16)
-        out_ref[2 * m + 1, at : at + rows, :] = odd.astype(BF16)
+        put(chip, at, even, odd)
     at = at + rows
     copies[5].wait()
     copies[6].wait()
@@ -266,6 +289,9 @@
     tall_lane = lane_of((tall, LANES))
     row_half = tall // 2
     lead = (pos_ref[0] // row_half).astype(F32)
+    width = PIECES * 2 * group
+    first = planes * width
+    tiles = []
     for parity in range(2):
         spread = jnp.zeros((tall, LANES), F32)
         for t in range(2):
@@ -277,49 +303,64 @@
                 here = (tall_lane >= to) & (tall_lane < to + group)
                 moved = pltpu.roll(piece, (to - group * parity) % LANES, 1)
                 spread = jnp.where(here, moved, spread)
-        width = PIECES * 2 * group
         tile = jnp.zeros((rows, LANES), F32)
         for h in range(planes):
             part = spread[h * rows : (h + 1) * rows]
             moved = pltpu.roll(part, h * width, 1) if h else part
             tile = jnp.where((lane >= h * width) & (lane < (h + 1) * width), moved, tile)
-        first = planes * width
-        mine = (lane >= first) & (lane < first + planes * kv_heads) & (lane % kv_heads == block)
-        tile = jnp.where(mine, lead, tile).astype(BF16)
-        for c in range(parity, kv_heads, 2):
-            out_ref[c, at : at + rows, :] = tile
-
-
-def spread_kernel(in_ref, own_ref, *send_refs):
-    blocks, packet, _ = in_ref.shape
-    rows = own_ref.shape[0]
+        tiles.append(tile)
+    same = jnp.where(odd_core, tiles[1], tiles[0])
+    cross = jnp.where(odd_core, tiles[0], tiles[1])
+    in_lead = (lane >= first) & (lane < first + planes * kv_heads)
+    for chip in range(chips):
+        mine = in_lead & (lane % kv_heads == 2 * chip)
+        same_ref[chip, at : at + rows, :] = jnp.where(mine, lead, same).astype(BF16)
+        mine = in_lead & (lane % kv_heads == 2 * chip + 1)
+        cross_ref[chip, at : at + rows, :] = jnp.where(mine, lead, cross).astype(BF16)
+
+
+def join_kernel(same_ref, cross_ref, *out_refs):
+    packet = same_ref.shape[1]
+    for m, ref in enumerate(out_refs):
+        ref[0:packet, :] = same_ref[m + 1]
+        ref[packet : 2 * packet, :] = cross_ref[m + 1]
+
+
+def spread_kernel(*refs):
+    chips = refs[0].shape[0]
+    slots = slots_of(refs[:2], refs[2 : chips + 1])
+    send_refs = refs[chips + 1 :]
+    blocks = len(slots)
+    packet = slots[0].shape[0]
+    rows = send_refs[0].shape[0] // (blocks + 1)
     plane = lax.axis_index("head")
     width = LANES // blocks
     lane = lane_of((rows, LANES))
-    kv = in_ref[:, packet - 2 * rows : packet - rows, :].reshape(blocks * rows, LANES)
-    tiles = [in_ref[b, packet - rows : packet, :].astype(F32) for b in range(blocks)]
-    for j in range(len(send_refs) + 1):
+    tiles = [slot[packet - rows : packet, :].astype(F32) for slot in slots]
+    for j in range(len(send_refs)):
         wanted = plane ^ j
         tile = jnp.zeros((rows, LANES), F32)
         for b in range(blocks):
             shift = lax.rem(b * width - wanted * width + LANES, LANES)
             here = (lane >= b * width) & (lane < (b + 1) * width)
             tile = jnp.where(here, pltpu.roll(tiles[b], shift, 1), tile)
-        if j == 0:
-            own_ref[...] = tile.astype(BF16)
-        else:
-            send_refs[j - 1][0 : blocks * rows, :] = kv
-            send_refs[j - 1][blocks * rows : (blocks + 1) * rows, :] = tile.astype(BF16)
+        ref = send_refs[0 if j == 0 else 1 + ORDER.index(j)]
+        for b in range(blocks):
+            ref[b * rows : (b + 1) * rows, :] = slots[b][packet - 2 * rows : packet - rows, :]
+        ref[blocks * rows : (blocks + 1) * rows, :] = tile.astype(BF16)
 
 
 def make_attend_others(planes):
-    def attend_others_kernel(in_ref, own_ref, *refs):
-        got = refs[: planes - 1]
+    def attend_others_kernel(*refs):
+        chips = refs[0].shape[0]
+        slots = slots_of(refs[:2], refs[2 : chips + 1])
+        own_ref, refs = refs[chips + 1], refs[chips + 2 :]
+        got = [refs[ORDER.index(j)] for j in range(1, planes)]
         send_refs = refs[planes - 1 : 2 * planes - 2]
         right_ref, both_ref, scores_ref, query_ref, left_ref, prob_ref = refs[2 * planes - 2 :]
-        blocks = in_ref.shape[0]
-        rows = own_ref.shape[0]
-        group = in_ref.shape[1] // rows - 2
+        blocks = len(slots)
+        rows = own_ref.shape[0] // (blocks + 1)
+        group = slots[0].shape[0] // rows - 2
         tokens = blocks * rows
         width = LANES // blocks
         plane = lax.axis_index("head")
@@ -328,7 +369,7 @@
         lane_row = lane_of((1, LANES))
         first = planes * width
 
-        tile = own_ref[...].astype(F32)
+        tile = own_ref[tokens : tokens + rows, :].astype(F32)
         for j in range(1, planes):
             other = got[j - 1][tokens : tokens + rows, :].astype(F32)
             tile = jnp.where(holder == j, other, tile)
@@ -337,7 +378,7 @@
         lead = jnp.zeros((1, LANES), F32)
         for b in range(blocks):
             at = (group + 1) * rows
-            lead = lead + in_ref[b, at : at + rows, :].astype(F32)[0:1]
+            lead = lead + slots[b][at : at + rows, :].astype(F32)[0:1]
         key_plane = (lane_row - first) // blocks
         per_half = planes // 2
         count = 2 * blocks
@@ -350,13 +391,16 @@
         key_place = place(lead, key_plane.astype(F32))
         in_mask = (lane_row >= first) & (lane_row < first + planes * blocks)
 
-        low = lane_of((tokens, LANES)) < HEAD_WIDTH
-        nothing = jnp.zeros((tokens, LANES), BF16)
+        low = lane < HEAD_WIDTH
+        nothing = jnp.zeros((rows, LANES), BF16)
         for e in range(group):
-            pair = in_ref[:, e * rows : (e + 1) * rows, :].reshape(tokens, LANES)
-            both_ref[e * tokens : (e + 1) * tokens, :] = pair
-            right_ref[e, 0:tokens, 0:LANES] = jnp.where(low, pair, nothing)
-            right_ref[e, tokens : 2 * tokens, 0:LANES] = jnp.where(low, nothing, pair)
+            for b in range(blocks):
+                pair = slots[b][e * rows : (e + 1) * rows, :]
+                at = b * rows
+                both_ref[e * tokens + at : e * tokens + at + rows, :] = pair
+                right_ref[e, at : at + rows, 0:LANES] = jnp.where(low, pair, nothing)
+                at = tokens + at
+                right_ref[e, at : at + rows, 0:LANES] = jnp.where(low, nothing, pair)
         for b in range(blocks):
             lead_b = jnp.sum(
                 jnp.where(lane_row == first + b, lead, 0.0), axis=1, keepdims=True
@@ -381,7 +425,7 @@
                 kv, first + (plane ^ j) * blocks, first, rows, None,
                 left_ref, right_ref, both_ref, prob_ref, scores_here,
             )
-            send_refs[j - 1][...] = kv_sum.astype(BF16)
+            send_refs[ORDER.index(j)][...] = kv_sum.astype(BF16)
             query_ref[j - 1] = kv
 
     return attend_others_kernel
@@ -419,11 +463,12 @@
 
 
 def attend_own_kernel(
-    in_ref, right_ref, both_ref, scores_ref, keys_ref, out_ref, sum_ref, left_ref, prob_ref, score_ref
+    own_ref, right_ref, both_ref, scores_ref, keys_ref, out_ref, sum_ref, left_ref, prob_ref, score_ref
 ):
     others, tokens, _ = keys_ref.shape
-    blocks = in_ref.shape[0]
+    blocks = out_ref.shape[0]
     rows = tokens // blocks
+    block = lax.axis_index("ctx")
     group = right_ref.shape[0]
     plane = lax.axis_index("head")
     planes = others + 1
@@ -431,7 +476,7 @@
     square_key = lax.broadcasted_iota(jnp.int32, (tokens, tokens), 0)
     square_query = lane_of((tokens, tokens))
     allowed = (square_key <= square_query) | (square_key // rows != square_query // rows)
-    kv = in_ref[:, group * rows : (group + 1) * rows, :].reshape(tokens, LANES)
+    kv = own_ref[0:tokens, :]
     sum_ref[...] = pair_sums(
         kv, first + plane * blocks, first, rows, allowed,
         left_ref, right_ref, both_ref, prob_ref, score_ref,
@@ -453,7 +498,8 @@
             0,
         )
         done = (pair.T * scale).astype(BF16)
-        out_ref[:, m * rows : (m + 1) * rows, :] = done.reshape(blocks, rows, LANES)
+        for b in range(blocks):
+            out_ref[block ^ b, m * rows : (m + 1) * rows, :] = done[b * rows : (b + 1) * rows]
 
 
 def total_kernel(sum_ref, *refs):
@@ -461,7 +507,10 @@
     total = sum_ref[...]
     for ref in got:
         total = total + ref[...].astype(F32)
-    out_ref[...] = total.astype(BF16).reshape(out_ref.shape)
+    rows = out_ref.shape[1]
+    block = lax.axis_index("ctx")
+    for b in range(out_ref.shape[0]):
+        out_ref[block ^ b] = total[b * rows : (b + 1) * rows].astype(BF16)
 
 
 def unpack_kernel(in_ref, q_ref, k_ref, v_ref):
@@ -519,35 +568,50 @@
         norm_cols,
         delta_cols,
     )
-    packed = pl.pallas_call(
+    chips = blocks // 2
+    half = pltpu.VMEM((chips, packet, LANES), BF16)
+    same, cross = pl.pallas_call(
         pack_kernel,
         name="pack",
         compiler_params=ROOMY,
-        out_shape=pltpu.VMEM((blocks, packet, LANES), BF16),
+        out_shape=[half, half],
         in_specs=[pl.BlockSpec(memory_space=pl.ANY)] * len(arguments),
-        out_specs=KEPT,
+        out_specs=[KEPT, KEPT],
         scratch_shapes=[
             pltpu.SMEM(a.shape, a.dtype) if a.ndim == 1 else pltpu.VMEM(a.shape, a.dtype)
             for a in arguments
         ]
         + [pltpu.VMEM((2, LANES, tall), F32), pltpu.SemaphoreType.DMA((len(arguments),))],
     )(*[pltpu.with_memory_space_constraint(a, pltpu.HBM) for a in arguments])
-    packed = lax.all_to_all(packed, "ctx", split_axis=0, concat_axis=0, tiled=True)
-    (packed,) = kept(packed)
+
+    def trade(array, by):
+        return lax.ppermute(array, "ctx", [(i, i ^ by) for i in range(blocks)])
+
+    cross = trade(cross, 1)
+    joined = pl.pallas_call(
+        join_kernel,
+        name="join",
+        compiler_params=ROOMY,
+        out_shape=[pltpu.VMEM((2 * packet, LANES), BF16)] * (chips - 1),
+        in_specs=[KEPT] * 2,
+        out_specs=[KEPT] * (chips - 1),
+    )(*kept(same, cross))
+    joined = [trade(joined[m], 2 * (m + 1)) for m in range(chips - 1)]
+    packets = kept(same, cross, *joined)
     own, *sends = pl.pallas_call(
         spread_kernel,
         name="spread",
         compiler_params=ROOMY,
-        out_shape=[pltpu.VMEM((rows, LANES), BF16)]
-        + [pltpu.VMEM((tokens + rows, LANES), BF16)] * (planes - 1),
-        in_specs=[KEPT],
+        out_shape=[pltpu.VMEM((tokens + rows, LANES), BF16)] * planes,
+        in_specs=[KEPT] * (chips + 1),
         out_specs=[KEPT] * planes,
-    )(packed)
+    )(*packets)
 
     def swap(array, by):
         return lax.ppermute(array, "head", [(i, i ^ by) for i in range(planes)])
 
-    got = [swap(sends[j - 1], j) for j in range(1, planes)]
+    moved = {j: swap(sends[ORDER.index(j)], j) for j in ORDER}
+    got = [moved[j] for j in ORDER]
     wide = group * tokens
     *parts, right, both, scores, keys = pl.pallas_call(
         make_attend_others(planes),
@@ -560,14 +624,15 @@
             pltpu.VMEM(((planes - 1) * tokens, wide), BF16),
             pltpu.VMEM((planes - 1, tokens, LANES), BF16),
         ],
-        in_specs=[KEPT] * (planes + 1),
+        in_specs=[KEPT] * (chips + 1 + planes),
         out_specs=[KEPT] * (planes + 3),
         scratch_shapes=[
             pltpu.VMEM((tokens, 2 * LANES), BF16),
             pltpu.VMEM((tokens, wide), BF16),
         ],
-    )(*kept(packed, own, *got))
-    parts = [swap(parts[j - 1], j) for j in range(1, planes)]
+    )(*packets, *kept(own, *got))
+    moved = {j: swap(parts[ORDER.index(j)], j) for j in ORDER}
+    parts = [moved[j] for j in ORDER]
     packet = (group // 2 + 1) * rows
     back, total = pl.pallas_call(
         attend_own_kernel,
@@ -587,7 +652,7 @@
         cost_estimate=pl.CostEstimate(
             flops=4 * wide * tokens * LANES * 4, transcendentals=wide * tokens, bytes_accessed=1 << 22
         ),
-    )(*kept(packed, right, both, scores, keys))
+    )(*kept(own, right, both, scores, keys))
     last = pl.BlockSpec((blocks, rows, LANES), lambda i: (0, group // 2, 0))
     back = pl.pallas_call(
         total_kernel,

time: 46.4 us -> 43.2 us (0.931)
  blocking collectives: 21.9 us -> 9.02 us
  waiting for transfers between devices: 9.01 us -> 14.8 us
  starting transfers between devices: 8.9 us -> 12.8 us
    all_to_all x1 -> x0, blocking collectives: 13.3 us -> none  [by_heads(): lax.all_to_all(packed, 'ctx', split_axis=0, concat_axis=0, tiled=True)]
    ppermute x0 -> x4, waiting for transfers between devices: none -> 6.56 us  [trade(): return lax.ppermute(array, 'ctx', [(i, i ^ by) for i in range(blocks)])]
    ppermute x0 -> x4, starting transfers between devices: none -> 5.01 us  [trade(): return lax.ppermute(array, 'ctx', [(i, i ^ by) for i in range(blocks)])]
    ppermute x6, starting transfers between devices: 8.9 us -> 7.79 us  [swap(): return lax.ppermute(array, 'head', [(i, i ^ by) for i in range(planes)])]
    ppermute x6, waiting for transfers between devices: 9.01 us -> 8.24 us  [swap(): return lax.ppermute(array, 'head', [(i, i ^ by) for i in range(planes)])]
  transfers between devices with their start and end apart: 6 -> 10, of which waited for: 4 -> 10; matrix products, arithmetic and copies ran while one was open for 0% -> 0% of each run, Pallas kernels for 3% -> 3%
where the time goes in v3:
time: 43.2 us; the launch traced here: 43 us
  waiting for transfers between devices  14.8 us (34%)
  starting transfers between devices  12.8 us (30%)
  blocking collectives  9.02 us (21%)
  Pallas kernels  5.73 us (13%)
  between operations  0.68 us (2%)
    all_to_all x1, blocking collectives, by_heads(): back = lax.all_to_all(back, 'ctx', split_axis=0, concat_axis=0, tiled=True)  9.02 us
    ppermute x6, waiting for transfers between devices, swap(): return lax.ppermute(array, 'head', [(i, i ^ by) for i in range(planes)])  8.24 us
    ppermute x6, starting transfers between devices, swap(): return lax.ppermute(array, 'head', [(i, i ^ by) for i in range(planes)])  7.79 us
    ppermute x4, waiting for transfers between devices, trade(): return lax.ppermute(array, 'ctx', [(i, i ^ by) for i in range(blocks)])  6.56 us
    ppermute x4, starting transfers between devices, trade(): return lax.ppermute(array, 'ctx', [(i, i ^ by) for i in range(blocks)])  5.01 us
    pallas_call x1, Pallas kernels, by_heads(): pl.pallas_call(make_attend_others(planes), name='attend_others', compiler...  2.07 us
    pallas_call x1, Pallas kernels, by_heads(): pl.pallas_call(pack_kernel, name='pack', compiler_params=ROOMY, out_shape...  1.56 us
    pallas_call x1, Pallas kernels, by_heads(): pl.pallas_call(attend_own_kernel, name='attend_own', compiler_params=ROOM...  1.17 us
  transfers between devices with their start and end apart: 10, of which 10 were waited for; matrix products, arithmetic and copies ran while one was open for 0% of the time, Pallas kernels for 3%

profile of v3, /device:TPU:0, one launch (start us, length us, event | category | flops | bytes accessed | tf_op | source)
XLA Modules:
  0.0 43.0 jit_solution(12770293250348994167)
XLA Ops:
  0.6 1.6 %pack.1 = (bf16[4,192,128]{2,1,0:T(8,128)(2,1)S(1)}, bf16[4,192,128]{2,1,0:T(8,128)(2,1)S(1)}) custom-call(s32[128]{0:T(128)} %refs_0_.1, bf16[32,2048]{1,0:T(8,128)(2,1)} %refs_1_.1, bf16[32,2048]{1,0:T(8,128)(2,1)} %refs_2_.1, bf16[32,512]{1,0:T(8,128)(2,1)} %refs_3_.1, bf16[32,512]{1,0:T(8,128)(2,1)} %refs_4_.1, f32[8,128]{1,0:T(8,128)} %bitcast.2, ...), custom_call_target="tpu_custom_call" | custom-call | tf_op jit(solution)/shard_map/pack/pallas_call | solution.py:573
  2.2 0.6 %collective-permute-start = (bf16[4,192,128]{2,1,0:T(8,128)(2,1)S(1)}, bf16[4,192,128]{2,1,0:T(8,128)(2,1)S(1)}, u32[]{:S(2)}, u32[]{:S(2)}) collective-permute-start(bf16[4,192,128]{2,1,0:T(8,128)(2,1)S(1)} %get-tuple-element.22), channel_id=1, source_target_pairs={{0,4},{4,0},{8,12},{12,8},{16,20},{20,16},{24,28},{28,24},{1,5},{5... | collective-permute-start | bytes 589832 | tf_op jit(solution)/shard_map/ppermute | solution.py:588
  2.8 1.1 %collective-permute-done.cross_ref.refs_1_ = bf16[4,192,128]{2,1,0:T(8,128)(2,1)S(1)} collective-permute-done((bf16[4,192,128]{2,1,0:T(8,128)(2,1)S(1)}, bf16[4,192,128]{2,1,0:T(8,128)(2,1)S(1)}, u32[]{:S(2)}, u32[]{:S(2)}) %collective-permute-start) | collective-permute-done | bytes 196640 | tf_op jit(solution)/shard_map/ppermute | solution.py:588
  3.9 2.9 %collective-permute-start.1 = (bf16[384,128]{1,0:T(8,128)(2,1)S(1)}, bf16[384,128]{1,0:T(8,128)(2,1)S(1)}, u32[]{:S(2)}, u32[]{:S(2)}) collective-permute-start(bf16[384,128]{1,0:T(8,128)(2,1)S(1)} %get-tuple-element.23), channel_id=1, source_target_pairs={{0,8},{4,12},{8,0},{12,4},{16,24},{20,28},{24,16},{28,20},{1,9},{5... | collective-permute-start | bytes 294920 | tf_op jit(solution)/shard_map/ppermute | solution.py:588
  6.8 1.5 %collective-permute-start.2 = (bf16[384,128]{1,0:T(8,128)(2,1)S(1)}, bf16[384,128]{1,0:T(8,128)(2,1)S(1)}, u32[]{:S(2)}, u32[]{:S(2)}) collective-permute-start(bf16[384,128]{1,0:T(8,128)(2,1)S(1)} %get-tuple-element.24), channel_id=1, source_target_pairs={{0,16},{4,20},{8,24},{12,28},{16,0},{20,4},{24,8},{28,12},{1,17},{... | collective-permute-start | bytes 294920 | tf_op jit(solution)/shard_map/ppermute | solution.py:588
  8.3 1.6 %collective-permute-done.1.refs_2_ = bf16[384,128]{1,0:T(8,128)(2,1)S(1)} collective-permute-done((bf16[384,128]{1,0:T(8,128)(2,1)S(1)}, bf16[384,128]{1,0:T(8,128)(2,1)S(1)}, u32[]{:S(2)}, u32[]{:S(2)}) %collective-permute-start.1) | collective-permute-done | bytes 98336 | tf_op jit(solution)/shard_map/ppermute | solution.py:588
  10.0 2.6 %collective-permute-done.2.refs_3_ = bf16[384,128]{1,0:T(8,128)(2,1)S(1)} collective-permute-done((bf16[384,128]{1,0:T(8,128)(2,1)S(1)}, bf16[384,128]{1,0:T(8,128)(2,1)S(1)}, u32[]{:S(2)}, u32[]{:S(2)}) %collective-permute-start.2) | collective-permute-done | bytes 98336 | tf_op jit(solution)/shard_map/ppermute | solution.py:588
  12.5 1.3 %collective-permute-done.3.refs_4_ = bf16[384,128]{1,0:T(8,128)(2,1)S(1)} collective-permute-done((bf16[384,128]{1,0:T(8,128)(2,1)S(1)}, bf16[384,128]{1,0:T(8,128)(2,1)S(1)}, u32[]{:S(2)}, u32[]{:S(2)}) %collective-permute-start.3) | collective-permute-done | bytes 98336 | tf_op jit(solution)/shard_map/ppermute | solution.py:588
  13.8 0.2 spread.1
  14.0 2.7 %collective-permute-start.4 = (bf16[288,128]{1,0:T(8,128)(2,1)S(1)}, bf16[288,128]{1,0:T(8,128)(2,1)S(1)}, u32[]{:S(2)}, u32[]{:S(2)}) collective-permute-start(bf16[288,128]{1,0:T(8,128)(2,1)S(1)} %get-tuple-element.27), channel_id=1, source_target_pairs={{0,2},{1,3},{2,0},{3,1},{4,6},{5,7},{6,4},{7,5},{8,10},{9,11},{10,... | collective-permute-start | bytes 221192 | tf_op jit(solution)/shard_map/ppermute | solution.py:611
  16.6 1.3 %collective-permute-start.5 = (bf16[288,128]{1,0:T(8,128)(2,1)S(1)}, bf16[288,128]{1,0:T(8,128)(2,1)S(1)}, u32[]{:S(2)}, u32[]{:S(2)}) collective-permute-start(bf16[288,128]{1,0:T(8,128)(2,1)S(1)} %get-tuple-element.28), channel_id=1, source_target_pairs={{0,3},{1,2},{2,1},{3,0},{4,7},{5,6},{6,5},{7,4},{8,11},{9,10},{10,... | collective-permute-start | bytes 221192 | tf_op jit(solution)/shard_map/ppermute | solution.py:611
  18.0 0.2 collective-permute-start.6
  18.2 3.4 %collective-permute-done.4.refs_6_ = bf16[288,128]{1,0:T(8,128)(2,1)S(1)} collective-permute-done((bf16[288,128]{1,0:T(8,128)(2,1)S(1)}, bf16[288,128]{1,0:T(8,128)(2,1)S(1)}, u32[]{:S(2)}, u32[]{:S(2)}) %collective-permute-start.4) | collective-permute-done | bytes 73760 | tf_op jit(solution)/shard_map/ppermute | solution.py:611
  21.6 1.3 %collective-permute-done.5.refs_7_ = bf16[288,128]{1,0:T(8,128)(2,1)S(1)} collective-permute-done((bf16[288,128]{1,0:T(8,128)(2,1)S(1)}, bf16[288,128]{1,0:T(8,128)(2,1)S(1)}, u32[]{:S(2)}, u32[]{:S(2)}) %collective-permute-start.5) | collective-permute-done | bytes 73760 | tf_op jit(solution)/shard_map/ppermute | solution.py:611
  22.9 0.3 collective-permute-done.6.refs_8_
  23.1 2.1 %attend_others.1 = (bf16[256,128]{1,0:T(8,128)(2,1)S(1)}, bf16[256,128]{1,0:T(8,128)(2,1)S(1)}, bf16[256,128]{1,0:T(8,128)(2,1)S(1)}, bf16[4,512,256]{2,1,0:T(8,...) custom-call(bf16[4,192,128]{2,1,0:T(8,128)(2,1)S(1)} %get-tuple-elemen, ...), custom_call_target="tpu_custom_call" | custom-call | tf_op jit(solution)/shard_map/attend_others/pallas_call | solution.py:616
  25.2 1.8 %collective-permute-start.7 = (bf16[256,128]{1,0:T(8,128)(2,1)S(1)}, bf16[256,128]{1,0:T(8,128)(2,1)S(1)}, u32[]{:S(2)}, u32[]{:S(2)}) collective-permute-start(bf16[256,128]{1,0:T(8,128)(2,1)S(1)} %get-tuple-element.35), channel_id=1, source_target_pairs={{0,2},{1,3},{2,0},{3,1},{4,6},{5,7},{6,4},{7,5},{8,10},{9,11},{10,... | collective-permute-start | bytes 196616 | tf_op jit(solution)/shard_map/ppermute | solution.py:611
  27.0 1.2 %collective-permute-start.8 = (bf16[256,128]{1,0:T(8,128)(2,1)S(1)}, bf16[256,128]{1,0:T(8,128)(2,1)S(1)}, u32[]{:S(2)}, u32[]{:S(2)}) collective-permute-start(bf16[256,128]{1,0:T(8,128)(2,1)S(1)} %get-tuple-element.36), channel_id=1, source_target_pairs={{0,3},{1,2},{2,1},{3,0},{4,7},{5,6},{6,5},{7,4},{8,11},{9,10},{10,... | collective-permute-start | bytes 196616 | tf_op jit(solution)/shard_map/ppermute | solution.py:611
  28.2 0.6 %collective-permute-start.9 = (bf16[256,128]{1,0:T(8,128)(2,1)S(1)}, bf16[256,128]{1,0:T(8,128)(2,1)S(1)}, u32[]{:S(2)}, u32[]{:S(2)}) collective-permute-start(bf16[256,128]{1,0:T(8,128)(2,1)S(1)} %get-tuple-element.37), channel_id=1, source_target_pairs={{0,1},{1,0},{2,3},{3,2},{4,5},{5,4},{6,7},{7,6},{8,9},{9,8},{10,11... | collective-permute-start | bytes 196616 | tf_op jit(solution)/shard_map/ppermute | solution.py:611
  28.8 1.2 %attend_own.1 = (bf16[8,96,128]{2,1,0:T(8,128)(2,1)S(1)}, f32[256,128]{1,0:T(8,128)S(1)}) custom-call(bf16[288,128]{1,0:T(8,128)(2,1)S(1)} %get-tuple-element.26.refs_5_.own_ref, bf16[4,512,256]{2,1,0:T(8,128)(2,1)S(1)} %get-tuple-element.30.right_ref, bf16[1024,128]{1,0:T(8,128)(2,1)S(1)} %get-tuple-element.31.both_ref, ...), custom_call_target="tpu_custom_call" | custom-call | flops 536870912 | bytes 4194304 | tf_op jit(solution)/shard_map/attend_own/pallas_call | solution.py:637
  30.0 1.9 %collective-permute-done.7.refs_0_ = bf16[256,128]{1,0:T(8,128)(2,1)S(1)} collective-permute-done((bf16[256,128]{1,0:T(8,128)(2,1)S(1)}, bf16[256,128]{1,0:T(8,128)(2,1)S(1)}, u32[]{:S(2)}, u32[]{:S(2)}) %collective-permute-start.7) | collective-permute-done | bytes 65568 | tf_op jit(solution)/shard_map/ppermute | solution.py:611
  31.9 1.3 %collective-permute-done.8.refs_1_ = bf16[256,128]{1,0:T(8,128)(2,1)S(1)} collective-permute-done((bf16[256,128]{1,0:T(8,128)(2,1)S(1)}, bf16[256,128]{1,0:T(8,128)(2,1)S(1)}, u32[]{:S(2)}, u32[]{:S(2)}) %collective-permute-start.8) | collective-permute-done | bytes 65568 | tf_op jit(solution)/shard_map/ppermute | solution.py:611
  33.3 9.0 %all_to_all.5.in_ref = bf16[8,96,128]{2,1,0:T(8,128)(2,1)S(1)} all-to-all(bf16[8,96,128]{2,1,0:T(8,128)(2,1)S(1)} %total.1), channel_id=1, replica_groups=mesh['ctx'=8,'head'=4] {'ctx'}, dimensions={0} | all-to-all | bytes 393216 | tf_op jit(solution)/shard_map/all_to_all | solution.py:667
  42.3 0.7 %unpack.1 = (bf16[32,2048]{1,0:T(8,128)(2,1)}, bf16[32,512]{1,0:T(8,128)(2,1)}, bf16[32,512]{1,0:T(8,128)(2,1)}) custom-call(bf16[8,96,128]{2,1,0:T(8,128)(2,1)S(1)} %all_to_all.5.in_ref), custom_call_target="tpu_custom_call" | custom-call | tf_op jit(solution)/shard_map/unpack/pallas_call | solution.py:671
  (4 shorter events, 0.1 us)
Async XLA Ops:
  2.2 1.6 %collective-permute-start = (bf16[4,192,128]{2,1,0:T(8,128)(2,1)S(1)}, bf16[4,192,128]{2,1,0:T(8,128)(2,1)S(1)}, u32[]{:S(2)}, u32[]{:S(2)}) collective-permute-start(bf16[4,192,128]{2,1,0:T(8,128)(2,1)S(1)} %get-tuple-element.22), channel_id=1, source_target_pairs={{0,4},{4,0},{8,12},{12,8},{16,20},{20,16},{24,28},{28,24},{1,5},{5... | collective-permute-start | bytes 589832 | tf_op jit(solution)/shard_map/ppermute | solution.py:588
  3.9 6.1 %collective-permute-start.1 = (bf16[384,128]{1,0:T(8,128)(2,1)S(1)}, bf16[384,128]{1,0:T(8,128)(2,1)S(1)}, u32[]{:S(2)}, u32[]{:S(2)}) collective-permute-start(bf16[384,128]{1,0:T(8,128)(2,1)S(1)} %get-tuple-element.23), channel_id=1, source_target_pairs={{0,8},{4,12},{8,0},{12,4},{16,24},{20,28},{24,16},{28,20},{1,9},{5... | collective-permute-start | bytes 294920 | tf_op jit(solution)/shard_map/ppermute | solution.py:588
  6.8 5.8 %collective-permute-start.2 = (bf16[384,128]{1,0:T(8,128)(2,1)S(1)}, bf16[384,128]{1,0:T(8,128)(2,1)S(1)}, u32[]{:S(2)}, u32[]{:S(2)}) collective-permute-start(bf16[384,128]{1,0:T(8,128)(2,1)S(1)} %get-tuple-element.24), channel_id=1, source_target_pairs={{0,16},{4,20},{8,24},{12,28},{16,0},{20,4},{24,8},{28,12},{1,17},{... | collective-permute-start | bytes 294920 | tf_op jit(solution)/shard_map/ppermute | solution.py:588
  8.3 5.5 %collective-permute-start.3 = (bf16[384,128]{1,0:T(8,128)(2,1)S(1)}, bf16[384,128]{1,0:T(8,128)(2,1)S(1)}, u32[]{:S(2)}, u32[]{:S(2)}) collective-permute-start(bf16[384,128]{1,0:T(8,128)(2,1)S(1)} %get-tuple-element.25), channel_id=1, source_target_pairs={{0,24},{4,28},{8,16},{12,20},{16,8},{20,12},{24,0},{28,4},{1,25},{... | collective-permute-start | bytes 294920 | tf_op jit(solution)/shard_map/ppermute | solution.py:588
  14.0 7.6 %collective-permute-start.4 = (bf16[288,128]{1,0:T(8,128)(2,1)S(1)}, bf16[288,128]{1,0:T(8,128)(2,1)S(1)}, u32[]{:S(2)}, u32[]{:S(2)}) collective-permute-start(bf16[288,128]{1,0:T(8,128)(2,1)S(1)} %get-tuple-element.27), channel_id=1, source_target_pairs={{0,2},{1,3},{2,0},{3,1},{4,6},{5,7},{6,4},{7,5},{8,10},{9,11},{10,... | collective-permute-start | bytes 221192 | tf_op jit(solution)/shard_map/ppermute | solution.py:611
  16.6 6.3 %collective-permute-start.5 = (bf16[288,128]{1,0:T(8,128)(2,1)S(1)}, bf16[288,128]{1,0:T(8,128)(2,1)S(1)}, u32[]{:S(2)}, u32[]{:S(2)}) collective-permute-start(bf16[288,128]{1,0:T(8,128)(2,1)S(1)} %get-tuple-element.28), channel_id=1, source_target_pairs={{0,3},{1,2},{2,1},{3,0},{4,7},{5,6},{6,5},{7,4},{8,11},{9,10},{10,... | collective-permute-start | bytes 221192 | tf_op jit(solution)/shard_map/ppermute | solution.py:611
  18.0 5.2 %collective-permute-start.6 = (bf16[288,128]{1,0:T(8,128)(2,1)S(1)}, bf16[288,128]{1,0:T(8,128)(2,1)S(1)}, u32[]{:S(2)}, u32[]{:S(2)}) collective-permute-start(bf16[288,128]{1,0:T(8,128)(2,1)S(1)} %get-tuple-element.29), channel_id=1, source_target_pairs={{0,1},{1,0},{2,3},{3,2},{4,5},{5,4},{6,7},{7,6},{8,9},{9,8},{10,11... | collective-permute-start | bytes 221192 | tf_op jit(solution)/shard_map/ppermute | solution.py:611
  25.2 6.6 %collective-permute-start.7 = (bf16[256,128]{1,0:T(8,128)(2,1)S(1)}, bf16[256,128]{1,0:T(8,128)(2,1)S(1)}, u32[]{:S(2)}, u32[]{:S(2)}) collective-permute-start(bf16[256,128]{1,0:T(8,128)(2,1)S(1)} %get-tuple-element.35), channel_id=1, source_target_pairs={{0,2},{1,3},{2,0},{3,1},{4,6},{5,7},{6,4},{7,5},{8,10},{9,11},{10,... | collective-permute-start | bytes 196616 | tf_op jit(solution)/shard_map/ppermute | solution.py:611
  27.0 6.2 %collective-permute-start.8 = (bf16[256,128]{1,0:T(8,128)(2,1)S(1)}, bf16[256,128]{1,0:T(8,128)(2,1)S(1)}, u32[]{:S(2)}, u32[]{:S(2)}) collective-permute-start(bf16[256,128]{1,0:T(8,128)(2,1)S(1)} %get-tuple-element.36), channel_id=1, source_target_pairs={{0,3},{1,2},{2,1},{3,0},{4,7},{5,6},{6,5},{7,4},{8,11},{9,10},{10,... | collective-permute-start | bytes 196616 | tf_op jit(solution)/shard_map/ppermute | solution.py:611
  28.2 5.0 %collective-permute-start.9 = (bf16[256,128]{1,0:T(8,128)(2,1)S(1)}, bf16[256,128]{1,0:T(8,128)(2,1)S(1)}, u32[]{:S(2)}, u32[]{:S(2)}) collective-permute-start(bf16[256,128]{1,0:T(8,128)(2,1)S(1)} %get-tuple-element.37), channel_id=1, source_target_pairs={{0,1},{1,0},{2,3},{3,2},{4,5},{5,4},{6,7},{7,6},{8,9},{9,8},{10,11... | collective-permute-start | bytes 196616 | tf_op jit(solution)/shard_map/ppermute | solution.py:611

commit v4 on v0

--- a/solution.py
+++ b/solution.py
@@ -1,9 +1,18 @@
 import jax
 import jax.numpy as jnp
 from jax import lax
+from jax.experimental import pallas as pl
+from jax.experimental.pallas import tpu as pltpu
 from jax.sharding import PartitionSpec as P
 
 HEAD_WIDTH = 64
+LANES = 128
+PIECES = 2
+NOTE_ROWS = 8
+CHIP_ORDER = (1, 2, 3)
+MASKED = 16384.0
+F32 = jnp.float32
+BF16 = jnp.bfloat16
 
 
 def for_sending(array):
@@ -205,9 +214,445 @@
     return (query_out, key_out, value_out)
 
 
+def lane_of(shape):
+    return lax.broadcasted_iota(jnp.int32, shape, len(shape) - 1)
+
+
+def pair_sums(kv, mark_from, first, rows, allowed, left_ref, right_ref, prob_ref, score_ref):
+    tokens = kv.shape[0]
+    group = right_ref.shape[0]
+    key_row = lax.broadcasted_iota(jnp.int32, (tokens, LANES), 0)
+    wide_lane = lane_of((tokens, LANES))
+    low = wide_lane < HEAD_WIDTH
+    mark = mark_from + key_row // rows
+    ones = jnp.where((wide_lane < first) | (wide_lane == mark), -1.0, 0.0)
+    left_ref[:, 0:LANES] = kv
+    left_ref[:, LANES:] = ones.astype(BF16)
+    for e in range(group):
+        both = lax.dot_general(
+            left_ref[...],
+            right_ref[e, 0 : 2 * tokens],
+            (((1,), (1,)), ((), ())),
+            preferred_element_type=F32,
+        )
+        prob = jnp.exp(both[:, 0:tokens])
+        if allowed is not None:
+            prob = jnp.where(allowed, prob, 0.0)
+        score = prob * both[:, tokens:]
+        across = slice(e * tokens, (e + 1) * tokens)
+        prob_ref[:, across] = prob.astype(BF16)
+        score_ref[:, across] = score.astype(BF16)
+    pairs = jnp.concatenate(
+        [right_ref[e, 2 * tokens : 3 * tokens, 0:LANES] for e in range(group)], 0
+    )
+    value_side = jnp.dot(prob_ref[...], pairs, preferred_element_type=F32)
+    key_side = jnp.dot(score_ref[...], pairs, preferred_element_type=F32)
+    return jnp.where(low, key_side, value_side)
+
+
+def pack_kernel(*refs):
+    sources, (out_ref, same_ref, cross_ref) = refs[:7], refs[7:10]
+    near, key_ref, sems = refs[10:17], refs[17], refs[18]
+    pos_ref, q_ref, g_ref, k_ref, v_ref, n_ref, d_ref = near
+    copies = [
+        pltpu.make_async_copy(source, target, sems.at[i])
+        for i, (source, target) in enumerate(zip(sources, near))
+    ]
+    for i in (5, 6, 0, 3, 4, 1, 2):
+        copies[i].start()
+    rows = q_ref.shape[0]
+    tall = pos_ref.shape[0]
+    planes = tall // rows
+    chips = same_ref.shape[0]
+    group = q_ref.shape[1] // k_ref.shape[1]
+    block = lax.axis_index("ctx")
+    odd_core = (block & 1) == 1
+    lane = lane_of((rows, LANES))
+    low = lane < HEAD_WIDTH
+    scale = HEAD_WIDTH ** (-0.5)
+
+    copies[5].wait()
+    copies[6].wait()
+    copies[0].wait()
+    lead = (pos_ref[0] // (tall // 2)).astype(F32)
+    eight = NOTE_ROWS
+    sub = lax.broadcasted_iota(jnp.int32, (eight, LANES), 0)
+    quarter = lane_of((eight, LANES)) // rows
+    turns = []
+    for s in range(PIECES):
+        for t, ref in enumerate((n_ref, d_ref)):
+            rest = ref[...]
+            for _ in range(s):
+                rest = rest - rest.astype(BF16).astype(F32)
+            piece = rest.astype(BF16).astype(F32)
+            turns.append([pltpu.roll(piece, d * rows, 1) if d else piece for d in range(planes)])
+    for parity in range(2):
+        for h in range(planes):
+            note = jnp.where(sub == len(turns), lead, 0.0)
+            for r, turn in enumerate(turns):
+                for e in range(group):
+                    head = group * parity + e
+                    line = turn[(e - h) % planes][head : head + 1, :]
+                    note = jnp.where((sub == r) & (quarter == e), line, note)
+            note = note.astype(BF16)
+            for c in range(parity, 2 * chips, 2):
+                key_ref[c * planes + h, rows : rows + eight, :] = note
+
+    copies[3].wait()
+    copies[4].wait()
+    for chip in range(chips):
+        cols = slice(chip * LANES, (chip + 1) * LANES)
+        k = k_ref[:, cols].astype(F32)
+        v = v_ref[:, cols].astype(F32)
+        even = jnp.where(low, k, pltpu.roll(v, HEAD_WIDTH, 1)).astype(BF16)
+        odd = jnp.where(low, pltpu.roll(k, HEAD_WIDTH, 1), v).astype(BF16)
+        for h in range(planes):
+            key_ref[2 * chip * planes + h, 0:rows, :] = even
+            key_ref[(2 * chip + 1) * planes + h, 0:rows, :] = odd
+
+    out = pltpu.make_async_copy(key_ref, out_ref, sems.at[7])
+    out.start()
+
+    def query_tiles(m):
+        cols = slice(m * LANES, (m + 1) * LANES)
+        q = q_ref[:, cols].astype(F32) * scale
+        g = g_ref[:, cols].astype(F32)
+        even = jnp.where(low, q, pltpu.roll(g, HEAD_WIDTH, 1))
+        odd = jnp.where(low, pltpu.roll(q, HEAD_WIDTH, 1), g)
+        return even, odd
+
+    copies[1].wait()
+    copies[2].wait()
+    pairs = group // 2
+    for chip in range(chips):
+        to = (block >> 1) ^ chip
+        for e in range(pairs):
+            here = query_tiles(2 * chip * pairs + e)
+            there = query_tiles((2 * chip + 1) * pairs + e)
+            for side in range(2):
+                first, second = here[side], there[side]
+                at = (2 * e + side) * rows
+                same = jnp.where(odd_core, second, first).astype(BF16)
+                cross = jnp.where(odd_core, first, second).astype(BF16)
+                same_ref[to, at : at + rows, :] = same
+                cross_ref[to, at : at + rows, :] = cross
+    out.wait()
+
+
+def join_kernel(same_ref, cross_ref, *out_refs):
+    packet = same_ref.shape[1]
+    for m, ref in enumerate(out_refs):
+        ref[0:packet, :] = same_ref[CHIP_ORDER[m]]
+        ref[packet : 2 * packet, :] = cross_ref[CHIP_ORDER[m]]
+
+
+def prepare_kernel(same_ref, cross_ref, *refs):
+    far_refs, right_ref = refs[:-1], refs[-1]
+    packet = same_ref.shape[1]
+    group = right_ref.shape[0]
+    tokens = right_ref.shape[1] // 3
+    rows = packet // group
+    block = lax.axis_index("ctx")
+    slots = {0: same_ref.at[0], 1: cross_ref.at[0]}
+    for m, ref in enumerate(far_refs):
+        slots[2 * CHIP_ORDER[m]] = ref.at[0:packet]
+        slots[2 * CHIP_ORDER[m] + 1] = ref.at[packet : 2 * packet]
+    low = lane_of((rows, LANES)) < HEAD_WIDTH
+    nothing = jnp.zeros((rows, LANES), BF16)
+    for i, slot in slots.items():
+        at = pl.multiple_of((block ^ i) * rows, rows)
+        for e in range(group):
+            pair = slot[e * rows : (e + 1) * rows, :]
+            right_ref[e, pl.ds(2 * tokens + at, rows), 0:LANES] = pair
+            right_ref[e, pl.ds(at, rows), 0:LANES] = jnp.where(low, pair, nothing)
+            right_ref[e, pl.ds(tokens + at, rows), 0:LANES] = jnp.where(low, nothing, pair)
+
+
+def plane_keys(key_ref, which, blocks, rows):
+    planes = key_ref.shape[0] // blocks
+    return jnp.concatenate([key_ref[b * planes + which, 0:rows, :] for b in range(blocks)], 0)
+
+
+def attend_kernel(
+    ready_ref, key_ref, right_ref, out_ref, same_ref, cross_ref,
+    scores_ref, wide_ref, left_ref, prob_ref, part_ref, all_ref, sems,
+):
+    group = right_ref.shape[0]
+    tokens = right_ref.shape[1] // 3
+    blocks, planes, rows, _ = out_ref.shape
+    eight = NOTE_ROWS
+    count = 2 * PIECES
+    plane = lax.axis_index("head")
+    holder = lax.axis_index("ctx") // (blocks // planes)
+    first = LANES // 2
+    lane = lane_of((rows, LANES))
+    lane_row = lane_of((1, LANES))
+    quarter = lane_of((eight, LANES)) // rows
+
+    lead = jnp.zeros((1, LANES), F32)
+    notes = []
+    for b in range(blocks):
+        note = key_ref[b * planes + holder, rows : rows + eight, :].astype(F32)
+        lead = jnp.where(lane_row % blocks == b, note[count : count + 1], lead)
+        notes.append(note)
+    wide_ref[...] = jnp.zeros(wide_ref.shape, F32)
+    per_tile = LANES // rows
+    for e in range(group):
+        for b in range(blocks):
+            spot = b % per_tile
+            turn = ((spot - e) * rows) % LANES
+            moved = pltpu.roll(notes[b], turn, 1) if turn else notes[b]
+            down = slice((b // per_tile) * LANES + e * eight, (b // per_tile) * LANES + (e + 1) * eight)
+            wide_ref[down, :] = jnp.where(quarter == spot, moved, wide_ref[down, :])
+    columns = [
+        wide_ref[m * LANES : (m + 1) * LANES, :].T for m in range(tokens // LANES)
+    ]
+
+    key_plane = (lane_row - first) // blocks
+    per_half = planes // 2
+
+    def place(lead_of, which):
+        front = per_half * lead_of + which
+        back = per_half * (2 * blocks - 1 - lead_of) + (which - per_half)
+        return jnp.where(which < per_half, front, back)
+
+    key_place = place(lead, key_plane.astype(F32))
+    in_mask = (lane_row >= first) & (lane_row < first + planes * blocks)
+    for b in range(blocks):
+        lead_b = jnp.sum(jnp.where(lane_row == first + b, lead, 0.0), axis=1, keepdims=True)
+        query_place = place(lead_b, plane.astype(F32))
+        hidden = jnp.where(in_mask & (key_place > query_place), MASKED, 0.0)
+        at = (b % per_tile) * rows
+        column = columns[b // per_tile][at : at + rows]
+        for e in range(group):
+            mine = (lane >= e * eight) & (lane < e * eight + count)
+            norm = jnp.where(mine & (lane % 2 == 0), column, hidden)
+            delta = jnp.where(mine & (lane % 2 == 1), column, 0.0)
+            right_ref[e, b * rows : (b + 1) * rows, LANES:] = norm.astype(BF16)
+            down = slice(tokens + b * rows, tokens + (b + 1) * rows)
+            right_ref[e, down, LANES:] = delta.astype(BF16)
+
+    square_key = lax.broadcasted_iota(jnp.int32, (tokens, tokens), 0)
+    square_query = lane_of((tokens, tokens))
+    allowed = (square_key <= square_query) | (square_key // rows != square_query // rows)
+    copies = []
+    for j in range(planes):
+        which = plane ^ j
+        kv_sum = pair_sums(
+            plane_keys(key_ref, which, blocks, rows),
+            first + which * blocks, first, rows, None if j else allowed,
+            left_ref, right_ref, prob_ref,
+            scores_ref.at[j * tokens : (j + 1) * tokens],
+        )
+        part_ref[j] = kv_sum.astype(BF16).reshape(blocks, rows, LANES)
+        copies.append(pltpu.make_async_copy(part_ref.at[j], out_ref.at[:, which], sems.at[j]))
+        copies[j].start()
+    query_sum = jnp.zeros((HEAD_WIDTH, group * tokens), F32)
+    for j in range(planes):
+        keys = plane_keys(key_ref, plane ^ j, blocks, rows)
+        turned = keys.astype(F32).T[0:HEAD_WIDTH].astype(BF16)
+        here = scores_ref[j * tokens : (j + 1) * tokens, :]
+        query_sum = query_sum + jnp.dot(turned, here, preferred_element_type=F32)
+    scale = HEAD_WIDTH ** (-0.5)
+    for m in range(group // 2):
+        pair = jnp.concatenate(
+            [
+                query_sum[:, 2 * m * tokens : (2 * m + 1) * tokens],
+                query_sum[:, (2 * m + 1) * tokens : (2 * m + 2) * tokens],
+            ],
+            0,
+        )
+        done = (pair.T * scale).astype(BF16)
+        all_ref[:, m * rows : (m + 1) * rows, :] = done.reshape(blocks, rows, LANES)
+    block = lax.axis_index("ctx")
+    for m in range(blocks // 2):
+        same_ref[m] = all_ref[block ^ (2 * m)]
+        cross_ref[m] = all_ref[block ^ (2 * m + 1)]
+    for copy in copies:
+        copy.wait()
+
+
+def unpack_kernel(part_ref, same_ref, cross_ref, *refs):
+    chips = same_ref.shape[0]
+    far_refs, (q_ref, k_ref, v_ref, all_ref) = refs[: chips - 1], refs[chips - 1 :]
+    rows = q_ref.shape[0]
+    tall = same_ref.shape[1]
+    tiles = tall // rows
+    planes = part_ref.shape[0] // (2 * chips)
+    block = lax.axis_index("ctx")
+    all_ref[block] = same_ref[0]
+    all_ref[block ^ 1] = cross_ref[0]
+    for m, ref in enumerate(far_refs):
+        chip = 2 * CHIP_ORDER[m]
+        all_ref[block ^ chip] = ref[0:tall, :]
+        all_ref[block ^ (chip + 1)] = ref[tall : 2 * tall, :]
+    for c in range(2 * chips):
+        for m in range(tiles):
+            at = (c * tiles + m) * LANES
+            q_ref[:, at : at + LANES] = all_ref[c, m * rows : (m + 1) * rows, :]
+
+    def added(c):
+        total = part_ref[c * planes].astype(F32)
+        for h in range(1, planes):
+            total = total + part_ref[c * planes + h].astype(F32)
+        return total
+
+    low = lane_of((rows, LANES)) < HEAD_WIDTH
+    for m in range(chips):
+        even, odd = added(2 * m), added(2 * m + 1)
+        cols = slice(m * LANES, (m + 1) * LANES)
+        k_ref[:, cols] = jnp.where(low, even, pltpu.roll(odd, HEAD_WIDTH, 1)).astype(BF16)
+        v_ref[:, cols] = jnp.where(low, pltpu.roll(even, HEAD_WIDTH, 1), odd).astype(BF16)
+
+
+def whole(shape):
+    return pl.BlockSpec(shape, lambda: (0,) * len(shape))
+
+
+ROOMY = pltpu.CompilerParams(vmem_limit_bytes=24 << 20)
+KEPT = pl.BlockSpec(memory_space=pltpu.VMEM)
+
+
+def kept(*arrays):
+    return [pltpu.with_memory_space_constraint(a, pltpu.VMEM) for a in arrays]
+
+
+def by_heads(
+    query_input,
+    key_input,
+    value_input,
+    output_gradient,
+    log_softmax_norm,
+    output_delta_rows,
+    positions,
+):
+    blocks = lax.axis_size("ctx")
+    planes = lax.axis_size("head")
+    rows = query_input.shape[0]
+    tokens = blocks * rows
+    group = query_input.shape[1] // key_input.shape[1]
+    packet = group * rows
+    chips = blocks // 2
+    devices = blocks * planes
+    wide = group * tokens
+    arguments = (
+        positions,
+        query_input,
+        output_gradient,
+        key_input,
+        value_input,
+        log_softmax_norm.T,
+        output_delta_rows.T,
+    )
+    half = pltpu.VMEM((chips, packet, LANES), BF16)
+    keys, same, cross = pl.pallas_call(
+        pack_kernel,
+        name="pack",
+        compiler_params=ROOMY,
+        out_shape=[jax.ShapeDtypeStruct((devices, rows + NOTE_ROWS, LANES), BF16), half, half],
+        in_specs=[pl.BlockSpec(memory_space=pl.ANY)] * len(arguments),
+        out_specs=[pl.BlockSpec(memory_space=pl.ANY), KEPT, KEPT],
+        scratch_shapes=[
+            pltpu.SMEM(a.shape, a.dtype) if a.ndim == 1 else pltpu.VMEM(a.shape, a.dtype)
+            for a in arguments
+        ]
+        + [
+            pltpu.VMEM((devices, rows + NOTE_ROWS, LANES), BF16),
+            pltpu.SemaphoreType.DMA((len(arguments) + 1,)),
+        ],
+    )(*[pltpu.with_memory_space_constraint(a, pltpu.HBM) for a in arguments])
+
+    def trade(array, by):
+        return lax.ppermute(array, "ctx", [(i, i ^ by) for i in range(blocks)])
+
+    def to_all(array):
+        return lax.all_to_all(array, ("ctx", "head"), split_axis=0, concat_axis=0, tiled=True)
+
+    keys = to_all(keys)
+
+    def exchange(same, cross):
+        tall = same.shape[1]
+        cross = trade(cross, 1)
+        joined = pl.pallas_call(
+            join_kernel,
+            name="join",
+            compiler_params=ROOMY,
+            out_shape=[pltpu.VMEM((2 * tall, LANES), BF16)] * (chips - 1),
+            in_specs=[KEPT] * 2,
+            out_specs=[KEPT] * (chips - 1),
+        )(*kept(same, cross))
+        joined = [trade(array, 2 * CHIP_ORDER[m]) for m, array in enumerate(joined)]
+        return kept(same, cross, *joined)
+
+    received = exchange(same, cross)
+    right_shape = pltpu.VMEM((group, 3 * tokens, 2 * LANES), BF16)
+    right = pl.pallas_call(
+        prepare_kernel,
+        name="prepare",
+        compiler_params=ROOMY,
+        out_shape=right_shape,
+        in_specs=[KEPT] * (chips + 1),
+        out_specs=KEPT,
+    )(*received)
+    (keys,) = kept(keys)
+    tall = group // 2 * rows
+    half = pltpu.VMEM((chips, tall, LANES), BF16)
+    right, parts, same, cross = pl.pallas_call(
+        attend_kernel,
+        name="attend",
+        compiler_params=ROOMY,
+        out_shape=[
+            right_shape,
+            jax.ShapeDtypeStruct((blocks, planes, rows, LANES), BF16),
+            half,
+            half,
+        ],
+        in_specs=[KEPT] * 2,
+        out_specs=[KEPT, pl.BlockSpec(memory_space=pl.ANY), KEPT, KEPT],
+        input_output_aliases={0: 0},
+        scratch_shapes=[
+            pltpu.VMEM((planes * tokens, wide), BF16),
+            pltpu.VMEM((tokens // LANES * LANES, LANES), F32),
+            pltpu.VMEM((tokens, 2 * LANES), BF16),
+            pltpu.VMEM((tokens, wide), BF16),
+            pltpu.VMEM((planes, blocks, rows, LANES), BF16),
+            pltpu.VMEM((blocks, tall, LANES), BF16),
+            pltpu.SemaphoreType.DMA((planes,)),
+        ],
+    )(*kept(right), keys)
+    parts = to_all(parts.reshape(devices, rows, LANES))
+    received = exchange(same, cross)
+    shapes = [query_input.shape, key_input.shape, value_input.shape]
+    return tuple(
+        pl.pallas_call(
+            unpack_kernel,
+            name="unpack",
+            compiler_params=ROOMY,
+            out_shape=[jax.ShapeDtypeStruct(s, BF16) for s in shapes],
+            in_specs=[KEPT] * (chips + 2),
+            out_specs=[whole(s) for s in shapes],
+            scratch_shapes=[pltpu.VMEM((blocks, tall, LANES), BF16)],
+        )(*kept(parts), *received)
+    )
+
+
 def solution(mesh):
+    def on_each(*args):
+        query_input, key_input = args[0], args[1]
+        kv_heads = key_input.shape[1] // HEAD_WIDTH
+        group = query_input.shape[1] // key_input.shape[1]
+        blocks, planes = mesh.shape["ctx"], mesh.shape["head"]
+        by_head = (
+            blocks == kv_heads
+            and group == 4
+            and planes == 4
+            and kv_heads == 8
+            and query_input.shape[0] % 16 == 0
+        )
+        return (by_heads if by_head else on_device)(*args)
+
     return jax.shard_map(
-        on_device,
+        on_each,
         mesh=mesh,
         in_specs=(
             P(("ctx", "head"), None),

time: 197 us -> 39.1 us (0.20)
  waiting for transfers between devices: 69.1 us -> 13.4 us
  starting transfers between devices: 46.8 us -> 18.6 us
  local copies, waits for them, and re-layouts: 26.8 us -> 0 us
  loops' own time: 20.5 us -> 0 us
  matrix products: 20.1 us -> 0 us
  other arithmetic: 9.31 us -> 0 us
  Pallas kernels: 0 us -> 6.07 us
  between operations: 3.36 us -> 0.69 us
    all_to_all x7 -> x2, waiting for transfers between devices: 34.5 us -> 1.43 us  [to_all(): lax.all_to_all(array, ('ctx', 'head'), split_axis=0, concat_axis=0, tiled...]
    ppermute x37 -> x8, waiting for transfers between devices: 34.6 us -> 11.9 us  [trade(): return lax.ppermute(array, 'ctx', [(i, i ^ by) for i in range(blocks)])]
    another operation x33 -> x0, loops' own time: 20.5 us -> none  [the longest x1 18.6 us: on_device(): lax.fori_loop(0, lax.axis_size('ctx') - 1, cycle_turn, (grad_query, trave...]
    dot_general x85 -> x0, matrix products: 20.1 us -> none  [the longest x17 4.51 us: block_terms(): jnp.einsum('qhgd,khd->qhgk', query_per_head, key_per_head, preferred_elem...]
    all_to_all x7 -> x2, starting transfers between devices: 26.2 us -> 10.9 us  [to_all(): lax.all_to_all(array, ('ctx', 'head'), split_axis=0, concat_axis=0, tiled...]
    reshape x119 -> x0, local copies, waits for them, and re-layouts: 13.5 us -> none  [the longest x17 2.74 us: block_terms(): query_term.reshape(row_count, -1)]
    ppermute x37 -> x8, starting transfers between devices: 20.6 us -> 7.74 us  [trade(): return lax.ppermute(array, 'ctx', [(i, i ^ by) for i in range(blocks)])]
    pallas_call x0 -> x6, Pallas kernels: none -> 6.07 us  [the longest x1 3.4 us: by_heads(): pl.pallas_call(attend_kernel, name='attend', compiler_params=ROOMY, out_s...]
  transfers between devices with their start and end apart: 44 -> 10, of which waited for: 22 -> 10; matrix products, arithmetic and copies ran while one was open for 24% -> 0% of each run, Pallas kernels for 0% -> 0%
where the time goes in v4:
time: 39.1 us; the launch traced here: 38.7 us
  starting transfers between devices  18.6 us (48%)
  waiting for transfers between devices  13.4 us (34%)
  Pallas kernels  6.07 us (16%)
  between operations  0.69 us (2%)
    ppermute x8, waiting for transfers between devices, trade(): return lax.ppermute(array, 'ctx', [(i, i ^ by) for i in range(blocks)])  11.9 us
    all_to_all x2, starting transfers between devices, to_all(): lax.all_to_all(array, ('ctx', 'head'), split_axis=0, concat_axis=0, tiled...  10.9 us
    ppermute x8, starting transfers between devices, trade(): return lax.ppermute(array, 'ctx', [(i, i ^ by) for i in range(blocks)])  7.74 us
    pallas_call x1, Pallas kernels, by_heads(): pl.pallas_call(attend_kernel, name='attend', compiler_params=ROOMY, out_s...  3.4 us
    pallas_call x1, Pallas kernels, by_heads(): pl.pallas_call(pack_kernel, name='pack', compiler_params=ROOMY, out_shape...  1.8 us
    all_to_all x2, waiting for transfers between devices, to_all(): lax.all_to_all(array, ('ctx', 'head'), split_axis=0, concat_axis=0, tiled...  1.43 us
  transfers between devices with their start and end apart: 10, of which 10 were waited for; matrix products, arithmetic and copies ran while one was open for 0% of the time, Pallas kernels for 0%

profile of v4, /device:TPU:0, one launch (start us, length us, event | category | flops | bytes accessed | tf_op | source)
XLA Modules:
  0.0 38.7 jit_solution(13348808413337455790)
XLA Ops:
  0.6 1.8 %pack.1 = (bf16[32,40,128]{2,1,0:T(8,128)(2,1)}, bf16[4,128,128]{2,1,0:T(8,128)(2,1)S(1)}, bf16[4,128,128]{2,1,0:T(8,128)(2,1)S(1)}) custom-call(s32[128]{0:T(128)} %refs_0_.1, bf16[32,2048]{1,0:T(8,128)(2,1)} %refs_1_.1, bf16[32,2048]{1,0:T(8,128)(2,1)} %refs_2_.1, bf16[32,512]{1,0:T(8,128)(2,1)} %refs_3_.1, bf16[32,512]{1,0:T(8,128)(2,1)} %refs_4_.1, ...), custom_call_target="tpu_custom_call" | custom-call | tf_op jit(solution)/shard_map/pack/pallas_call | solution.py:548
  2.4 7.3 %all-to-all-start = ((bf16[32,40,128]{2,1,0:T(8,128)(2,1)}), bf16[32,40,128]{2,1,0:T(8,128)(2,1)S(1)}, u32[]{:S(2)}, u32[]{:S(2)}) async-start(bf16[32,40,128]{2,1,0:T(8,128)(2,1)} %get-tuple-element.20), calls=%async_computation | async-start | bytes 655360 | tf_op jit(solution)/shard_map/all_to_all | solution.py:569
  9.8 0.3 collective-permute-start
  10.1 1.1 %collective-permute-done.cross_ref = bf16[4,128,128]{2,1,0:T(8,128)(2,1)S(1)} collective-permute-done((bf16[4,128,128]{2,1,0:T(8,128)(2,1)S(1)}, bf16[4,128,128]{2,1,0:T(8,128)(2,1)S(1)}, u32[]{:S(2)}, u32[]{:S(2)}) %collective-permute-start) | collective-permute-done | bytes 131104 | tf_op jit(solution)/shard_map/ppermute | solution.py:566
  11.2 1.8 %collective-permute-start.1 = (bf16[256,128]{1,0:T(8,128)(2,1)S(1)}, bf16[256,128]{1,0:T(8,128)(2,1)S(1)}, u32[]{:S(2)}, u32[]{:S(2)}) collective-permute-start(bf16[256,128]{1,0:T(8,128)(2,1)S(1)} %get-tuple-element.17), channel_id=1, source_target_pairs={{0,8},{4,12},{8,0},{12,4},{16,24},{20,28},{24,16},{28,20},{1,9},{5... | collective-permute-start | bytes 196616 | tf_op jit(solution)/shard_map/ppermute | solution.py:566
  13.0 1.5 %collective-permute-start.2 = (bf16[256,128]{1,0:T(8,128)(2,1)S(1)}, bf16[256,128]{1,0:T(8,128)(2,1)S(1)}, u32[]{:S(2)}, u32[]{:S(2)}) collective-permute-start(bf16[256,128]{1,0:T(8,128)(2,1)S(1)} %get-tuple-element.18), channel_id=1, source_target_pairs={{0,16},{4,20},{8,24},{12,28},{16,0},{20,4},{24,8},{28,12},{1,17},{... | collective-permute-start | bytes 196616 | tf_op jit(solution)/shard_map/ppermute | solution.py:566
  14.5 0.3 collective-permute-start.3
  14.8 1.9 %collective-permute-done.1.refs_0_ = bf16[256,128]{1,0:T(8,128)(2,1)S(1)} collective-permute-done((bf16[256,128]{1,0:T(8,128)(2,1)S(1)}, bf16[256,128]{1,0:T(8,128)(2,1)S(1)}, u32[]{:S(2)}, u32[]{:S(2)}) %collective-permute-start.1) | collective-permute-done | bytes 65568 | tf_op jit(solution)/shard_map/ppermute | solution.py:566
  16.7 2.1 %collective-permute-done.2.refs_1_ = bf16[256,128]{1,0:T(8,128)(2,1)S(1)} collective-permute-done((bf16[256,128]{1,0:T(8,128)(2,1)S(1)}, bf16[256,128]{1,0:T(8,128)(2,1)S(1)}, u32[]{:S(2)}, u32[]{:S(2)}) %collective-permute-start.2) | collective-permute-done | bytes 65568 | tf_op jit(solution)/shard_map/ppermute | solution.py:566
  18.8 1.1 %collective-permute-done.3.refs_2_ = bf16[256,128]{1,0:T(8,128)(2,1)S(1)} collective-permute-done((bf16[256,128]{1,0:T(8,128)(2,1)S(1)}, bf16[256,128]{1,0:T(8,128)(2,1)S(1)}, u32[]{:S(2)}, u32[]{:S(2)}) %collective-permute-start.3) | collective-permute-done | bytes 65568 | tf_op jit(solution)/shard_map/ppermute | solution.py:566
  19.9 0.1 prepare.1.ready_ref
  20.1 0.8 %all-to-all-done.key_ref = bf16[32,40,128]{2,1,0:T(8,128)(2,1)S(1)} async-done(((bf16[32,40,128]{2,1,0:T(8,128)(2,1)}), bf16[32,40,128]{2,1,0:T(8,128)(2,1)S(1)}, u32[]{:S(2)}, u32[]{:S(2)}) %all-to-all-start) | async-done | bytes 327712 | tf_op jit(solution)/shard_map/all_to_all | solution.py:569
  20.8 3.4 %attend.1 = (bf16[4,768,256]{2,1,0:T(8,128)(2,1)S(1)}, bf16[8,4,32,128]{3,2,1,0:T(8,128)(2,1)}, bf16[4,64,128]{2,1,0:T(8,128)(2,1)S(1)}, bf16[4,64,128]{2,1,0:T(8,128)(2,1)S(1)}) custom-call(bf16[4,768,256]{2,1,0:T(8,128)(2,1)S(1)} %prepare.1.ready_ref, bf16[32,40,128]{2,1,0:T(8,128)(2,1)S(1)} %all-to-all-done.key_ref), custom_call_target="tpu_custom_call", output_to_operand_aliasing={{0}: (0, {})} | custom-call | tf_op jit(solution)/shard_map/attend/pallas_call | solution.py:600
  24.2 3.5 %all-to-all-start.1 = ((bf16[32,32,128]{2,1,0:T(8,128)(2,1)}), bf16[32,32,128]{2,1,0:T(8,128)(2,1)S(1)}, u32[]{:S(2)}, u32[]{:S(2)}) async-start(bf16[32,32,128]{2,1,0:T(8,128)(2,1)} %bitcast.2), calls=%async_computation.1 | async-start | bytes 524288 | tf_op jit(solution)/shard_map/all_to_all | solution.py:569
  27.8 0.3 collective-permute-start.4
  28.1 1.0 %collective-permute-done.4.cross_ref = bf16[4,64,128]{2,1,0:T(8,128)(2,1)S(1)} collective-permute-done((bf16[4,64,128]{2,1,0:T(8,128)(2,1)S(1)}, bf16[4,64,128]{2,1,0:T(8,128)(2,1)S(1)}, u32[]{:S(2)}, u32[]{:S(2)}) %collective-permute-start.4) | collective-permute-done | bytes 65568 | tf_op jit(solution)/shard_map/ppermute | solution.py:566
  29.1 1.8 %collective-permute-start.5 = (bf16[128,128]{1,0:T(8,128)(2,1)S(1)}, bf16[128,128]{1,0:T(8,128)(2,1)S(1)}, u32[]{:S(2)}, u32[]{:S(2)}) collective-permute-start(bf16[128,128]{1,0:T(8,128)(2,1)S(1)} %get-tuple-element.24), channel_id=1, source_target_pairs={{0,8},{4,12},{8,0},{12,4},{16,24},{20,28},{24,16},{28,20},{1,9},{5... | collective-permute-start | bytes 98312 | tf_op jit(solution)/shard_map/ppermute | solution.py:566
  31.0 1.5 %collective-permute-start.6 = (bf16[128,128]{1,0:T(8,128)(2,1)S(1)}, bf16[128,128]{1,0:T(8,128)(2,1)S(1)}, u32[]{:S(2)}, u32[]{:S(2)}) collective-permute-start(bf16[128,128]{1,0:T(8,128)(2,1)S(1)} %get-tuple-element.25), channel_id=1, source_target_pairs={{0,16},{4,20},{8,24},{12,28},{16,0},{20,4},{24,8},{28,12},{1,17},{... | collective-permute-start | bytes 98312 | tf_op jit(solution)/shard_map/ppermute | solution.py:566
  32.4 0.3 collective-permute-start.7
  32.7 0.9 %collective-permute-done.5.refs_0_ = bf16[128,128]{1,0:T(8,128)(2,1)S(1)} collective-permute-done((bf16[128,128]{1,0:T(8,128)(2,1)S(1)}, bf16[128,128]{1,0:T(8,128)(2,1)S(1)}, u32[]{:S(2)}, u32[]{:S(2)}) %collective-permute-start.5) | collective-permute-done | bytes 32800 | tf_op jit(solution)/shard_map/ppermute | solution.py:566
  33.5 1.4 %collective-permute-done.6.refs_1_ = bf16[128,128]{1,0:T(8,128)(2,1)S(1)} collective-permute-done((bf16[128,128]{1,0:T(8,128)(2,1)S(1)}, bf16[128,128]{1,0:T(8,128)(2,1)S(1)}, u32[]{:S(2)}, u32[]{:S(2)}) %collective-permute-start.6) | collective-permute-done | bytes 32800 | tf_op jit(solution)/shard_map/ppermute | solution.py:566
  35.0 2.4 %collective-permute-done.7.refs_2_ = bf16[128,128]{1,0:T(8,128)(2,1)S(1)} collective-permute-done((bf16[128,128]{1,0:T(8,128)(2,1)S(1)}, bf16[128,128]{1,0:T(8,128)(2,1)S(1)}, u32[]{:S(2)}, u32[]{:S(2)}) %collective-permute-start.7) | collective-permute-done | bytes 32800 | tf_op jit(solution)/shard_map/ppermute | solution.py:566
  37.4 0.7 %all-to-all-done.1.part_ref = bf16[32,32,128]{2,1,0:T(8,128)(2,1)S(1)} async-done(((bf16[32,32,128]{2,1,0:T(8,128)(2,1)}), bf16[32,32,128]{2,1,0:T(8,128)(2,1)S(1)}, u32[]{:S(2)}, u32[]{:S(2)}) %all-to-all-start.1) | async-done | bytes 262176 | tf_op jit(solution)/shard_map/all_to_all | solution.py:569
  38.0 0.7 %unpack.1 = (bf16[32,2048]{1,0:T(8,128)(2,1)}, bf16[32,512]{1,0:T(8,128)(2,1)}, bf16[32,512]{1,0:T(8,128)(2,1)}) custom-call(bf16[32,32,128]{2,1,0:T(8,128)(2,1)S(1)} %all-to-all-done.1.part_ref, bf16[4,64,128]{2,1,0:T(8,128)(2,1)S(1)} %get-tuple-element.22.same_ref, bf16[4,64,128]{2,1,0:T(8,128)(2,1)S(1)} %collective-permute-done.4.cross_ref, ...), custom_call_target="tpu_custom_call" | custom-call | tf_op jit(solution)/shard_map/unpack/pallas_call | solution.py:627
  (2 shorter events, 0.0 us)
Async XLA Ops:
  2.4 18.4 %all-to-all-start = ((bf16[32,40,128]{2,1,0:T(8,128)(2,1)}), bf16[32,40,128]{2,1,0:T(8,128)(2,1)S(1)}, u32[]{:S(2)}, u32[]{:S(2)}) async-start(bf16[32,40,128]{2,1,0:T(8,128)(2,1)} %get-tuple-element.20), calls=%async_computation | async-start | bytes 655360 | tf_op jit(solution)/shard_map/all_to_all | solution.py:569
  9.8 1.4 %collective-permute-start = (bf16[4,128,128]{2,1,0:T(8,128)(2,1)S(1)}, bf16[4,128,128]{2,1,0:T(8,128)(2,1)S(1)}, u32[]{:S(2)}, u32[]{:S(2)}) collective-permute-start(bf16[4,128,128]{2,1,0:T(8,128)(2,1)S(1)} %get-tuple-element.16), channel_id=1, source_target_pairs={{0,4},{4,0},{8,12},{12,8},{16,20},{20,16},{24,28},{28,24},{1,5},{5... | collective-permute-start | bytes 393224 | tf_op jit(solution)/shard_map/ppermute | solution.py:566
  11.2 5.5 %collective-permute-start.1 = (bf16[256,128]{1,0:T(8,128)(2,1)S(1)}, bf16[256,128]{1,0:T(8,128)(2,1)S(1)}, u32[]{:S(2)}, u32[]{:S(2)}) collective-permute-start(bf16[256,128]{1,0:T(8,128)(2,1)S(1)} %get-tuple-element.17), channel_id=1, source_target_pairs={{0,8},{4,12},{8,0},{12,4},{16,24},{20,28},{24,16},{28,20},{1,9},{5... | collective-permute-start | bytes 196616 | tf_op jit(solution)/shard_map/ppermute | solution.py:566
  13.0 5.7 %collective-permute-start.2 = (bf16[256,128]{1,0:T(8,128)(2,1)S(1)}, bf16[256,128]{1,0:T(8,128)(2,1)S(1)}, u32[]{:S(2)}, u32[]{:S(2)}) collective-permute-start(bf16[256,128]{1,0:T(8,128)(2,1)S(1)} %get-tuple-element.18), channel_id=1, source_target_pairs={{0,16},{4,20},{8,24},{12,28},{16,0},{20,4},{24,8},{28,12},{1,17},{... | collective-permute-start | bytes 196616 | tf_op jit(solution)/shard_map/ppermute | solution.py:566
  14.5 5.4 %collective-permute-start.3 = (bf16[256,128]{1,0:T(8,128)(2,1)S(1)}, bf16[256,128]{1,0:T(8,128)(2,1)S(1)}, u32[]{:S(2)}, u32[]{:S(2)}) collective-permute-start(bf16[256,128]{1,0:T(8,128)(2,1)S(1)} %get-tuple-element.19), channel_id=1, source_target_pairs={{0,24},{4,28},{8,16},{12,20},{16,8},{20,12},{24,0},{28,4},{1,25},{... | collective-permute-start | bytes 196616 | tf_op jit(solution)/shard_map/ppermute | solution.py:566
  24.2 13.8 %all-to-all-start.1 = ((bf16[32,32,128]{2,1,0:T(8,128)(2,1)}), bf16[32,32,128]{2,1,0:T(8,128)(2,1)S(1)}, u32[]{:S(2)}, u32[]{:S(2)}) async-start(bf16[32,32,128]{2,1,0:T(8,128)(2,1)} %bitcast.2), calls=%async_computation.1 | async-start | bytes 524288 | tf_op jit(solution)/shard_map/all_to_all | solution.py:569
  27.8 1.3 %collective-permute-start.4 = (bf16[4,64,128]{2,1,0:T(8,128)(2,1)S(1)}, bf16[4,64,128]{2,1,0:T(8,128)(2,1)S(1)}, u32[]{:S(2)}, u32[]{:S(2)}) collective-permute-start(bf16[4,64,128]{2,1,0:T(8,128)(2,1)S(1)} %get-tuple-element.23), channel_id=1, source_target_pairs={{0,4},{4,0},{8,12},{12,8},{16,20},{20,16},{24,28},{28,24},{1,5},{5... | collective-permute-start | bytes 196616 | tf_op jit(solution)/shard_map/ppermute | solution.py:566
  29.1 4.4 %collective-permute-start.5 = (bf16[128,128]{1,0:T(8,128)(2,1)S(1)}, bf16[128,128]{1,0:T(8,128)(2,1)S(1)}, u32[]{:S(2)}, u32[]{:S(2)}) collective-permute-start(bf16[128,128]{1,0:T(8,128)(2,1)S(1)} %get-tuple-element.24), channel_id=1, source_target_pairs={{0,8},{4,12},{8,0},{12,4},{16,24},{20,28},{24,16},{28,20},{1,9},{5... | collective-permute-start | bytes 98312 | tf_op jit(solution)/shard_map/ppermute | solution.py:566
  31.0 4.0 %collective-permute-start.6 = (bf16[128,128]{1,0:T(8,128)(2,1)S(1)}, bf16[128,128]{1,0:T(8,128)(2,1)S(1)}, u32[]{:S(2)}, u32[]{:S(2)}) collective-permute-start(bf16[128,128]{1,0:T(8,128)(2,1)S(1)} %get-tuple-element.25), channel_id=1, source_target_pairs={{0,16},{4,20},{8,24},{12,28},{16,0},{20,4},{24,8},{28,12},{1,17},{... | collective-permute-start | bytes 98312 | tf_op jit(solution)/shard_map/ppermute | solution.py:566
  32.4 4.9 %collective-permute-start.7 = (bf16[128,128]{1,0:T(8,128)(2,1)S(1)}, bf16[128,128]{1,0:T(8,128)(2,1)S(1)}, u32[]{:S(2)}, u32[]{:S(2)}) collective-permute-start(bf16[128,128]{1,0:T(8,128)(2,1)S(1)} %get-tuple-element.26), channel_id=1, source_target_pairs={{0,24},{4,28},{8,16},{12,20},{16,8},{20,12},{24,0},{28,4},{1,25},{... | collective-permute-start | bytes 98312 | tf_op jit(solution)/shard_map/ppermute | solution.py:566

commit v5 on v4

--- a/solution.py
+++ b/solution.py
@@ -9,6 +9,7 @@
 LANES = 128
 PIECES = 2
 NOTE_ROWS = 8
+TOGETHER = 2
 CHIP_ORDER = (1, 2, 3)
 MASKED = 16384.0
 F32 = jnp.float32
@@ -218,35 +219,37 @@
     return lax.broadcasted_iota(jnp.int32, shape, len(shape) - 1)
 
 
-def pair_sums(kv, mark_from, first, rows, allowed, left_ref, right_ref, prob_ref, score_ref):
-    tokens = kv.shape[0]
+def pair_sums(kvs, marks, first, rows, allowed, left_ref, right_ref, both_ref, prob_ref, score_ref):
+    tokens = kvs[0].shape[0]
     group = right_ref.shape[0]
     key_row = lax.broadcasted_iota(jnp.int32, (tokens, LANES), 0)
-    wide_lane = lane_of((tokens, LANES))
-    low = wide_lane < HEAD_WIDTH
-    mark = mark_from + key_row // rows
-    ones = jnp.where((wide_lane < first) | (wide_lane == mark), -1.0, 0.0)
-    left_ref[:, 0:LANES] = kv
-    left_ref[:, LANES:] = ones.astype(BF16)
+    lane = lane_of((tokens, LANES))
+    for i, (kv, mark_from) in enumerate(zip(kvs, marks)):
+        down = slice(i * tokens, (i + 1) * tokens)
+        mark = mark_from + key_row // rows
+        ones = jnp.where((lane < first) | (lane == mark), -1.0, 0.0)
+        left_ref[down, 0:LANES] = kv
+        left_ref[down, LANES:] = ones.astype(BF16)
     for e in range(group):
         both = lax.dot_general(
             left_ref[...],
-            right_ref[e, 0 : 2 * tokens],
+            right_ref[e],
             (((1,), (1,)), ((), ())),
             preferred_element_type=F32,
         )
-        prob = jnp.exp(both[:, 0:tokens])
-        if allowed is not None:
-            prob = jnp.where(allowed, prob, 0.0)
-        score = prob * both[:, tokens:]
         across = slice(e * tokens, (e + 1) * tokens)
-        prob_ref[:, across] = prob.astype(BF16)
-        score_ref[:, across] = score.astype(BF16)
-    pairs = jnp.concatenate(
-        [right_ref[e, 2 * tokens : 3 * tokens, 0:LANES] for e in range(group)], 0
-    )
+        for i in range(len(kvs)):
+            down = slice(i * tokens, (i + 1) * tokens)
+            prob = jnp.exp(both[down, 0:tokens])
+            if i == 0 and allowed is not None:
+                prob = jnp.where(allowed, prob, 0.0)
+            score = prob * both[down, tokens:]
+            prob_ref[down, across] = prob.astype(BF16)
+            score_ref[down, across] = score.astype(BF16)
+    pairs = both_ref[...].reshape(group * tokens, LANES)
     value_side = jnp.dot(prob_ref[...], pairs, preferred_element_type=F32)
     key_side = jnp.dot(score_ref[...], pairs, preferred_element_type=F32)
+    low = lane_of(value_side.shape) < HEAD_WIDTH
     return jnp.where(low, key_side, value_side)
 
 
@@ -261,7 +264,7 @@
     for i in (5, 6, 0, 3, 4, 1, 2):
         copies[i].start()
     rows = q_ref.shape[0]
-    tall = pos_ref.shape[0]
+    tall = pos_ref.shape[1]
     planes = tall // rows
     chips = same_ref.shape[0]
     group = q_ref.shape[1] // k_ref.shape[1]
@@ -274,7 +277,7 @@
     copies[5].wait()
     copies[6].wait()
     copies[0].wait()
-    lead = (pos_ref[0] // (tall // 2)).astype(F32)
+    lead = jnp.floor(pos_ref[0:1, 0:1].astype(F32) / (tall // 2))
     eight = NOTE_ROWS
     sub = lax.broadcasted_iota(jnp.int32, (eight, LANES), 0)
     quarter = lane_of((eight, LANES)) // rows
@@ -347,25 +350,19 @@
 
 
 def prepare_kernel(same_ref, cross_ref, *refs):
-    far_refs, right_ref = refs[:-1], refs[-1]
+    far_refs, both_ref = refs[:-1], refs[-1]
+    group, tokens, _ = both_ref.shape
     packet = same_ref.shape[1]
-    group = right_ref.shape[0]
-    tokens = right_ref.shape[1] // 3
     rows = packet // group
     block = lax.axis_index("ctx")
     slots = {0: same_ref.at[0], 1: cross_ref.at[0]}
     for m, ref in enumerate(far_refs):
         slots[2 * CHIP_ORDER[m]] = ref.at[0:packet]
         slots[2 * CHIP_ORDER[m] + 1] = ref.at[packet : 2 * packet]
-    low = lane_of((rows, LANES)) < HEAD_WIDTH
-    nothing = jnp.zeros((rows, LANES), BF16)
     for i, slot in slots.items():
         at = pl.multiple_of((block ^ i) * rows, rows)
         for e in range(group):
-            pair = slot[e * rows : (e + 1) * rows, :]
-            right_ref[e, pl.ds(2 * tokens + at, rows), 0:LANES] = pair
-            right_ref[e, pl.ds(at, rows), 0:LANES] = jnp.where(low, pair, nothing)
-            right_ref[e, pl.ds(tokens + at, rows), 0:LANES] = jnp.where(low, nothing, pair)
+            both_ref[e, pl.ds(at, rows), :] = slot[e * rows : (e + 1) * rows, :]
 
 
 def plane_keys(key_ref, which, blocks, rows):
@@ -374,11 +371,10 @@
 
 
 def attend_kernel(
-    ready_ref, key_ref, right_ref, out_ref, same_ref, cross_ref,
-    scores_ref, wide_ref, left_ref, prob_ref, part_ref, all_ref, sems,
+    both_ref, key_ref, out_ref, same_ref, cross_ref,
+    scores_ref, right_ref, wide_ref, left_ref, prob_ref, part_ref, all_ref, sems,
 ):
-    group = right_ref.shape[0]
-    tokens = right_ref.shape[1] // 3
+    group, tokens, _ = both_ref.shape
     blocks, planes, rows, _ = out_ref.shape
     eight = NOTE_ROWS
     count = 2 * PIECES
@@ -404,6 +400,11 @@
             moved = pltpu.roll(notes[b], turn, 1) if turn else notes[b]
             down = slice((b // per_tile) * LANES + e * eight, (b // per_tile) * LANES + (e + 1) * eight)
             wide_ref[down, :] = jnp.where(quarter == spot, moved, wide_ref[down, :])
+    low = lane_of((tokens, LANES)) < HEAD_WIDTH
+    nothing = jnp.zeros((tokens, LANES), BF16)
+    for e in range(group):
+        right_ref[e, 0:tokens, 0:LANES] = jnp.where(low, both_ref[e], nothing)
+        right_ref[e, tokens : 2 * tokens, 0:LANES] = jnp.where(low, nothing, both_ref[e])
     columns = [
         wide_ref[m * LANES : (m + 1) * LANES, :].T for m in range(tokens // LANES)
     ]
@@ -436,17 +437,21 @@
     square_query = lane_of((tokens, tokens))
     allowed = (square_key <= square_query) | (square_key // rows != square_query // rows)
     copies = []
-    for j in range(planes):
-        which = plane ^ j
+    for j in range(0, planes, TOGETHER):
+        group_of = [plane ^ (j + i) for i in range(TOGETHER)]
         kv_sum = pair_sums(
-            plane_keys(key_ref, which, blocks, rows),
-            first + which * blocks, first, rows, None if j else allowed,
-            left_ref, right_ref, prob_ref,
-            scores_ref.at[j * tokens : (j + 1) * tokens],
-        )
-        part_ref[j] = kv_sum.astype(BF16).reshape(blocks, rows, LANES)
-        copies.append(pltpu.make_async_copy(part_ref.at[j], out_ref.at[:, which], sems.at[j]))
-        copies[j].start()
+            [plane_keys(key_ref, which, blocks, rows) for which in group_of],
+            [first + which * blocks for which in group_of],
+            first, rows, None if j else allowed,
+            left_ref, right_ref, both_ref, prob_ref,
+            scores_ref.at[j * tokens : (j + TOGETHER) * tokens],
+        ).astype(BF16)
+        for i, which in enumerate(group_of):
+            part = kv_sum[i * tokens : (i + 1) * tokens]
+            part_ref[j + i] = part.reshape(blocks, rows, LANES)
+            copy = pltpu.make_async_copy(part_ref.at[j + i], out_ref.at[:, which], sems.at[j + i])
+            copy.start()
+            copies.append(copy)
     query_sum = jnp.zeros((HEAD_WIDTH, group * tokens), F32)
     for j in range(planes):
         keys = plane_keys(key_ref, plane ^ j, blocks, rows)
@@ -536,7 +541,7 @@
     devices = blocks * planes
     wide = group * tokens
     arguments = (
-        positions,
+        positions.reshape(1, -1),
         query_input,
         output_gradient,
         key_input,
@@ -553,8 +558,7 @@
         in_specs=[pl.BlockSpec(memory_space=pl.ANY)] * len(arguments),
         out_specs=[pl.BlockSpec(memory_space=pl.ANY), KEPT, KEPT],
         scratch_shapes=[
-            pltpu.SMEM(a.shape, a.dtype) if a.ndim == 1 else pltpu.VMEM(a.shape, a.dtype)
-            for a in arguments
+            pltpu.VMEM(a.shape, a.dtype) for a in arguments
         ]
         + [
             pltpu.VMEM((devices, rows + NOTE_ROWS, LANES), BF16),
@@ -585,41 +589,35 @@
         return kept(same, cross, *joined)
 
     received = exchange(same, cross)
-    right_shape = pltpu.VMEM((group, 3 * tokens, 2 * LANES), BF16)
-    right = pl.pallas_call(
+    both = pl.pallas_call(
         prepare_kernel,
         name="prepare",
         compiler_params=ROOMY,
-        out_shape=right_shape,
+        out_shape=pltpu.VMEM((group, tokens, LANES), BF16),
         in_specs=[KEPT] * (chips + 1),
         out_specs=KEPT,
     )(*received)
     (keys,) = kept(keys)
     tall = group // 2 * rows
     half = pltpu.VMEM((chips, tall, LANES), BF16)
-    right, parts, same, cross = pl.pallas_call(
+    parts, same, cross = pl.pallas_call(
         attend_kernel,
         name="attend",
         compiler_params=ROOMY,
-        out_shape=[
-            right_shape,
-            jax.ShapeDtypeStruct((blocks, planes, rows, LANES), BF16),
-            half,
-            half,
-        ],
+        out_shape=[jax.ShapeDtypeStruct((blocks, planes, rows, LANES), BF16), half, half],
         in_specs=[KEPT] * 2,
-        out_specs=[KEPT, pl.BlockSpec(memory_space=pl.ANY), KEPT, KEPT],
-        input_output_aliases={0: 0},
+        out_specs=[pl.BlockSpec(memory_space=pl.ANY), KEPT, KEPT],
         scratch_shapes=[
             pltpu.VMEM((planes * tokens, wide), BF16),
+            pltpu.VMEM((group, 2 * tokens, 2 * LANES), BF16),
             pltpu.VMEM((tokens // LANES * LANES, LANES), F32),
-            pltpu.VMEM((tokens, 2 * LANES), BF16),
-            pltpu.VMEM((tokens, wide), BF16),
+            pltpu.VMEM((TOGETHER * tokens, 2 * LANES), BF16),
+            pltpu.VMEM((TOGETHER * tokens, wide), BF16),
             pltpu.VMEM((planes, blocks, rows, LANES), BF16),
             pltpu.VMEM((blocks, tall, LANES), BF16),
             pltpu.SemaphoreType.DMA((planes,)),
         ],
-    )(*kept(right), keys)
+    )(*kept(both), keys)
     parts = to_all(parts.reshape(devices, rows, LANES))
     received = exchange(same, cross)
     shapes = [query_input.shape, key_input.shape, value_input.shape]

time: 39.1 us -> 38.8 us (level)
  no operation moved by 1% of the time
where the time goes in v5:
time: 38.8 us; the launch traced here: 38.5 us
  starting transfers between devices  18.5 us (48%)
  waiting for transfers between devices  13.5 us (35%)
  Pallas kernels  5.8 us (15%)
  between operations  0.69 us (2%)
    ppermute x8, waiting for transfers between devices, trade(): return lax.ppermute(array, 'ctx', [(i, i ^ by) for i in range(blocks)])  11.9 us
    all_to_all x2, starting transfers between devices, to_all(): lax.all_to_all(array, ('ctx', 'head'), split_axis=0, concat_axis=0, tiled...  10.8 us
    ppermute x8, starting transfers between devices, trade(): return lax.ppermute(array, 'ctx', [(i, i ^ by) for i in range(blocks)])  7.74 us
    pallas_call x1, Pallas kernels, by_heads(): pl.pallas_call(attend_kernel, name='attend', compiler_params=ROOMY, out_s...  3.32 us
    pallas_call x1, Pallas kernels, by_heads(): pl.pallas_call(pack_kernel, name='pack', compiler_params=ROOMY, out_shape...  1.7 us
    all_to_all x2, waiting for transfers between devices, to_all(): lax.all_to_all(array, ('ctx', 'head'), split_axis=0, concat_axis=0, tiled...  1.53 us
  transfers between devices with their start and end apart: 10, of which 10 were waited for; matrix products, arithmetic and copies ran while one was open for 0% of the time, Pallas kernels for 0%

profile of v5, /device:TPU:0, one launch (start us, length us, event | category | flops | bytes accessed | tf_op | source)
XLA Modules:
  0.0 38.5 jit_solution(5462889852295211915)
XLA Ops:
  0.6 1.7 %pack.1 = (bf16[32,40,128]{2,1,0:T(8,128)(2,1)}, bf16[4,128,128]{2,1,0:T(8,128)(2,1)S(1)}, bf16[4,128,128]{2,1,0:T(8,128)(2,1)S(1)}) custom-call(s32[1,128]{1,0:T(1,128)} %bitcast.6, bf16[32,2048]{1,0:T(8,128)(2,1)} %refs_1_.1, bf16[32,2048]{1,0:T(8,128)(2,1)} %refs_2_.1, bf16[32,512]{1,0:T(8,128)(2,1)} %refs_3_.1, bf16[32,512]{1,0:T(8,128)(2,1)} %refs_4_.1, ...), custom_call_target="tpu_custom_call" | custom-call | tf_op jit(solution)/shard_map/pack/pallas_call | solution.py:553
  2.3 7.3 %all-to-all-start = ((bf16[32,40,128]{2,1,0:T(8,128)(2,1)}), bf16[32,40,128]{2,1,0:T(8,128)(2,1)S(1)}, u32[]{:S(2)}, u32[]{:S(2)}) async-start(bf16[32,40,128]{2,1,0:T(8,128)(2,1)} %get-tuple-element.20), calls=%async_computation | async-start | bytes 655360 | tf_op jit(solution)/shard_map/all_to_all | solution.py:573
  9.7 0.3 collective-permute-start
  10.0 1.1 %collective-permute-done.cross_ref = bf16[4,128,128]{2,1,0:T(8,128)(2,1)S(1)} collective-permute-done((bf16[4,128,128]{2,1,0:T(8,128)(2,1)S(1)}, bf16[4,128,128]{2,1,0:T(8,128)(2,1)S(1)}, u32[]{:S(2)}, u32[]{:S(2)}) %collective-permute-start) | collective-permute-done | bytes 131104 | tf_op jit(solution)/shard_map/ppermute | solution.py:570
  11.1 1.8 %collective-permute-start.1 = (bf16[256,128]{1,0:T(8,128)(2,1)S(1)}, bf16[256,128]{1,0:T(8,128)(2,1)S(1)}, u32[]{:S(2)}, u32[]{:S(2)}) collective-permute-start(bf16[256,128]{1,0:T(8,128)(2,1)S(1)} %get-tuple-element.17), channel_id=1, source_target_pairs={{0,8},{4,12},{8,0},{12,4},{16,24},{20,28},{24,16},{28,20},{1,9},{5... | collective-permute-start | bytes 196616 | tf_op jit(solution)/shard_map/ppermute | solution.py:570
  12.9 1.5 %collective-permute-start.2 = (bf16[256,128]{1,0:T(8,128)(2,1)S(1)}, bf16[256,128]{1,0:T(8,128)(2,1)S(1)}, u32[]{:S(2)}, u32[]{:S(2)}) collective-permute-start(bf16[256,128]{1,0:T(8,128)(2,1)S(1)} %get-tuple-element.18), channel_id=1, source_target_pairs={{0,16},{4,20},{8,24},{12,28},{16,0},{20,4},{24,8},{28,12},{1,17},{... | collective-permute-start | bytes 196616 | tf_op jit(solution)/shard_map/ppermute | solution.py:570
  14.4 0.3 collective-permute-start.3
  14.7 1.9 %collective-permute-done.1.refs_0_ = bf16[256,128]{1,0:T(8,128)(2,1)S(1)} collective-permute-done((bf16[256,128]{1,0:T(8,128)(2,1)S(1)}, bf16[256,128]{1,0:T(8,128)(2,1)S(1)}, u32[]{:S(2)}, u32[]{:S(2)}) %collective-permute-start.1) | collective-permute-done | bytes 65568 | tf_op jit(solution)/shard_map/ppermute | solution.py:570
  16.6 2.1 %collective-permute-done.2.refs_1_ = bf16[256,128]{1,0:T(8,128)(2,1)S(1)} collective-permute-done((bf16[256,128]{1,0:T(8,128)(2,1)S(1)}, bf16[256,128]{1,0:T(8,128)(2,1)S(1)}, u32[]{:S(2)}, u32[]{:S(2)}) %collective-permute-start.2) | collective-permute-done | bytes 65568 | tf_op jit(solution)/shard_map/ppermute | solution.py:570
  18.7 1.1 %collective-permute-done.3.refs_2_ = bf16[256,128]{1,0:T(8,128)(2,1)S(1)} collective-permute-done((bf16[256,128]{1,0:T(8,128)(2,1)S(1)}, bf16[256,128]{1,0:T(8,128)(2,1)S(1)}, u32[]{:S(2)}, u32[]{:S(2)}) %collective-permute-start.3) | collective-permute-done | bytes 65568 | tf_op jit(solution)/shard_map/ppermute | solution.py:570
  19.9 0.9 %all-to-all-done.key_ref = bf16[32,40,128]{2,1,0:T(8,128)(2,1)S(1)} async-done(((bf16[32,40,128]{2,1,0:T(8,128)(2,1)}), bf16[32,40,128]{2,1,0:T(8,128)(2,1)S(1)}, u32[]{:S(2)}, u32[]{:S(2)}) %all-to-all-start) | async-done | bytes 327712 | tf_op jit(solution)/shard_map/all_to_all | solution.py:573
  20.7 3.3 %attend.1 = (bf16[8,4,32,128]{3,2,1,0:T(8,128)(2,1)}, bf16[4,64,128]{2,1,0:T(8,128)(2,1)S(1)}, bf16[4,64,128]{2,1,0:T(8,128)(2,1)S(1)}) custom-call(bf16[4,256,128]{2,1,0:T(8,128)(2,1)S(1)} %prepare.1.both_ref, bf16[32,40,128]{2,1,0:T(8,128)(2,1)S(1)} %all-to-all-done.key_ref), custom_call_target="tpu_custom_call" | custom-call | tf_op jit(solution)/shard_map/attend/pallas_call | solution.py:603
  24.1 3.5 %all-to-all-start.1 = ((bf16[32,32,128]{2,1,0:T(8,128)(2,1)}), bf16[32,32,128]{2,1,0:T(8,128)(2,1)S(1)}, u32[]{:S(2)}, u32[]{:S(2)}) async-start(bf16[32,32,128]{2,1,0:T(8,128)(2,1)} %bitcast.3), calls=%async_computation.1 | async-start | bytes 524288 | tf_op jit(solution)/shard_map/all_to_all | solution.py:573
  27.5 0.3 collective-permute-start.4
  27.8 1.0 %collective-permute-done.4.cross_ref = bf16[4,64,128]{2,1,0:T(8,128)(2,1)S(1)} collective-permute-done((bf16[4,64,128]{2,1,0:T(8,128)(2,1)S(1)}, bf16[4,64,128]{2,1,0:T(8,128)(2,1)S(1)}, u32[]{:S(2)}, u32[]{:S(2)}) %collective-permute-start.4) | collective-permute-done | bytes 65568 | tf_op jit(solution)/shard_map/ppermute | solution.py:570
  28.9 1.8 %collective-permute-start.5 = (bf16[128,128]{1,0:T(8,128)(2,1)S(1)}, bf16[128,128]{1,0:T(8,128)(2,1)S(1)}, u32[]{:S(2)}, u32[]{:S(2)}) collective-permute-start(bf16[128,128]{1,0:T(8,128)(2,1)S(1)} %get-tuple-element.24), channel_id=1, source_target_pairs={{0,8},{4,12},{8,0},{12,4},{16,24},{20,28},{24,16},{28,20},{1,9},{5... | collective-permute-start | bytes 98312 | tf_op jit(solution)/shard_map/ppermute | solution.py:570
  30.7 1.5 %collective-permute-start.6 = (bf16[128,128]{1,0:T(8,128)(2,1)S(1)}, bf16[128,128]{1,0:T(8,128)(2,1)S(1)}, u32[]{:S(2)}, u32[]{:S(2)}) collective-permute-start(bf16[128,128]{1,0:T(8,128)(2,1)S(1)} %get-tuple-element.25), channel_id=1, source_target_pairs={{0,16},{4,20},{8,24},{12,28},{16,0},{20,4},{24,8},{28,12},{1,17},{... | collective-permute-start | bytes 98312 | tf_op jit(solution)/shard_map/ppermute | solution.py:570
  32.2 0.3 collective-permute-start.7
  32.4 0.9 %collective-permute-done.5.refs_0_ = bf16[128,128]{1,0:T(8,128)(2,1)S(1)} collective-permute-done((bf16[128,128]{1,0:T(8,128)(2,1)S(1)}, bf16[128,128]{1,0:T(8,128)(2,1)S(1)}, u32[]{:S(2)}, u32[]{:S(2)}) %collective-permute-start.5) | collective-permute-done | bytes 32800 | tf_op jit(solution)/shard_map/ppermute | solution.py:570
  33.3 1.4 %collective-permute-done.6.refs_1_ = bf16[128,128]{1,0:T(8,128)(2,1)S(1)} collective-permute-done((bf16[128,128]{1,0:T(8,128)(2,1)S(1)}, bf16[128,128]{1,0:T(8,128)(2,1)S(1)}, u32[]{:S(2)}, u32[]{:S(2)}) %collective-permute-start.6) | collective-permute-done | bytes 32800 | tf_op jit(solution)/shard_map/ppermute | solution.py:570
  34.7 2.4 %collective-permute-done.7.refs_2_ = bf16[128,128]{1,0:T(8,128)(2,1)S(1)} collective-permute-done((bf16[128,128]{1,0:T(8,128)(2,1)S(1)}, bf16[128,128]{1,0:T(8,128)(2,1)S(1)}, u32[]{:S(2)}, u32[]{:S(2)}) %collective-permute-start.7) | collective-permute-done | bytes 32800 | tf_op jit(solution)/shard_map/ppermute | solution.py:570
  37.1 0.7 %all-to-all-done.1.part_ref = bf16[32,32,128]{2,1,0:T(8,128)(2,1)S(1)} async-done(((bf16[32,32,128]{2,1,0:T(8,128)(2,1)}), bf16[32,32,128]{2,1,0:T(8,128)(2,1)S(1)}, u32[]{:S(2)}, u32[]{:S(2)}) %all-to-all-start.1) | async-done | bytes 262176 | tf_op jit(solution)/shard_map/all_to_all | solution.py:573
  37.8 0.7 %unpack.1 = (bf16[32,2048]{1,0:T(8,128)(2,1)}, bf16[32,512]{1,0:T(8,128)(2,1)}, bf16[32,512]{1,0:T(8,128)(2,1)}) custom-call(bf16[32,32,128]{2,1,0:T(8,128)(2,1)S(1)} %all-to-all-done.1.part_ref, bf16[4,64,128]{2,1,0:T(8,128)(2,1)S(1)} %get-tuple-element.22.same_ref, bf16[4,64,128]{2,1,0:T(8,128)(2,1)S(1)} %collective-permute-done.4.cross_ref, ...), custom_call_target="tpu_custom_call" | custom-call | tf_op jit(solution)/shard_map/unpack/pallas_call | solution.py:625
  (3 shorter events, 0.1 us)
Async XLA Ops:
  2.3 18.4 %all-to-all-start = ((bf16[32,40,128]{2,1,0:T(8,128)(2,1)}), bf16[32,40,128]{2,1,0:T(8,128)(2,1)S(1)}, u32[]{:S(2)}, u32[]{:S(2)}) async-start(bf16[32,40,128]{2,1,0:T(8,128)(2,1)} %get-tuple-element.20), calls=%async_computation | async-start | bytes 655360 | tf_op jit(solution)/shard_map/all_to_all | solution.py:573
  9.7 1.4 %collective-permute-start = (bf16[4,128,128]{2,1,0:T(8,128)(2,1)S(1)}, bf16[4,128,128]{2,1,0:T(8,128)(2,1)S(1)}, u32[]{:S(2)}, u32[]{:S(2)}) collective-permute-start(bf16[4,128,128]{2,1,0:T(8,128)(2,1)S(1)} %get-tuple-element.16), channel_id=1, source_target_pairs={{0,4},{4,0},{8,12},{12,8},{16,20},{20,16},{24,28},{28,24},{1,5},{5... | collective-permute-start | bytes 393224 | tf_op jit(solution)/shard_map/ppermute | solution.py:570
  11.1 5.5 %collective-permute-start.1 = (bf16[256,128]{1,0:T(8,128)(2,1)S(1)}, bf16[256,128]{1,0:T(8,128)(2,1)S(1)}, u32[]{:S(2)}, u32[]{:S(2)}) collective-permute-start(bf16[256,128]{1,0:T(8,128)(2,1)S(1)} %get-tuple-element.17), channel_id=1, source_target_pairs={{0,8},{4,12},{8,0},{12,4},{16,24},{20,28},{24,16},{28,20},{1,9},{5... | collective-permute-start | bytes 196616 | tf_op jit(solution)/shard_map/ppermute | solution.py:570
  12.9 5.7 %collective-permute-start.2 = (bf16[256,128]{1,0:T(8,128)(2,1)S(1)}, bf16[256,128]{1,0:T(8,128)(2,1)S(1)}, u32[]{:S(2)}, u32[]{:S(2)}) collective-permute-start(bf16[256,128]{1,0:T(8,128)(2,1)S(1)} %get-tuple-element.18), channel_id=1, source_target_pairs={{0,16},{4,20},{8,24},{12,28},{16,0},{20,4},{24,8},{28,12},{1,17},{... | collective-permute-start | bytes 196616 | tf_op jit(solution)/shard_map/ppermute | solution.py:570
  14.4 5.4 %collective-permute-start.3 = (bf16[256,128]{1,0:T(8,128)(2,1)S(1)}, bf16[256,128]{1,0:T(8,128)(2,1)S(1)}, u32[]{:S(2)}, u32[]{:S(2)}) collective-permute-start(bf16[256,128]{1,0:T(8,128)(2,1)S(1)} %get-tuple-element.19), channel_id=1, source_target_pairs={{0,24},{4,28},{8,16},{12,20},{16,8},{20,12},{24,0},{28,4},{1,25},{... | collective-permute-start | bytes 196616 | tf_op jit(solution)/shard_map/ppermute | solution.py:570
  24.1 13.7 %all-to-all-start.1 = ((bf16[32,32,128]{2,1,0:T(8,128)(2,1)}), bf16[32,32,128]{2,1,0:T(8,128)(2,1)S(1)}, u32[]{:S(2)}, u32[]{:S(2)}) async-start(bf16[32,32,128]{2,1,0:T(8,128)(2,1)} %bitcast.3), calls=%async_computation.1 | async-start | bytes 524288 | tf_op jit(solution)/shard_map/all_to_all | solution.py:573
  27.5 1.3 %collective-permute-start.4 = (bf16[4,64,128]{2,1,0:T(8,128)(2,1)S(1)}, bf16[4,64,128]{2,1,0:T(8,128)(2,1)S(1)}, u32[]{:S(2)}, u32[]{:S(2)}) collective-permute-start(bf16[4,64,128]{2,1,0:T(8,128)(2,1)S(1)} %get-tuple-element.23), channel_id=1, source_target_pairs={{0,4},{4,0},{8,12},{12,8},{16,20},{20,16},{24,28},{28,24},{1,5},{5... | collective-permute-start | bytes 196616 | tf_op jit(solution)/shard_map/ppermute | solution.py:570
  28.9 4.4 %collective-permute-start.5 = (bf16[128,128]{1,0:T(8,128)(2,1)S(1)}, bf16[128,128]{1,0:T(8,128)(2,1)S(1)}, u32[]{:S(2)}, u32[]{:S(2)}) collective-permute-start(bf16[128,128]{1,0:T(8,128)(2,1)S(1)} %get-tuple-element.24), channel_id=1, source_target_pairs={{0,8},{4,12},{8,0},{12,4},{16,24},{20,28},{24,16},{28,20},{1,9},{5... | collective-permute-start | bytes 98312 | tf_op jit(solution)/shard_map/ppermute | solution.py:570
  30.7 4.0 %collective-permute-start.6 = (bf16[128,128]{1,0:T(8,128)(2,1)S(1)}, bf16[128,128]{1,0:T(8,128)(2,1)S(1)}, u32[]{:S(2)}, u32[]{:S(2)}) collective-permute-start(bf16[128,128]{1,0:T(8,128)(2,1)S(1)} %get-tuple-element.25), channel_id=1, source_target_pairs={{0,16},{4,20},{8,24},{12,28},{16,0},{20,4},{24,8},{28,12},{1,17},{... | collective-permute-start | bytes 98312 | tf_op jit(solution)/shard_map/ppermute | solution.py:570
  32.2 4.9 %collective-permute-start.7 = (bf16[128,128]{1,0:T(8,128)(2,1)S(1)}, bf16[128,128]{1,0:T(8,128)(2,1)S(1)}, u32[]{:S(2)}, u32[]{:S(2)}) collective-permute-start(bf16[128,128]{1,0:T(8,128)(2,1)S(1)} %get-tuple-element.26), channel_id=1, source_target_pairs={{0,24},{4,28},{8,16},{12,20},{16,8},{20,12},{24,0},{28,4},{1,25},{... | collective-permute-start | bytes 98312 | tf_op jit(solution)/shard_map/ppermute | solution.py:570
